TPU v7x, 32 devices: a whole 2x2x4 slice. The times are simulated.
32 devices in a mesh: dp: 4 (over y, core), seq: 8 (over z, x).
Axes of the slice: x: 2, y: 2, z: 4, core: 2. Of those that a mesh axis runs over, the one named last changes fastest.
Arguments:
- tokens: bfloat16 [4, 1024, 2048], P('dp', 'seq'), may hold values from -6 to 6
- query_proj: bfloat16 [2048, 1024], P(('dp', 'seq')), may hold values from -0.125 to 0.125
- key_proj: bfloat16 [2048, 1024], P(('dp', 'seq')), may hold values from -0.125 to 0.125
- value_proj: bfloat16 [2048, 2048], P(('dp', 'seq')), may hold values from -0.125 to 0.125
- swish_proj: bfloat16 [2048, 2048], P(('dp', 'seq')), may hold values from -0.125 to 0.125
- rank_in: bfloat16 [2048, 16], P(('dp', 'seq')), may hold values from -0.125 to 0.125
- rank_out: bfloat16 [1024, 16], P(('dp', 'seq')), may hold values from -1.5 to 1.5
- decay_bias: bfloat16 [1024], P(('dp', 'seq')), may hold values from 0.5 to 10
- attn_gain: bfloat16 [2048], P(('dp', 'seq')), may hold values from 0.5 to 1.5
- head_gain: bfloat16 [512], P(('dp', 'seq')), may hold values from 0.5 to 1.5
- out_proj: bfloat16 [2048, 2048], P(('dp', 'seq')), may hold values from -0.1875 to 0.1875
- mlp_gain: bfloat16 [2048], P(('dp', 'seq')), may hold values from 0.5 to 1.5
- gate_proj: bfloat16 [2048, 5632], P(('dp', 'seq')), may hold values from -0.125 to 0.125
- up_proj: bfloat16 [2048, 5632], P(('dp', 'seq')), may hold values from -0.125 to 0.125
- down_proj: bfloat16 [5632, 2048], P(('dp', 'seq')), may hold values from -0.078125 to 0.078125
- cotangent: bfloat16 [4, 1024, 2048], P('dp', 'seq'), may hold values from -6 to 6
Outputs:
- block_out: bfloat16 [4, 1024, 2048], P('dp', 'seq')
- grad_tokens: bfloat16 [4, 1024, 2048], P('dp', 'seq')
- grad_query: float32 [2048, 1024], P(('dp', 'seq'))
- grad_key: float32 [2048, 1024], P(('dp', 'seq'))
- grad_value: float32 [2048, 2048], P(('dp', 'seq'))
- grad_swish: float32 [2048, 2048], P(('dp', 'seq'))
- grad_rankin: float32 [2048, 16], P(('dp', 'seq'))
- grad_rankout: float32 [1024, 16], P(('dp', 'seq'))
- grad_bias: float32 [1024], P(('dp', 'seq'))
- grad_attngain: float32 [2048], P(('dp', 'seq'))
- grad_headgain: float32 [512], P(('dp', 'seq'))
- grad_outproj: float32 [2048, 2048], P(('dp', 'seq'))
- grad_mlpgain: float32 [2048], P(('dp', 'seq'))
- grad_gate: float32 [2048, 5632], P(('dp', 'seq'))
- grad_upproj: float32 [2048, 5632], P(('dp', 'seq'))
- grad_down: float32 [5632, 2048], P(('dp', 'seq'))
All inputs are finite; a program needn't handle non-finite values.
Results may differ from a plain program's by a relative error of at most 0.025.
Values may be sent and summed in bfloat16 or wider, within the bound.
No kernel may reach another device: no remote copies, remote signals or barrier semaphores. Data moves between devices by JAX's collectives and lax.ppermute only.
A program may use at most 640 MiB of HBM per device.

v0:
```python
import jax
import jax.numpy as jnp
from jax import lax
from jax.sharding import PartitionSpec as P

HEADS = 4
BLOCK = 64


norm_eps = 1e-06
exact = lax.Precision.HIGHEST


def prefix(shard, axis, combine, identity):
    devices, place = (lax.axis_size(axis), lax.axis_index(axis))
    everything = jax.tree.map(
        lambda part, kind: lax.all_gather(part.astype(kind), axis),
        shard,
        (jnp.bfloat16, jnp.bfloat16),
    )
    start = jax.tree.map(
        lambda part, zero: jnp.broadcast_to(jnp.asarray(zero, part.dtype), part.shape),
        shard,
        identity,
    )

    def prefix_turn(k, before):
        reached = k < place
        new = combine(
            before, jax.tree.map(lambda part, own: part[k].astype(own.dtype), everything, shard)
        )
        return jax.tree.map(lambda a, b: jnp.where(reached, a, b), new, before)

    return lax.fori_loop(0, devices, prefix_turn, start)


def entering(shard, axis, combine, identity):
    devices, place = (lax.axis_size(axis), lax.axis_index(axis))
    everything = jax.tree.map(
        lambda part, kind: lax.all_gather(part.astype(kind), axis),
        shard,
        jax.tree.map(lambda a: jnp.bfloat16 if a.dtype == jnp.float32 else a.dtype, shard),
    )
    start = jax.tree.map(
        lambda part, zero: jnp.broadcast_to(jnp.asarray(zero, part.dtype), part.shape),
        shard,
        identity,
    )

    def entering_turn(k, before):
        at = devices - 1 - k
        reached = at > place
        new = combine(
            before, jax.tree.map(lambda part, own: part[at].astype(own.dtype), everything, shard)
        )
        return jax.tree.map(lambda a, b: jnp.where(reached, a, b), new, before)

    return lax.fori_loop(0, devices, entering_turn, start)


def norm_rows(values, gain):
    return values * lax.rsqrt(jnp.mean(values * values, axis=-1, keepdims=True) + norm_eps) * gain


def block_step(kv_state, block_data):
    queries, keys_in, values_in, log_decay = block_data
    span_len = queries.shape[-2]
    scaling = queries.shape[-1] ** (-0.5)
    cumulative = jnp.cumsum(log_decay, axis=-2)
    last_row = cumulative[..., span_len - 1 :, :]
    mid_row = cumulative[..., span_len // 2 : span_len // 2 + 1, :]
    query_state = queries * jnp.exp(cumulative) * scaling
    carried = jnp.einsum("shck,shkv->shcv", query_state, kv_state, precision=exact)
    query_mid = queries * jnp.exp(cumulative - mid_row) * scaling
    key_mid = keys_in * jnp.exp(mid_row - cumulative)
    scores = jnp.einsum("shik,shjk->shij", query_mid, key_mid, precision=exact)
    causal = jnp.arange(span_len)[:, None] >= jnp.arange(span_len)[None, :]
    scores = jnp.where(causal, scores, 0.0)
    within = jnp.einsum("shij,shjv->shiv", scores, values_in, precision=exact)
    key_last = keys_in * jnp.exp(last_row - cumulative)
    new_state = jnp.exp(last_row[..., 0, :])[..., None] * kv_state + jnp.einsum(
        "shck,shcv->shkv", key_last, values_in, precision=exact
    )
    return (new_state, carried + within)


def state_step(carry, block_data):
    total_log, kv_state = carry
    keys_in, values_in, log_decay = block_data
    cumulative = jnp.cumsum(log_decay, axis=-2)
    last_row = cumulative[..., -1:, :]
    key_last = keys_in * jnp.exp(last_row - cumulative)
    kv_state = jnp.exp(last_row[..., 0, :])[..., None] * kv_state + jnp.einsum(
        "shck,shcv->shkv", key_last, values_in, precision=exact
    )
    return ((total_log + last_row[..., 0, :], kv_state), None)


def local_mixer(queries, keys_in, values_in, log_decay, state_in):
    final_state, outputs = lax.scan(block_step, state_in, (queries, keys_in, values_in, log_decay))
    return (outputs, final_state)


def join_states(earlier, later):
    return (earlier[0] + later[0], jnp.exp(later[0])[..., None] * earlier[1] + later[1])


def to_blocks(values, seq_count):
    rows_all, features = values.shape
    head_size = features // HEADS
    tok_count = rows_all // seq_count
    blocks = values.reshape(seq_count, tok_count // BLOCK, BLOCK, HEADS, head_size)
    return blocks.transpose(1, 0, 3, 2, 4)


def from_blocks(blocks):
    count_blocks, seq_count, head_count, span_len, head_size = blocks.shape
    return blocks.transpose(1, 0, 3, 2, 4).reshape(
        seq_count * count_blocks * span_len, head_count * head_size
    )


def gate_heads(mixed_rows, swish_in, head_gain):
    rows_all, features = swish_in.shape
    normed = norm_rows(mixed_rows.reshape(rows_all, HEADS, features // HEADS), head_gain)
    return normed.reshape(rows_all, features) * jax.nn.silu(swish_in)


def swiglu(gate_val, up_val):
    return jax.nn.silu(gate_val) * up_val


def decay_map(low_rank, rank_out, decay_bias):
    logits = jnp.dot(low_rank, rank_out.T, precision=exact) + decay_bias
    return jax.nn.log_sigmoid(logits) / 16.0


def dot_low(left, right):
    return jnp.dot(left, right, preferred_element_type=jnp.float32)


def dot_left(left, right, precision=None):
    return lax.dot_general(
        left,
        right,
        (((0,), (0,)), ((), ())),
        precision=precision,
        preferred_element_type=jnp.float32,
    )


def dot_right(left, right, precision=None):
    return lax.dot_general(
        left,
        right,
        (((1,), (1,)), ((), ())),
        precision=precision,
        preferred_element_type=jnp.float32,
    )


def fold_rows(member, parts):
    return member.reshape((parts, member.shape[0] // parts) + member.shape[1:])


def unfold_rows(member):
    return member.reshape(member.shape[1:])


def per_device(
    tokens,
    query_proj,
    key_proj,
    value_proj,
    swish_proj,
    rank_in,
    rank_out,
    decay_bias,
    attn_gain,
    head_gain,
    out_proj,
    mlp_gain,
    gate_proj,
    up_proj,
    down_proj,
    cotangent,
):
    seq_count, tok_count, features = tokens.shape
    rows_all = seq_count * tok_count
    value_size = features // HEADS
    attn_full = (
        lax.all_gather(query_proj, ("dp", "seq"), axis=0, tiled=True),
        lax.all_gather(key_proj, ("dp", "seq"), axis=0, tiled=True),
        lax.all_gather(value_proj, ("dp", "seq"), axis=0, tiled=True),
        lax.all_gather(swish_proj, ("dp", "seq"), axis=0, tiled=True),
        lax.all_gather(rank_in, ("dp", "seq"), axis=0, tiled=True),
        lax.all_gather(rank_out, ("dp", "seq"), axis=0, tiled=True),
        lax.all_gather(decay_bias, ("dp", "seq"), axis=0, tiled=True),
        lax.all_gather(attn_gain, ("dp", "seq"), axis=0, tiled=True),
        lax.all_gather(head_gain, ("dp", "seq"), axis=0, tiled=True),
        lax.all_gather(out_proj, ("dp", "seq"), axis=0, tiled=True),
    )
    mlp_full = (
        lax.all_gather(mlp_gain, ("dp", "seq"), axis=0, tiled=True),
        lax.all_gather(gate_proj, ("dp", "seq"), axis=0, tiled=True),
        lax.all_gather(up_proj, ("dp", "seq"), axis=0, tiled=True),
        lax.all_gather(down_proj, ("dp", "seq"), axis=0, tiled=True),
    )
    (
        query_full,
        key_full,
        value_full,
        swish_full,
        rankin_full,
        rankout_full,
        bias_full,
        attngain_full,
        headgain_full,
        output_full,
    ) = attn_full
    mlpgain_full, gate_full, upward_full, down_full = mlp_full
    key_width = query_full.shape[1]
    key_size = key_width // HEADS
    residual = tokens.reshape(rows_all, features).astype(jnp.float32)
    normed, attn_norm_back = jax.vjp(norm_rows, residual, attngain_full.astype(jnp.float32))
    normed_low = normed.astype(jnp.bfloat16)
    query_low = dot_low(normed_low, query_full).astype(jnp.bfloat16)
    key_low = dot_low(normed_low, key_full).astype(jnp.bfloat16)
    value_low = dot_low(normed_low, value_full).astype(jnp.bfloat16)
    swish_in = dot_low(normed_low, swish_full)
    normed_wide = normed_low.astype(jnp.float32)
    low_rank = jnp.dot(normed_wide, rankin_full.astype(jnp.float32), precision=exact)
    log_decay, decay_back = jax.vjp(
        decay_map, low_rank, rankout_full.astype(jnp.float32), bias_full.astype(jnp.float32)
    )
    query_blocks = to_blocks(query_low.astype(jnp.float32), seq_count)
    key_blocks = to_blocks(key_low.astype(jnp.float32), seq_count)
    value_blocks = to_blocks(value_low.astype(jnp.float32), seq_count)
    decay_blocks = to_blocks(log_decay, seq_count)
    zero_log = jnp.zeros((seq_count, HEADS, key_size), jnp.float32)
    zero_state = jnp.zeros((seq_count, HEADS, key_size, value_size), jnp.float32)
    local_end, unused = lax.scan(
        state_step, (zero_log, zero_state), (key_blocks, value_blocks, decay_blocks)
    )
    end_log, end_state = local_end
    in_log, in_state = prefix((end_log, end_state), "seq", join_states, (zero_log, zero_state))
    mixer_result, mixer_back = jax.vjp(
        local_mixer, query_blocks, key_blocks, value_blocks, decay_blocks, in_state
    )
    mixed_rows = from_blocks(mixer_result[0])
    gated, gate_back = jax.vjp(gate_heads, mixed_rows, swish_in, headgain_full.astype(jnp.float32))
    gated_low = gated.astype(jnp.bfloat16)
    hidden = residual + dot_low(gated_low, output_full)
    hidden_norm, mlp_norm_back = jax.vjp(norm_rows, hidden, mlpgain_full.astype(jnp.float32))
    hidden_low = hidden_norm.astype(jnp.bfloat16)
    gate_val = dot_low(hidden_low, gate_full)
    up_val = dot_low(hidden_low, upward_full)
    product, swiglu_back = jax.vjp(swiglu, gate_val, up_val)
    product_low = product.astype(jnp.bfloat16)
    block_out = (
        (hidden + dot_low(product_low, down_full)).astype(jnp.bfloat16).reshape(tokens.shape)
    )
    attn_back = (
        lax.all_gather(query_proj, ("dp", "seq"), axis=0, tiled=True),
        lax.all_gather(key_proj, ("dp", "seq"), axis=0, tiled=True),
        lax.all_gather(value_proj, ("dp", "seq"), axis=0, tiled=True),
        lax.all_gather(swish_proj, ("dp", "seq"), axis=0, tiled=True),
        lax.all_gather(rank_in, ("dp", "seq"), axis=0, tiled=True),
        lax.all_gather(rank_out, ("dp", "seq"), axis=0, tiled=True),
        lax.all_gather(decay_bias, ("dp", "seq"), axis=0, tiled=True),
        lax.all_gather(attn_gain, ("dp", "seq"), axis=0, tiled=True),
        lax.all_gather(head_gain, ("dp", "seq"), axis=0, tiled=True),
        lax.all_gather(out_proj, ("dp", "seq"), axis=0, tiled=True),
    )
    mlp_back = (
        lax.all_gather(mlp_gain, ("dp", "seq"), axis=0, tiled=True),
        lax.all_gather(gate_proj, ("dp", "seq"), axis=0, tiled=True),
        lax.all_gather(up_proj, ("dp", "seq"), axis=0, tiled=True),
        lax.all_gather(down_proj, ("dp", "seq"), axis=0, tiled=True),
    )
    (
        query_full,
        key_full,
        value_full,
        swish_full,
        rankin_full,
        rankout_full,
        bias_full,
        attngain_full,
        headgain_full,
        output_full,
    ) = attn_back
    mlpgain_full, gate_full, upward_full, down_full = mlp_back
    parts_dp = lax.axis_size("dp")
    upstream = cotangent.reshape(rows_all, features)
    back_product = dot_right(upstream, down_full)
    grad_down = dot_left(product_low, upstream)
    back_gate, back_up = swiglu_back(back_product)
    gate_low = back_gate.astype(jnp.bfloat16)
    up_low = back_up.astype(jnp.bfloat16)
    back_hnorm = dot_right(gate_low, gate_full) + dot_right(up_low, upward_full)
    grad_gate = dot_left(hidden_low, gate_low)
    grad_upward = dot_left(hidden_low, up_low)
    back_hidden, grad_mlp_gain = mlp_norm_back(back_hnorm)
    back_hidden = back_hidden + upstream.astype(jnp.float32)
    mlp_first = (
        lax.psum_scatter(
            fold_rows(grad_mlp_gain, parts_dp).astype(jnp.bfloat16),
            "seq",
            scatter_dimension=1,
            tiled=True,
        ).astype(jnp.float32),
        lax.psum_scatter(
            fold_rows(grad_gate, parts_dp).astype(jnp.bfloat16),
            "seq",
            scatter_dimension=1,
            tiled=True,
        ).astype(jnp.float32),
        lax.psum_scatter(
            fold_rows(grad_upward, parts_dp).astype(jnp.bfloat16),
            "seq",
            scatter_dimension=1,
            tiled=True,
        ).astype(jnp.float32),
        lax.psum_scatter(
            fold_rows(grad_down, parts_dp).astype(jnp.bfloat16),
            "seq",
            scatter_dimension=1,
            tiled=True,
        ).astype(jnp.float32),
    )
    mlp_second = (
        lax.psum_scatter(
            mlp_first[0].astype(jnp.bfloat16), "dp", scatter_dimension=0, tiled=True
        ).astype(jnp.float32),
        lax.psum_scatter(
            mlp_first[1].astype(jnp.bfloat16), "dp", scatter_dimension=0, tiled=True
        ).astype(jnp.float32),
        lax.psum_scatter(
            mlp_first[2].astype(jnp.bfloat16), "dp", scatter_dimension=0, tiled=True
        ).astype(jnp.float32),
        lax.psum_scatter(
            mlp_first[3].astype(jnp.bfloat16), "dp", scatter_dimension=0, tiled=True
        ).astype(jnp.float32),
    )
    mlp_shards = tuple((unfold_rows(member) for member in mlp_second))
    back_attn = back_hidden.astype(jnp.bfloat16)
    back_gated = dot_right(back_attn, output_full)
    grad_output = dot_left(gated_low, back_attn)
    back_mixed, back_swish, grad_head_gain = gate_back(back_gated)
    swish_low = back_swish.astype(jnp.bfloat16)
    scaling = key_size ** (-0.5)
    query_heads = query_low.astype(jnp.float32).reshape(seq_count, tok_count, HEADS, key_size)
    decay_sums = jnp.cumsum(log_decay.reshape(seq_count, tok_count, HEADS, key_size), axis=1)
    back_heads = back_mixed.reshape(seq_count, tok_count, HEADS, value_size)
    direct_state = jnp.einsum(
        "sthk,sthv->shkv", query_heads * jnp.exp(decay_sums) * scaling, back_heads, precision=exact
    )
    later_log, out_state = entering(
        (end_log, direct_state), "seq", join_states, (zero_log, zero_state)
    )
    back_query, back_key, back_value, back_decay, unused = mixer_back(
        (to_blocks(back_mixed, seq_count), out_state)
    )
    query_back = from_blocks(back_query).astype(jnp.bfloat16)
    key_back = from_blocks(back_key).astype(jnp.bfloat16)
    value_back = from_blocks(back_value).astype(jnp.bfloat16)
    back_rank, grad_rank_out, grad_bias = decay_back(from_blocks(back_decay))
    back_normed = (
        dot_right(query_back, query_full)
        + dot_right(key_back, key_full)
        + dot_right(value_back, value_full)
        + dot_right(swish_low, swish_full)
    )
    back_normed = back_normed + dot_right(back_rank, rankin_full.astype(jnp.float32), exact)
    grad_query = dot_left(normed_low, query_back)
    grad_key = dot_left(normed_low, key_back)
    grad_value = dot_left(normed_low, value_back)
    grad_swish = dot_left(normed_low, swish_low)
    grad_rank_in = dot_left(normed_wide, back_rank, exact)
    back_tokens, grad_attn_gain = attn_norm_back(back_normed)
    grad_tokens = (back_tokens + back_hidden).astype(jnp.bfloat16).reshape(tokens.shape)
    attn_first = (
        lax.psum_scatter(
            fold_rows(grad_query, parts_dp).astype(jnp.bfloat16),
            "seq",
            scatter_dimension=1,
            tiled=True,
        ).astype(jnp.float32),
        lax.psum_scatter(
            fold_rows(grad_key, parts_dp).astype(jnp.bfloat16),
            "seq",
            scatter_dimension=1,
            tiled=True,
        ).astype(jnp.float32),
        lax.psum_scatter(
            fold_rows(grad_value, parts_dp).astype(jnp.bfloat16),
            "seq",
            scatter_dimension=1,
            tiled=True,
        ).astype(jnp.float32),
        lax.psum_scatter(
            fold_rows(grad_swish, parts_dp).astype(jnp.bfloat16),
            "seq",
            scatter_dimension=1,
            tiled=True,
        ).astype(jnp.float32),
        lax.psum_scatter(
            fold_rows(grad_rank_in, parts_dp).astype(jnp.bfloat16),
            "seq",
            scatter_dimension=1,
            tiled=True,
        ).astype(jnp.float32),
        lax.psum_scatter(
            fold_rows(grad_rank_out, parts_dp).astype(jnp.bfloat16),
            "seq",
            scatter_dimension=1,
            tiled=True,
        ).astype(jnp.float32),
        lax.psum_scatter(
            fold_rows(grad_bias, parts_dp).astype(jnp.bfloat16),
            "seq",
            scatter_dimension=1,
            tiled=True,
        ).astype(jnp.float32),
        lax.psum_scatter(
            fold_rows(grad_attn_gain, parts_dp).astype(jnp.bfloat16),
            "seq",
            scatter_dimension=1,
            tiled=True,
        ).astype(jnp.float32),
        lax.psum_scatter(
            fold_rows(grad_head_gain, parts_dp).astype(jnp.bfloat16),
            "seq",
            scatter_dimension=1,
            tiled=True,
        ).astype(jnp.float32),
        lax.psum_scatter(
            fold_rows(grad_output, parts_dp).astype(jnp.bfloat16),
            "seq",
            scatter_dimension=1,
            tiled=True,
        ).astype(jnp.float32),
    )
    attn_second = (
        lax.psum_scatter(
            attn_first[0].astype(jnp.bfloat16), "dp", scatter_dimension=0, tiled=True
        ).astype(jnp.float32),
        lax.psum_scatter(
            attn_first[1].astype(jnp.bfloat16), "dp", scatter_dimension=0, tiled=True
        ).astype(jnp.float32),
        lax.psum_scatter(
            attn_first[2].astype(jnp.bfloat16), "dp", scatter_dimension=0, tiled=True
        ).astype(jnp.float32),
        lax.psum_scatter(
            attn_first[3].astype(jnp.bfloat16), "dp", scatter_dimension=0, tiled=True
        ).astype(jnp.float32),
        lax.psum_scatter(
            attn_first[4].astype(jnp.bfloat16), "dp", scatter_dimension=0, tiled=True
        ).astype(jnp.float32),
        lax.psum_scatter(
            attn_first[5].astype(jnp.bfloat16), "dp", scatter_dimension=0, tiled=True
        ).astype(jnp.float32),
        lax.psum_scatter(
            attn_first[6].astype(jnp.bfloat16), "dp", scatter_dimension=0, tiled=True
        ).astype(jnp.float32),
        lax.psum_scatter(
            attn_first[7].astype(jnp.bfloat16), "dp", scatter_dimension=0, tiled=True
        ).astype(jnp.float32),
        lax.psum_scatter(
            attn_first[8].astype(jnp.bfloat16), "dp", scatter_dimension=0, tiled=True
        ).astype(jnp.float32),
        lax.psum_scatter(
            attn_first[9].astype(jnp.bfloat16), "dp", scatter_dimension=0, tiled=True
        ).astype(jnp.float32),
    )
    attn_shards = tuple((unfold_rows(member) for member in attn_second))
    return (
        block_out,
        grad_tokens,
        attn_shards[0],
        attn_shards[1],
        attn_shards[2],
        attn_shards[3],
        attn_shards[4],
        attn_shards[5],
        attn_shards[6],
        attn_shards[7],
        attn_shards[8],
        attn_shards[9],
        mlp_shards[0],
        mlp_shards[1],
        mlp_shards[2],
        mlp_shards[3],
    )


def solution(mesh):
    return jax.shard_map(
        per_device,
        mesh=mesh,
        in_specs=(
            P("dp", "seq", None),
            P(("dp", "seq"), None),
            P(("dp", "seq"), None),
            P(("dp", "seq"), None),
            P(("dp", "seq"), None),
            P(("dp", "seq"), None),
            P(("dp", "seq"), None),
            P(("dp", "seq")),
            P(("dp", "seq")),
            P(("dp", "seq")),
            P(("dp", "seq"), None),
            P(("dp", "seq")),
            P(("dp", "seq"), None),
            P(("dp", "seq"), None),
            P(("dp", "seq"), None),
            P("dp", "seq", None),
        ),
        out_specs=(
            P("dp", "seq", None),
            P("dp", "seq", None),
            P(("dp", "seq"), None),
            P(("dp", "seq"), None),
            P(("dp", "seq"), None),
            P(("dp", "seq"), None),
            P(("dp", "seq"), None),
            P(("dp", "seq"), None),
            P(("dp", "seq")),
            P(("dp", "seq")),
            P(("dp", "seq")),
            P(("dp", "seq"), None),
            P(("dp", "seq")),
            P(("dp", "seq"), None),
            P(("dp", "seq"), None),
            P(("dp", "seq"), None),
        ),
        check_vma=False,
    )
```

profile of v0, /device:TPU:5, one launch (start us, length us, event | category | flops | bytes accessed | tf_op | source)
XLA Modules:
  0.0 3663.3 jit_solution(3953163253730008426)
XLA Ops:
  12.9 39.9 %all-reduce.10 = (bf16[2048]{0:T(1024)(128)(2,1)S(1)}, bf16[1024]{0:T(1024)(128)(2,1)S(1)}, bf16[512]{0:T(512)(128)(2,1)S(1)}, bf16[2048]{0:T(1024)(128)(2,1)S(1)}) all-reduce(bf16[2048]{0:T(1024)(128)(2,1)S(1)} %dynamic-update-slice, bf16[1024]{0:T(1024)(128)(2,1)S(1)} %dynamic-update-slice.1, ...), channel_id=1, replica_groups=mesh['dp'=4,'seq'=8] {'dp','seq'}, use_global_device_ids=true, to_apply=%add.2 | all-reduce | flops 5632 | bytes 22528
  52.8 62.4 %all-gather.3 = bf16[32,64,16]{1,2,0:T(8,128)(2,1)S(1)} all-gather(bf16[1,64,16]{1,2,0:T(8,128)(2,1)} %bitcast.802), channel_id=1, replica_groups=mesh['dp'=4,'seq'=8] {'dp','seq'}, dimensions={0}, use_global_device_ids=true | all-gather | bytes 67584 | tf_op jit(solution)/shard_map/all_gather | solution.py:196
  115.4 63.7 %all-gather.4 = bf16[32,32,16]{1,2,0:T(8,128)(2,1)S(1)} all-gather(bf16[1,32,16]{1,2,0:T(8,128)(2,1)} %bitcast.803), channel_id=1, replica_groups=mesh['dp'=4,'seq'=8] {'dp','seq'}, dimensions={0}, use_global_device_ids=true | all-gather | bytes 33792 | tf_op jit(solution)/shard_map/all_gather | solution.py:197
  187.8 5.7 fusion.150
  197.9 9.2 while.106
  198.3 3.4 bitcast_add_fusion.12
  202.0 5.0 bitcast_add_fusion.12
  215.8 3.5 all-gather.20.cloned.1.call-done
  219.3 3.9 fusion.156
  231.7 23.5 all-gather
  255.1 89.7 %all-gather.32.cloned.1.call-done = bf16[8,4,256,512]{3,2,1,0:T(8,128)(2,1)} async-done(((bf16[1,4,256,512]{3,2,1,0:T(8,128)(2,1)}), bf16[8,4,256,512]{3,2,1,0:T(8,128)(2,1)}) %all-gather.32.cloned.1.call-update) | async-done | bytes 8388624 | tf_op jit(solution)/shard_map/all_gather | solution.py:17
  344.8 16.5 while.107
  368.0 30.3 while.104
  403.6 20.4 all-gather.22.cloned.1.call-done
  424.0 6.8 multiply_convert_fusion.4
  430.8 72.1 %all-gather.24.cloned.1.call-done = bf16[2048,2048]{1,0:T(8,128)(2,1)} async-done(((bf16[64,2048]{1,0:T(8,128)(2,1)}), bf16[2048,2048]{1,0:T(8,128)(2,1)}) %all-gather.24.cloned.1.call-update) | async-done | bytes 8388624 | tf_op jit(solution)/shard_map/all_gather | solution.py:201
  502.9 4.8 multiply_reduce_fusion.4
  508.8 140.2 %all-gather.26.cloned.1.call-done = bf16[2048,5632]{1,0:T(8,128)(2,1)} async-done(((bf16[64,5632]{1,0:T(8,128)(2,1)}), bf16[2048,5632]{1,0:T(8,128)(2,1)}) %all-gather.26.cloned.1.call-update) | async-done | bytes 23068688 | tf_op jit(solution)/shard_map/all_gather | solution.py:205
  649.0 12.3 fusion.219
  661.3 133.4 %all-gather.28.cloned.1.call-done = bf16[2048,5632]{1,0:T(8,128)(2,1)} async-done(((bf16[64,5632]{1,0:T(8,128)(2,1)}), bf16[2048,5632]{1,0:T(8,128)(2,1)}) %all-gather.28.cloned.1.call-update) | async-done | bytes 23068688 | tf_op jit(solution)/shard_map/all_gather | solution.py:206
  794.7 14.3 fusion.143
  809.1 131.4 %all-gather.30.cloned.1.call-done = bf16[5632,2048]{1,0:T(8,128)(2,1)} async-done(((bf16[176,2048]{1,0:T(8,128)(2,1)}), bf16[5632,2048]{1,0:T(8,128)(2,1)}) %all-gather.30.cloned.1.call-update) | async-done | bytes 23068688 | tf_op jit(solution)/shard_map/all_gather | solution.py:207
  940.5 14.8 multiply_convert_fusion
  955.3 13.0 fusion.220
  968.3 14.0 multiply_reduce_fusion
  984.2 8.0 multiply_reduce_fusion.1
  996.9 4.3 convolution_convert_fusion.9
  1006.6 8.1 fusion.223
  1014.7 108.9 %all-gather.34.cloned.1.call-done = bf16[32,256,512]{2,1,0:T(8,128)(2,1)} async-done(((bf16[4,256,512]{2,1,0:T(8,128)(2,1)}), bf16[32,256,512]{2,1,0:T(8,128)(2,1)}) %all-gather.34.cloned.1.call-update) | async-done | bytes 8388624 | tf_op jit(solution)/shard_map/all_gather | solution.py:40
  1123.6 16.5 while.108
  1145.1 52.2 %while.105 = (s32[]{:T(128)}, f32[1,4,256,512]{2,3,1,0:T(8,128)S(1)}, bf16[2,1,4,64,256]{4,3,2,1,0:T(8,128)(2,1)}, bf16[2,1,4,64,256]{4,3,2,1,0:T(8,128)(2,1)}, ...) while((s32[]{:T(128)}, ...), condition=%wide.region_22.23_spmd.clone, body=%wide.region_16.22_spmd.clone.sunk | while | flops 1921073152 | bytes 84444288 | solution.py:100
  1203.1 6.4 fusion.222
  1222.8 5.7 convolution_convert_fusion.3
  1232.3 3.2 convolution_convert_fusion.6
  1236.0 5.7 convolution_convert_fusion.5
  1242.8 5.6 convolution_convert_fusion.4
  1249.8 10.9 convolution_convert_fusion.2
  1262.1 10.9 convolution_convert_fusion.1
  1275.2 10.8 convolution_convert_fusion
  1291.2 49.5 %reduce-scatter.73.cloned.1.call-done = bf16[64,64]{1,0:T(8,128)(2,1)} async-done(((bf16[512,64]{1,0:T(8,128)(2,1)}), bf16[64,64]{1,0:T(8,128)(2,1)}) %reduce-scatter.73.cloned.1.call-update) | async-done | bytes 8208
  1342.3 152.5 %reduce-scatter.57.cloned.1.call-done = bf16[4,64,2048]{2,1,0:T(8,128)(2,1)} async-done(((bf16[4,512,2048]{2,1,0:T(8,128)(2,1)}), bf16[4,64,2048]{2,1,0:T(8,128)(2,1)}) %reduce-scatter.57.cloned.1.call-update) | async-done | bytes 1048592 | tf_op jit(solution)/shard_map/reduce_scatter | solution.py:438
  1494.8 91.3 %reduce-scatter.37.cloned.1.call-done = bf16[4,64,1024]{2,1,0:T(8,128)(2,1)} async-done(((bf16[4,512,1024]{2,1,0:T(8,128)(2,1)}), bf16[4,64,1024]{2,1,0:T(8,128)(2,1)}) %reduce-scatter.37.cloned.1.call-update) | async-done | bytes 524304 | tf_op jit(solution)/shard_map/reduce_scatter | solution.py:384
  1586.2 91.6 %reduce-scatter.41.cloned.1.call-done = bf16[4,64,1024]{2,1,0:T(8,128)(2,1)} async-done(((bf16[4,512,1024]{2,1,0:T(8,128)(2,1)}), bf16[4,64,1024]{2,1,0:T(8,128)(2,1)}) %reduce-scatter.41.cloned.1.call-update) | async-done | bytes 524304 | tf_op jit(solution)/shard_map/reduce_scatter | solution.py:390
  1677.9 153.1 %reduce-scatter.45.cloned.1.call-done = bf16[4,64,2048]{2,1,0:T(8,128)(2,1)} async-done(((bf16[4,512,2048]{2,1,0:T(8,128)(2,1)}), bf16[4,64,2048]{2,1,0:T(8,128)(2,1)}) %reduce-scatter.45.cloned.1.call-update) | async-done | bytes 1048592 | tf_op jit(solution)/shard_map/reduce_scatter | solution.py:396
  1831.0 151.8 %reduce-scatter.49.cloned.1.call-done = bf16[4,64,2048]{2,1,0:T(8,128)(2,1)} async-done(((bf16[4,512,2048]{2,1,0:T(8,128)(2,1)}), bf16[4,64,2048]{2,1,0:T(8,128)(2,1)}) %reduce-scatter.49.cloned.1.call-update) | async-done | bytes 1048592 | tf_op jit(solution)/shard_map/reduce_scatter | solution.py:402
  1983.0 376.8 %reduce-scatter.61.cloned.1.call-done = bf16[4,64,5632]{2,1,0:T(8,128)(2,1)} async-done(((bf16[4,512,5632]{2,1,0:T(8,128)(2,1)}), bf16[4,64,5632]{2,1,0:T(8,128)(2,1)}) %reduce-scatter.61.cloned.1.call-update) | async-done | bytes 2883600 | tf_op jit(solution)/shard_map/reduce_scatter | solution.py:313
  2359.8 377.1 %reduce-scatter.65.cloned.1.call-done = bf16[4,64,5632]{2,1,0:T(8,128)(2,1)} async-done(((bf16[4,512,5632]{2,1,0:T(8,128)(2,1)}), bf16[4,64,5632]{2,1,0:T(8,128)(2,1)}) %reduce-scatter.65.cloned.1.call-update) | async-done | bytes 2883600 | tf_op jit(solution)/shard_map/reduce_scatter | solution.py:319
  2737.6 376.2 %reduce-scatter.69.cloned.1.call-done = bf16[4,176,2048]{2,1,0:T(8,128)(2,1)} async-done(((bf16[4,1408,2048]{2,1,0:T(8,128)(2,1)}), bf16[4,176,2048]{2,1,0:T(8,128)(2,1)}) %reduce-scatter.69.cloned.1.call-update) | async-done | bytes 2883600 | tf_op jit(solution)/shard_map/reduce_scatter | solution.py:325
  3113.9 13.4 fusion.152
  3127.3 41.0 %reduce-scatter.81.cloned.1.call-done = bf16[16,4]{1,0:T(8,128)(2,1)} async-done(((bf16[128,4]{1,0:T(8,128)(2,1)}), bf16[16,4]{1,0:T(8,128)(2,1)}) %reduce-scatter.81.cloned.1.call-update) | async-done | bytes 144
  3169.1 63.7 %reduce-scatter.83.cloned.1.call-done = bf16[64,4]{1,0:T(8,128)(2,1)} async-done(((bf16[512,4]{1,0:T(8,128)(2,1)}), bf16[64,4]{1,0:T(8,128)(2,1)}) %reduce-scatter.83.cloned.1.call-update) | async-done | bytes 528
  3233.6 63.9 %reduce-scatter.77.cloned.1.call-done = bf16[32,4]{1,0:T(8,128)(2,1)} async-done(((bf16[256,4]{1,0:T(8,128)(2,1)}), bf16[32,4]{1,0:T(8,128)(2,1)}) %reduce-scatter.77.cloned.1.call-update) | async-done | bytes 272
  3298.2 63.2 %reduce-scatter.79.cloned.1.call-done = bf16[64,4]{1,0:T(8,128)(2,1)} async-done(((bf16[512,4]{1,0:T(8,128)(2,1)}), bf16[64,4]{1,0:T(8,128)(2,1)}) %reduce-scatter.79.cloned.1.call-update) | async-done | bytes 528
  3362.3 7.6 all-reduce.11
  3374.5 8.7 reduce-scatter.55.cloned.1.call-done
  3384.5 20.9 reduce-scatter.53.cloned.1.call-done
  3406.7 26.8 reduce-scatter.59.cloned.1.call-done
  3435.3 22.4 reduce-scatter.39.cloned.1.call-done
  3459.3 22.7 reduce-scatter.43.cloned.1.call-done
  3483.6 25.6 reduce-scatter.47.cloned.1.call-done
  3511.1 25.8 reduce-scatter.51.cloned.1.call-done
  3538.7 37.2 %reduce-scatter.63.cloned.1.call-done = bf16[1,64,5632]{2,1,0:T(8,128)(2,1)} async-done(((bf16[4,64,5632]{2,1,0:T(8,128)(2,1)}), bf16[1,64,5632]{2,1,0:T(8,128)(2,1)}) %reduce-scatter.63.cloned.1.call-update) | async-done | bytes 720912 | tf_op jit(solution)/shard_map/reduce_scatter | solution.py:336
  3578.1 36.6 reduce-scatter.67.cloned.1.call-done
  3617.1 36.6 %reduce-scatter.71.cloned.1.call-done = bf16[1,176,2048]{2,1,0:T(8,128)(2,1)} async-done(((bf16[4,176,2048]{2,1,0:T(8,128)(2,1)}), bf16[1,176,2048]{2,1,0:T(8,128)(2,1)}) %reduce-scatter.71.cloned.1.call-update) | async-done | bytes 720912 | tf_op jit(solution)/shard_map/reduce_scatter | solution.py:342
  (536 shorter events, 242.1 us)
Async XLA Ops:
  7.2 177.1 %all-gather.16.cloned.1.call-start = ((), (), s32[]{:S(2)}) async-start(), calls=%async_computation.24 | async-start | bytes 4325376 | tf_op jit(solution)/shard_map/all_gather | solution.py:193
  7.9 176.4 %copy-start.17 = (bf16[1,128,2048]{2,1,0:T(8,128)(2,1)S(1)}, bf16[1,128,2048]{2,1,0:T(8,128)(2,1)}, u32[]{:S(2)}) copy-start(bf16[1,128,2048]{2,1,0:T(8,128)(2,1)} %param.26) | copy-start | bytes 1572868
  7.9 179.9 %all-gather.18.cloned.1.call-start = ((), (), s32[]{:S(2)}) async-start(), calls=%async_computation.25 | async-start | bytes 8650752 | tf_op jit(solution)/shard_map/all_gather | solution.py:194
  8.7 210.6 %all-gather.20.cloned.1.call-start = ((), (), s32[]{:S(2)}) async-start(), calls=%async_computation.26 | async-start | bytes 4325376 | tf_op jit(solution)/shard_map/all_gather | solution.py:192
  9.4 335.4 %all-gather.32.cloned.1.call-start = ((), (), s32[]{:S(2)}) async-start(), calls=%async_computation.50 | async-start | bytes 9437184 | tf_op jit(solution)/shard_map/all_gather | solution.py:17
  115.4 65.8 %copy-start.63 = (bf16[2048,16]{0,1:T(8,128)(2,1)}, bf16[2048,16]{0,1:T(8,128)(2,1)S(1)}, u32[]{:S(2)}) copy-start(bf16[2048,16]{0,1:T(8,128)(2,1)S(1)} %reshape.1056) | copy-start | bytes 196612
  179.3 8.0 copy-start.65
  182.5 4.8 copy-start.68
  207.1 5.8 copy-start
  207.1 5.8 copy-start.24
  210.2 213.8 %all-gather.22.cloned.1.call-start = ((), (), s32[]{:S(2)}) async-start(), calls=%async_computation.27 | async-start | bytes 8650752 | tf_op jit(solution)/shard_map/all_gather | solution.py:195
  210.8 292.1 %all-gather.24.cloned.1.call-start = ((), (), s32[]{:S(2)}) async-start(), calls=%async_computation.28 | async-start | bytes 8650752 | tf_op jit(solution)/shard_map/all_gather | solution.py:201
  211.3 437.7 %all-gather.26.cloned.1.call-start = ((), (), s32[]{:S(2)}) async-start(), calls=%async_computation.29 | async-start | bytes 23789568 | tf_op jit(solution)/shard_map/all_gather | solution.py:205
  212.1 582.7 %all-gather.28.cloned.1.call-start = ((), (), s32[]{:S(2)}) async-start(), calls=%async_computation.30 | async-start | bytes 23789568 | tf_op jit(solution)/shard_map/all_gather | solution.py:206
  212.9 727.7 %all-gather.30.cloned.1.call-start = ((), (), s32[]{:S(2)}) async-start(), calls=%async_computation.31 | async-start | bytes 23789568 | tf_op jit(solution)/shard_map/all_gather | solution.py:207
  213.6 910.0 %all-gather.34.cloned.1.call-start = ((), (), s32[]{:S(2)}) async-start(), calls=%async_computation.51 | async-start | bytes 9437184 | tf_op jit(solution)/shard_map/all_gather | solution.py:40
  371.5 6.0 copy-start.1
  386.5 6.0 copy-start.1
  400.4 23.6 copy-start.18
  430.8 76.8 %copy-start.49 = (bf16[128,2048]{1,0:T(8,128)(2,1)}, bf16[128,2048]{1,0:T(8,128)(2,1)S(1)}, u32[]{:S(2)}) copy-start(bf16[128,2048]{1,0:T(8,128)(2,1)S(1)} %get-tuple-element.1328) | copy-start | bytes 1572868
  508.8 286.0 %copy-start.32 = (bf16[128,2048]{1,0:T(8,128)(2,1)}, bf16[128,2048]{1,0:T(8,128)(2,1)S(1)}, u32[]{:S(2)}) copy-start(bf16[128,2048]{1,0:T(8,128)(2,1)S(1)} %multiply_convert_fusion.3) | copy-start | bytes 1572868
  661.3 279.2 %copy-start.54 = (bf16[1,128,2048]{2,1,0:T(8,128)(2,1)S(1)}, bf16[1,128,2048]{2,1,0:T(8,128)(2,1)}, u32[]{:S(2)}) copy-start(bf16[1,128,2048]{2,1,0:T(8,128)(2,1)} %param.41) | copy-start | bytes 1572868
  955.3 13.0 copy-start.27
  984.0 8.1 copy-start.35
  992.1 4.7 copy-start.56
  1001.2 288.4 %reduce-scatter.75.cloned.1.call-start = ((), (), s32[]{:S(2)}) async-start(), calls=%async_computation.53 | async-start | bytes 73728
  1001.3 5.4 copy-start.52
  1153.4 3.8 copy-start.2
  1153.4 3.8 copy-start.10
  1157.3 4.7 copy-start.45
  1161.3 3.9 copy-start.16
  1161.3 3.9 copy-start.48
  1179.2 3.8 copy-start.2
  1179.2 3.8 copy-start.10
  1183.1 4.7 copy-start.45
  1187.1 3.9 copy-start.16
  1187.1 3.9 copy-start.48
  1203.1 6.5 copy-start.30
  1214.9 7.9 copy-start.50
  1219.0 121.7 %reduce-scatter.73.cloned.1.call-start = ((), (), s32[]{:S(2)}) async-start(), calls=%async_computation.52 | async-start | bytes 147456
  1222.7 272.1 %reduce-scatter.57.cloned.1.call-start = ((), (), s32[]{:S(2)}) async-start(), calls=%async_computation.42 | async-start | bytes 9437184 | tf_op jit(solution)/shard_map/reduce_scatter | solution.py:438
  1228.4 357.7 %reduce-scatter.37.cloned.1.call-start = ((), (), s32[]{:S(2)}) async-start(), calls=%async_computation.32 | async-start | bytes 4718592 | tf_op jit(solution)/shard_map/reduce_scatter | solution.py:384
  1232.1 445.7 %reduce-scatter.41.cloned.1.call-start = ((), (), s32[]{:S(2)}) async-start(), calls=%async_computation.34 | async-start | bytes 4718592 | tf_op jit(solution)/shard_map/reduce_scatter | solution.py:390
  1235.6 595.4 %reduce-scatter.45.cloned.1.call-start = ((), (), s32[]{:S(2)}) async-start(), calls=%async_computation.36 | async-start | bytes 9437184 | tf_op jit(solution)/shard_map/reduce_scatter | solution.py:396
  1241.7 741.1 %reduce-scatter.49.cloned.1.call-start = ((), (), s32[]{:S(2)}) async-start(), calls=%async_computation.38 | async-start | bytes 9437184 | tf_op jit(solution)/shard_map/reduce_scatter | solution.py:402
  1248.4 1111.4 %reduce-scatter.61.cloned.1.call-start = ((), (), s32[]{:S(2)}) async-start(), calls=%async_computation.44 | async-start | bytes 25952256 | tf_op jit(solution)/shard_map/reduce_scatter | solution.py:313
  1260.8 1476.2 %reduce-scatter.65.cloned.1.call-start = ((), (), s32[]{:S(2)}) async-start(), calls=%async_computation.46 | async-start | bytes 25952256 | tf_op jit(solution)/shard_map/reduce_scatter | solution.py:319
  1273.0 1840.8 %reduce-scatter.69.cloned.1.call-start = ((), (), s32[]{:S(2)}) async-start(), calls=%async_computation.48 | async-start | bytes 25952256 | tf_op jit(solution)/shard_map/reduce_scatter | solution.py:325
  1286.1 1882.3 %reduce-scatter.81.cloned.1.call-start = ((), (), s32[]{:S(2)}) async-start(), calls=%async_computation.56 | async-start | bytes 36864
  1286.9 1945.9 %reduce-scatter.83.cloned.1.call-start = ((), (), s32[]{:S(2)}) async-start(), calls=%async_computation.57 | async-start | bytes 147456
  1287.8 2009.6 %reduce-scatter.77.cloned.1.call-start = ((), (), s32[]{:S(2)}) async-start(), calls=%async_computation.54 | async-start | bytes 73728
  1288.7 2072.8 %reduce-scatter.79.cloned.1.call-start = ((), (), s32[]{:S(2)}) async-start(), calls=%async_computation.55 | async-start | bytes 147456
  1289.6 2093.7 %reduce-scatter.55.cloned.1.call-start = ((), (), s32[]{:S(2)}) async-start(), calls=%async_computation.41 | async-start | bytes 20480 | tf_op jit(solution)/shard_map/reduce_scatter | solution.py:461
  1291.1 2114.3 %reduce-scatter.53.cloned.1.call-start = ((), (), s32[]{:S(2)}) async-start(), calls=%async_computation.40 | async-start | bytes 20480 | tf_op jit(solution)/shard_map/reduce_scatter | solution.py:458
  1342.2 2091.3 %reduce-scatter.59.cloned.1.call-start = ((), (), s32[]{:S(2)}) async-start(), calls=%async_computation.43 | async-start | bytes 1310720 | tf_op jit(solution)/shard_map/reduce_scatter | solution.py:473
  1494.8 1962.9 %reduce-scatter.39.cloned.1.call-start = ((), (), s32[]{:S(2)}) async-start(), calls=%async_computation.33 | async-start | bytes 655360 | tf_op jit(solution)/shard_map/reduce_scatter | solution.py:446
  1586.2 1895.9 %reduce-scatter.43.cloned.1.call-start = ((), (), s32[]{:S(2)}) async-start(), calls=%async_computation.35 | async-start | bytes 655360 | tf_op jit(solution)/shard_map/reduce_scatter | solution.py:449
  1677.9 1831.4 %reduce-scatter.47.cloned.1.call-start = ((), (), s32[]{:S(2)}) async-start(), calls=%async_computation.37 | async-start | bytes 1310720 | tf_op jit(solution)/shard_map/reduce_scatter | solution.py:452
  1831.0 1705.9 %reduce-scatter.51.cloned.1.call-start = ((), (), s32[]{:S(2)}) async-start(), calls=%async_computation.39 | async-start | bytes 1310720 | tf_op jit(solution)/shard_map/reduce_scatter | solution.py:455
  1982.9 1592.9 %reduce-scatter.63.cloned.1.call-start = ((), (), s32[]{:S(2)}) async-start(), calls=%async_computation.45 | async-start | bytes 3604480 | tf_op jit(solution)/shard_map/reduce_scatter | solution.py:336
  2359.8 377.2 %copy-start.72 = (u32[32]{0:T(128)S(1)}, u32[32]{0:T(128)}, u32[]{:S(2)}) copy-start(u32[32]{0:T(128)} %constant.275) | copy-start | bytes 388
  2359.8 1255.0 %reduce-scatter.67.cloned.1.call-start = ((), (), s32[]{:S(2)}) async-start(), calls=%async_computation.47 | async-start | bytes 3604480 | tf_op jit(solution)/shard_map/reduce_scatter | solution.py:339
  2736.9 376.9 %copy-start.28 = (f32[128,2048]{1,0:T(8,128)S(1)}, f32[128,2048]{1,0:T(8,128)}, u32[]{:S(2)}) copy-start(f32[128,2048]{1,0:T(8,128)} %copy-done.26) | copy-start | bytes 3145732
  2736.9 916.7 %reduce-scatter.71.cloned.1.call-start = ((), (), s32[]{:S(2)}) async-start(), calls=%async_computation.49 | async-start | bytes 3604480 | tf_op jit(solution)/shard_map/reduce_scatter | solution.py:342
  (78 other events, 167.2 us)
Sparse Core Ops, SparseCore 0:
  11.0 64.5 all-gather.15
  78.6 76.8 all-gather.17
  158.5 60.7 all-gather.19
  221.8 122.9 all-gather.31
  347.7 76.2 all-gather.21
  426.8 75.9 all-gather.23
  505.8 143.1 all-gather.25
  651.9 142.7 all-gather.27
  797.7 142.8 all-gather.29
  1001.3 122.2 all-gather.33
  1219.1 57.8 reduce-scatter.74
  1280.8 59.8 reduce-scatter.72
  1344.3 150.3 reduce-scatter.56
  1498.7 87.4 reduce-scatter.36
  1589.6 88.1 reduce-scatter.40
  1681.8 149.1 reduce-scatter.44
  1834.4 148.3 reduce-scatter.48
  1987.1 372.6 reduce-scatter.60
  2364.1 372.7 reduce-scatter.64
  2741.1 372.6 reduce-scatter.68
  3117.9 50.4 reduce-scatter.80
  3172.6 60.1 reduce-scatter.82
  3237.1 60.2 reduce-scatter.76
  3301.6 59.8 reduce-scatter.78
  3364.6 18.6 reduce-scatter.54
  3386.1 19.2 reduce-scatter.52
  3407.9 25.5 reduce-scatter.58
  3436.0 21.6 reduce-scatter.38
  3460.4 21.6 reduce-scatter.42
  3484.4 24.8 reduce-scatter.46
  3512.0 24.8 reduce-scatter.50
  3539.4 36.3 reduce-scatter.62
  3578.4 36.3 reduce-scatter.66
  3617.3 36.3 reduce-scatter.70
where the time goes:
time: 3680 us; the launch traced here: 3660 us
  waiting for transfers between devices  3020 us (82%)
  matrix products  247 us (7%)
  blocking collectives  197 us (5%)
  local copies, waits for them, and re-layouts  91.8 us (2%)
  other arithmetic  86.7 us (2%)
    reduce_scatter x1, waiting for transfers between devices, per_device(): lax.psum_scatter(fold_rows(grad_upward, parts_dp).astype(jnp.bfloat16), '...  377 us
    reduce_scatter x1, waiting for transfers between devices, per_device(): lax.psum_scatter(fold_rows(grad_gate, parts_dp).astype(jnp.bfloat16), 'se...  377 us
    reduce_scatter x1, waiting for transfers between devices, per_device(): lax.psum_scatter(fold_rows(grad_down, parts_dp).astype(jnp.bfloat16), 'se...  376 us
    unnamed x40, waiting for transfers between devices  287 us
    reduce_scatter x1, waiting for transfers between devices, per_device(): lax.psum_scatter(fold_rows(grad_value, parts_dp).astype(jnp.bfloat16), 's...  153 us
    reduce_scatter x1, waiting for transfers between devices, per_device(): lax.psum_scatter(fold_rows(grad_output, parts_dp).astype(jnp.bfloat16), '...  152 us
    reduce_scatter x1, waiting for transfers between devices, per_device(): lax.psum_scatter(fold_rows(grad_swish, parts_dp).astype(jnp.bfloat16), 's...  152 us
    all_gather x1, waiting for transfers between devices, per_device(): lax.all_gather(gate_proj, ('dp', 'seq'), axis=0, tiled=True)  140 us
  transfers between devices with their start and end apart: 34, of which 31 were waited for; matrix products, arithmetic and copies ran while one was open for 7% of the time, Pallas kernels for 0%

commit v1 on v0

v1 whole, which is shorter than its diff:
```python
import functools

import jax
import jax.numpy as jnp
from jax import lax
from jax.experimental import pallas as pl
from jax.experimental.pallas import tpu as pltpu
from jax.sharding import Mesh, PartitionSpec as P

HEADS = 4
BLOCK = 64
EPS = 1e-06
F32 = jnp.float32
BF16 = jnp.bfloat16
EXACT = lax.Precision.HIGHEST
WAYS = ("y", "core", "hi", "t")


def to_partner(value, r):
    return lax.ppermute(value, "t", [(s, s ^ r) for s in range(HEADS)])


def swap(value, axis):
    return lax.ppermute(value, axis, [(0, 1), (1, 0)])


def natural(pieces):
    t = lax.axis_index("t")
    odd, high = (t & 1) == 1, (t & 2) == 2
    a, b, c, d = pieces
    a, b = jnp.where(odd, b, a), jnp.where(odd, a, b)
    c, d = jnp.where(odd, d, c), jnp.where(odd, c, d)
    return (
        jnp.where(high, c, a),
        jnp.where(high, d, b),
        jnp.where(high, a, c),
        jnp.where(high, b, d),
    )


def gather_rows(value):
    return jnp.concatenate([value] + [to_partner(value, r) for r in range(1, HEADS)])


def scatter_rows(value):
    rows = value.shape[0] // HEADS
    parts = [value[r * rows : (r + 1) * rows] for r in range(HEADS)]
    total = parts[0].astype(F32)
    for r in range(1, HEADS):
        total = total + to_partner(parts[r], r).astype(F32)
    return total


def stage(value, axis):
    if lax.axis_size(axis) != 2:
        return lax.all_gather(value, axis, axis=0, tiled=True)
    other = swap(value, axis)
    first = lax.axis_index(axis) == 0
    return jnp.concatenate([jnp.where(first, value, other), jnp.where(first, other, value)])


def stage_core(value):
    other = swap(value, "core")
    first = lax.axis_index("core") == 0
    half = value.shape[0] // 2
    out = []
    for i in range(2):
        v, o = value[i * half : (i + 1) * half], other[i * half : (i + 1) * half]
        out += [jnp.where(first, v, o), jnp.where(first, o, v)]
    return jnp.concatenate(out)


def slices_for(parts):
    four = []
    for n in range(HEADS):
        cols = [p[:, n * (p.shape[1] // HEADS) : (n + 1) * (p.shape[1] // HEADS)] for p in parts]
        four.append(jnp.concatenate(cols, axis=1) if len(cols) > 1 else cols[0])
    return natural(four)


def exchange_columns(parts):
    sent = slices_for(parts)
    got = [sent[0]] + [to_partner(sent[r], r) for r in range(1, HEADS)]
    return jnp.concatenate(natural(got))


def gather_columns(parts):
    return stage_core(stage(stage(exchange_columns(parts), "hi"), "y"))


def transposed(value):
    n_hi = lax.axis_size("hi")
    pairs = [
        ((i * n_hi + h) * HEADS + t, (t * n_hi + h) * HEADS + i)
        for i in range(HEADS)
        for h in range(n_hi)
        for t in range(HEADS)
    ]
    return lax.ppermute(value, WAYS, pairs)


def dot(a, b, precision=None):
    return jnp.dot(a, b, precision=precision, preferred_element_type=F32)


def dot_nt(a, b, precision=None):
    return lax.dot_general(
        a, b, (((1,), (1,)), ((), ())), precision=precision, preferred_element_type=F32
    )


def dot_tn(a, b, precision=None):
    return lax.dot_general(
        a, b, (((0,), (0,)), ((), ())), precision=precision, preferred_element_type=F32
    )


def lower(n, kind=F32):
    return (
        lax.broadcasted_iota(jnp.int32, (n, n), 0) >= lax.broadcasted_iota(jnp.int32, (n, n), 1)
    ).astype(kind)


def upper(n, kind=F32):
    return (
        lax.broadcasted_iota(jnp.int32, (n, n), 0) <= lax.broadcasted_iota(jnp.int32, (n, n), 1)
    ).astype(kind)


def running(log_decay):
    return dot(lower(log_decay.shape[0]), log_decay, EXACT)


def state_kernel(t_ref, k_ref, v_ref, ld_ref, end_ref, total_ref, state, total):
    step = pl.program_id(0)

    @pl.when(step == 0)
    def _():
        state[...] = jnp.zeros_like(state)
        total[...] = jnp.zeros_like(total)

    cum = running(ld_ref[...])
    last = cum[BLOCK - 1 :, :]
    key_last = (k_ref[...].astype(F32) * jnp.exp(last - cum)).astype(BF16)
    state[...] = state[...] * jnp.exp(last) + dot_tn(v_ref[...], key_last)
    total[...] += last

    @pl.when(step == pl.num_programs(0) - 1)
    def _():
        end_ref[...] = state[...].astype(BF16)
        total_ref[...] = total[...]


def forward_kernel(
    t_ref, q_ref, k_ref, v_ref, ld_ref, sw_ref, gain_ref, in_ref,
    gated_ref, mixed_ref, saved_ref, state,
):
    @pl.when(pl.program_id(0) == 0)
    def _():
        state[...] = in_ref[...].astype(F32)

    cum = running(ld_ref[...])
    last, mid = cum[BLOCK - 1 :, :], cum[BLOCK // 2 : BLOCK // 2 + 1, :]
    scale = q_ref.shape[1] ** -0.5
    query = q_ref[...].astype(F32) * scale
    key = k_ref[...].astype(F32)
    value = v_ref[...]
    query_state = (query * jnp.exp(cum)).astype(BF16)
    query_mid = (query * jnp.exp(cum - mid)).astype(BF16)
    key_mid = (key * jnp.exp(mid - cum)).astype(BF16)
    key_last = (key * jnp.exp(last - cum)).astype(BF16)
    low = state[...].astype(BF16)
    saved_ref[0] = low
    scores = jnp.where(lower(BLOCK) > 0, dot_nt(query_mid, key_mid), 0.0).astype(BF16)
    mixed = dot_nt(query_state, low) + dot(scores, value)
    state[...] = state[...] * jnp.exp(last) + dot_tn(value, key_last)
    mixed_ref[...] = mixed
    swish = sw_ref[...]
    normed = mixed * lax.rsqrt(jnp.mean(mixed * mixed, axis=-1, keepdims=True) + EPS)
    gated = normed * gain_ref[...] * (swish / (1.0 + jnp.exp(-swish)))
    gated_ref[...] = gated.astype(BF16)


def gate_back_kernel(
    t_ref, bg_ref, mixed_ref, sw_ref, gain_ref, q_ref, ld_ref,
    bm_ref, bs_ref, gain_grad_ref, direct_ref, state, total,
):
    step = pl.program_id(0)

    @pl.when(step == 0)
    def _():
        state[...] = jnp.zeros_like(state)
        total[...] = jnp.zeros_like(total)
        gain_grad_ref[...] = jnp.zeros_like(gain_grad_ref)

    mixed, swish, gain, back = mixed_ref[...], sw_ref[...], gain_ref[...], bg_ref[...]
    inv = lax.rsqrt(jnp.mean(mixed * mixed, axis=-1, keepdims=True) + EPS)
    unit = mixed * inv
    sig = 1.0 / (1.0 + jnp.exp(-swish))
    dy = back * (swish * sig)
    bs_ref[...] = (back * (unit * gain) * (sig * (1.0 + swish * (1.0 - sig)))).astype(BF16)
    gain_grad_ref[...] += jnp.sum(dy * unit, axis=0, keepdims=True)
    gdy = gain * dy
    back_mixed = inv * (gdy - unit * jnp.mean(unit * gdy, axis=-1, keepdims=True))
    low = back_mixed.astype(BF16)
    bm_ref[...] = low
    cum = running(ld_ref[...])
    scale = q_ref.shape[1] ** -0.5
    query_start = (q_ref[...].astype(F32) * scale * jnp.exp(cum + total[...])).astype(BF16)
    state[...] += dot_tn(low, query_start)
    total[...] += cum[BLOCK - 1 :, :]

    @pl.when(step == pl.num_programs(0) - 1)
    def _():
        direct_ref[...] = state[...].astype(BF16)


def backward_kernel(
    t_ref, q_ref, k_ref, v_ref, ld_ref, sig_ref, bm_ref, saved_ref, out_ref,
    dq_ref, dk_ref, dv_ref, dl_ref, grad,
):
    @pl.when(pl.program_id(0) == 0)
    def _():
        grad[...] = out_ref[...].astype(F32)

    cum = running(ld_ref[...])
    last, mid = cum[BLOCK - 1 :, :], cum[BLOCK // 2 : BLOCK // 2 + 1, :]
    scale = q_ref.shape[1] ** -0.5
    query = q_ref[...].astype(F32)
    key = k_ref[...].astype(F32)
    value, back = v_ref[...], bm_ref[...]
    e_state = jnp.exp(cum) * scale
    e_query = jnp.exp(cum - mid) * scale
    e_key = jnp.exp(mid - cum)
    e_last = jnp.exp(last - cum)
    query_state = (query * e_state).astype(BF16)
    query_mid = (query * e_query).astype(BF16)
    key_mid = (key * e_key).astype(BF16)
    key_last = (key * e_last).astype(BF16)
    mask = lower(BLOCK) > 0
    scores = jnp.where(mask, dot_nt(query_mid, key_mid), 0.0).astype(BF16)
    back_scores = jnp.where(mask, dot_nt(back, value), 0.0).astype(BF16)
    start = saved_ref[0]
    wide = grad[...]
    low = wide.astype(BF16)
    back_query = dot(back, start) * e_state + dot(back_scores, key_mid) * e_query
    key_end = dot(value, low) * e_last
    back_key = dot_tn(back_scores, query_mid) * e_key + key_end
    dv_ref[...] = (dot_tn(scores, back) + dot_nt(key_last, low)).astype(BF16)
    dq_ref[...] = back_query.astype(BF16)
    dk_ref[...] = back_key.astype(BF16)
    at_end = jnp.exp(last) * jnp.sum(start.astype(F32) * wide, axis=0, keepdims=True)
    at_end = at_end + jnp.sum(key * key_end, axis=0, keepdims=True)
    back_cum = query * back_query - key * back_key
    back_decay = dot(upper(BLOCK), back_cum, EXACT) + at_end
    dl_ref[...] = back_decay * sig_ref[...]
    grad[...] = wide * jnp.exp(last) + dot_tn(back, query_state)


def recurrence_calls(rows, local, key_size, value_size):
    blocks = rows // BLOCK
    each = local // BLOCK

    def at(step, t_ref):
        return jnp.bitwise_xor(step // each, t_ref[0]) * each + step % each

    def ahead(width):
        return pl.BlockSpec((BLOCK, width), lambda s, t_ref: (at(s, t_ref), 0))

    def behind(width):
        return pl.BlockSpec((BLOCK, width), lambda s, t_ref: (at(blocks - 1 - s, t_ref), 0))

    def whole(*shape):
        return pl.BlockSpec(shape, lambda s, t_ref: (0,) * len(shape))

    def shape(*dims, kind=BF16):
        return jax.ShapeDtypeStruct(dims, kind)

    params = pltpu.CompilerParams(
        dimension_semantics=("arbitrary",), vmem_limit_bytes=24 * 1024 * 1024
    )
    k, v = key_size, value_size

    def call(kernel, ins, outs, out_shape, scratch, flops, moved):
        return pl.pallas_call(
            kernel,
            grid_spec=pltpu.PrefetchScalarGridSpec(
                num_scalar_prefetch=1,
                grid=(blocks,),
                in_specs=ins,
                out_specs=outs,
                scratch_shapes=scratch,
            ),
            out_shape=out_shape,
            compiler_params=params,
            cost_estimate=pl.CostEstimate(
                flops=flops, transcendentals=rows * k * 4, bytes_accessed=moved
            ),
        )

    unit = 2 * rows * k * v
    state = call(
        state_kernel,
        [ahead(k), ahead(v), ahead(k)],
        [whole(v, k), whole(1, k)],
        [shape(v, k), shape(1, k, kind=F32)],
        [pltpu.VMEM((v, k), F32), pltpu.VMEM((1, k), F32)],
        unit,
        rows * (6 * k + 2 * v),
    )
    forward = call(
        forward_kernel,
        [ahead(k), ahead(k), ahead(v), ahead(k), ahead(v), whole(1, v), whole(v, k)],
        [ahead(v), ahead(v), pl.BlockSpec((1, v, k), lambda s, t_ref: (s, 0, 0))],
        [shape(rows, v), shape(rows, v, kind=F32), shape(blocks, v, k)],
        [pltpu.VMEM((v, k), F32)],
        3 * unit,
        rows * (8 * k + 12 * v),
    )
    gate_back = call(
        gate_back_kernel,
        [ahead(v), ahead(v), ahead(v), whole(1, v), ahead(k), ahead(k)],
        [ahead(v), ahead(v), whole(1, v), whole(v, k)],
        [shape(rows, v), shape(rows, v), shape(1, v, kind=F32), shape(v, k)],
        [pltpu.VMEM((v, k), F32), pltpu.VMEM((1, k), F32)],
        unit,
        rows * (6 * k + 16 * v),
    )
    backward = call(
        backward_kernel,
        [
            behind(k), behind(k), behind(v), behind(k), behind(k), behind(v),
            pl.BlockSpec((1, v, k), lambda s, t_ref: (blocks - 1 - s, 0, 0)), whole(v, k),
        ],
        [behind(k), behind(k), behind(v), behind(k)],
        [shape(rows, k), shape(rows, k), shape(rows, v), shape(rows, k, kind=F32)],
        [pltpu.VMEM((v, k), F32)],
        6 * unit,
        rows * (16 * k + 8 * v),
    )
    return state, forward, gate_back, backward


def chain(local, total, upward):
    n = lax.axis_size("hi")
    entering = jnp.zeros(local.shape, BF16)
    keep = jnp.exp(total)
    for s in range(n - 1):
        leaving = local
        if s:
            leaving = (local.astype(F32) + entering.astype(F32) * keep).astype(BF16)
        pair = (s, s + 1) if upward else (n - 1 - s, n - 2 - s)
        got = lax.ppermute(leaving, "hi", [pair])
        entering = entering + got if s else got
    return entering


def inverse(values):
    return lax.rsqrt(jnp.mean(values * values, axis=-1, keepdims=True) + EPS)


def norm_back(values, gain, dy):
    inv = inverse(values)
    unit = values * inv
    gdy = gain * dy
    dx = inv * (gdy - unit * jnp.mean(unit * gdy, axis=-1, keepdims=True))
    return dx, jnp.sum(dy * unit, axis=0)


def per_device(
    tokens,
    query_proj,
    key_proj,
    value_proj,
    swish_proj,
    rank_in,
    rank_out,
    decay_bias,
    attn_gain,
    head_gain,
    out_proj,
    mlp_gain,
    gate_proj,
    up_proj,
    down_proj,
    cotangent,
):
    _, local, width = tokens.shape
    t = lax.axis_index("t")
    devices = 1
    for axis in WAYS:
        devices *= lax.axis_size(axis)
    rank = rank_in.shape[1]
    keys_all = query_proj.shape[1]
    key_size, value_size = keys_all // HEADS, width // HEADS
    rows = local * HEADS

    small = (
        attn_gain, mlp_gain, head_gain, decay_bias, rank_in.reshape(-1), rank_out.reshape(-1),
    )
    sizes = [s.shape[0] for s in small]
    pad = -sum(sizes) % 1024
    packed = jnp.concatenate(small + (jnp.zeros((pad,), BF16),))
    packed = lax.all_gather(packed, WAYS, axis=0)
    got, place = [], 0
    for size in sizes:
        got.append(packed[:, place : place + size].reshape(-1))
        place += size
    attn_full, mlp_full, head_full, bias_full = [g.astype(F32) for g in got[:4]]
    rankin_full = got[4].reshape(width, rank)
    rankout_own = lax.dynamic_slice_in_dim(
        got[5].reshape(keys_all, rank), t * key_size, key_size, 0
    ).astype(F32)
    bias_own = lax.dynamic_slice_in_dim(bias_full, t * key_size, key_size, 0)

    residual = tokens[0].astype(F32)
    tokens_all = gather_rows(tokens[0])
    kv_full = gather_columns((key_proj, value_proj))
    qs_full = gather_columns((query_proj, swish_proj))
    order = ("hi", "y", "core")
    out_full = lax.all_gather(transposed(out_proj), order, axis=0, tiled=True)
    across = ("y", "core", "hi")
    gate_full = lax.all_gather(exchange_columns((gate_proj,)), across, axis=0, tiled=True)
    up_full = lax.all_gather(exchange_columns((up_proj,)), across, axis=0, tiled=True)
    down_full = lax.all_gather(transposed(down_proj), order, axis=0, tiled=True)
    cot_all = gather_rows(cotangent[0])

    wide_all = tokens_all.astype(F32)
    unit_all = wide_all * inverse(wide_all)
    normed = (unit_all * attn_full).astype(BF16)
    kv = dot(normed, kv_full)
    key = kv[:, :key_size].astype(BF16)
    value = kv[:, key_size:].astype(BF16)
    low_rank = dot(normed, rankin_full)
    logits = dot_nt(low_rank, rankout_own, EXACT) + bias_own
    log_decay = jax.nn.log_sigmoid(logits) / 16.0
    decay_slope = jax.nn.sigmoid(-logits) / 16.0
    state_call, forward_call, gate_back_call, backward_call = recurrence_calls(
        rows, local, key_size, value_size
    )
    where = t.reshape(1).astype(jnp.int32)
    end_state, end_log = state_call(where, key, value, log_decay)
    in_state = chain(end_state, end_log, True)
    qs = dot(normed, qs_full)
    query = qs[:, :key_size].astype(BF16)
    swish_in = qs[:, key_size:]
    gain_row = head_full.reshape(1, value_size)
    gated, mixed, saved = forward_call(
        where, query, key, value, log_decay, swish_in, gain_row, in_state
    )
    hidden = residual + scatter_rows(dot(gated, out_full).astype(BF16))

    hidden_norm = (hidden * inverse(hidden) * mlp_full).astype(BF16)
    hidden_all = gather_rows(hidden_norm)
    gate_val = dot(hidden_all, gate_full)
    up_val = dot(hidden_all, up_full)
    sig = jax.nn.sigmoid(gate_val)
    silu = gate_val * sig
    product = (silu * up_val).astype(BF16)
    block_out = (hidden + scatter_rows(dot(product, down_full).astype(BF16))).astype(BF16)

    back_product = dot_nt(cot_all, down_full)
    back_gate = (back_product * up_val * (sig * (1.0 + gate_val * (1.0 - sig)))).astype(BF16)
    back_up = (back_product * silu).astype(BF16)
    back_hnorm = scatter_rows(
        (dot_nt(back_gate, gate_full) + dot_nt(back_up, up_full)).astype(BF16)
    )
    grad_down = dot_tn(product, cot_all).astype(BF16)
    grad_gate = dot_tn(hidden_all, back_gate).astype(BF16)
    grad_up = dot_tn(hidden_all, back_up).astype(BF16)
    back_hidden, grad_mlpgain = norm_back(hidden, mlp_full, back_hnorm)
    back_hidden = back_hidden + cotangent[0].astype(F32)

    back_attn = gather_rows(back_hidden.astype(BF16))
    back_gated = dot_nt(back_attn, out_full)
    grad_out = dot_tn(gated, back_attn).astype(BF16)
    back_mixed, back_swish, grad_headgain, direct = gate_back_call(
        where, back_gated, mixed, swish_in, gain_row, query, log_decay
    )
    out_state = chain(direct, end_log, False)
    back_query, back_key, back_value, back_logits = backward_call(
        where, query, key, value, log_decay, decay_slope, back_mixed, saved, out_state
    )
    back_qs = jnp.concatenate([back_query, back_swish], axis=1)
    back_kv = jnp.concatenate([back_key, back_value], axis=1)
    back_rank = dot(back_logits, rankout_own, EXACT)
    back_normed = (
        dot_nt(back_kv, kv_full)
        + dot_nt(back_qs, qs_full)
        + dot_nt(back_rank.astype(BF16), rankin_full)
    )
    grad_kv = dot_tn(normed, back_kv).astype(BF16)
    grad_qs = dot_tn(normed, back_qs).astype(BF16)
    grad_bias = jnp.sum(back_logits, axis=0)
    grad_rankout = dot_tn(back_logits, low_rank, EXACT)
    grad_rankin = dot_tn(normed, back_rank.astype(BF16))
    grad_attngain = jnp.sum(back_normed * unit_all, axis=0)
    back_tokens, _ = norm_back(residual, attn_full, scatter_rows(back_normed.astype(BF16)))
    grad_tokens = (back_hidden + back_tokens).astype(BF16)

    def columns_home(grad, widths):
        part = lax.psum_scatter(grad, across, scatter_dimension=0, tiled=True)
        own = part.shape[0] // HEADS
        sent = natural([part[n * own : (n + 1) * own] for n in range(HEADS)])
        back = natural([sent[0]] + [to_partner(sent[r], r) for r in range(1, HEADS)])
        outs, place = [], 0
        for w in widths:
            outs.append(
                jnp.concatenate([b[:, place : place + w] for b in back], axis=1).astype(F32)
            )
            place += w
        return outs

    def rows_home(grad):
        part = lax.psum_scatter(grad, order, scatter_dimension=0, tiled=True)
        return transposed(part).astype(F32)

    down_home = rows_home(grad_down)
    (gate_home,) = columns_home(grad_gate, [grad_gate.shape[1]])
    (up_home,) = columns_home(grad_up, [grad_up.shape[1]])
    out_home = rows_home(grad_out)
    query_home, swish_home = columns_home(grad_qs, [key_size, value_size])
    key_home, value_home = columns_home(grad_kv, [key_size, value_size])

    def own_head(grad):
        full = jnp.zeros((keys_all,) + grad.shape[1:], F32)
        return lax.dynamic_update_slice_in_dim(full, grad, t * key_size, 0)

    grads = (
        grad_attngain, grad_mlpgain, grad_headgain.reshape(-1), own_head(grad_bias),
        grad_rankin, own_head(grad_rankout),
    )
    packed = jnp.concatenate(
        [g.reshape(devices, -1) for g in grads] + [jnp.zeros((devices, pad), F32)], axis=1
    )
    mine = lax.psum_scatter(packed, WAYS, scatter_dimension=0, tiled=True)[0]
    homes, place = [], 0
    for size in sizes:
        homes.append(mine[place : place + size])
        place += size
    return (
        block_out[None],
        grad_tokens[None],
        query_home,
        key_home,
        value_home,
        swish_home,
        homes[4].reshape(rank_in.shape),
        homes[5].reshape(rank_out.shape),
        homes[3],
        homes[0],
        homes[2],
        out_home,
        homes[1],
        gate_home,
        up_home,
        down_home,
    )


def solution(mesh):
    dp, seq = mesh.shape["dp"], mesh.shape["seq"]
    fine = Mesh(mesh.devices.reshape(dp // 2, 2, seq // HEADS, HEADS), WAYS)
    rows, flat = P(WAYS, None), P(WAYS)
    acts = P(("y", "core"), ("hi", "t"), None)
    return jax.shard_map(
        per_device,
        mesh=fine,
        in_specs=(
            acts, rows, rows, rows, rows, rows, rows, flat, flat, flat, rows, flat, rows, rows,
            rows, acts,
        ),
        out_specs=(
            acts, acts, rows, rows, rows, rows, rows, rows, flat, flat, flat, rows, flat, rows,
            rows, rows,
        ),
        check_vma=False,
    )
```

time: 3680 us -> 1140 us (0.31)
  waiting for transfers between devices: 3020 us -> 718 us
  matrix products: 247 us -> 111 us
  blocking collectives: 197 us -> 93.7 us
  starting transfers between devices: 1.82 us -> 98.6 us
  local copies, waits for them, and re-layouts: 91.8 us -> 35.4 us
  other arithmetic: 86.7 us -> 37.8 us
    reduce_scatter x18 -> x6, waiting for transfers between devices: 2030 us -> 390 us  [the longest x4 263 us: columns_home(): part = lax.psum_scatter(grad, across, scatter_dimension=0, tiled=True)]
    all_gather x10 -> x4, waiting for transfers between devices: 700 us -> 0.01 us  [the longest x1 0.01 us: per_device(): out_full = lax.all_gather(transposed(out_proj), order, axis=0, tiled=True)]
    ppermute x0 -> x60, waiting for transfers between devices: none -> 248 us  [the longest x48 138 us: to_partner(): return lax.ppermute(value, 't', [(s, s ^ r) for s in range(HEADS)])]
    unnamed x40 -> x12, waiting for transfers between devices: 287 us -> 80.5 us
    dot_general x57 -> x24, matrix products: 247 us -> 111 us  [the longest x8 46.4 us: dot_nt(): lax.dot_general(a, b, (((1,), (1,)), ((), ())), precision=precision, pref...]
    ppermute x0 -> x60, starting transfers between devices: none -> 97.7 us  [the longest x48 52.3 us: to_partner(): return lax.ppermute(value, 't', [(s, s ^ r) for s in range(HEADS)])]
    all_gather x3 -> x1, blocking collectives: 150 us -> 93.7 us  [per_device(): packed = lax.all_gather(packed, WAYS, axis=0)]
    unnamed x2 -> x0, blocking collectives: 47.4 us -> none
  transfers between devices with their start and end apart: 34 -> 71, of which waited for: 31 -> 42; matrix products, arithmetic and copies ran while one was open for 7% -> 10% of each run, Pallas kernels for 0% -> 1%
where the time goes in v1:
time: 1140 us; the launch traced here: 1130 us
  waiting for transfers between devices  718 us (63%)
  matrix products  111 us (10%)
  starting transfers between devices  98.6 us (9%)
  blocking collectives  93.7 us (8%)
  other arithmetic  37.8 us (3%)
  local copies, waits for them, and re-layouts  35.4 us (3%)
  Pallas kernels  23 us (2%)
  between operations  15.9 us (1%)
    reduce_scatter x4, waiting for transfers between devices, columns_home(): part = lax.psum_scatter(grad, across, scatter_dimension=0, tiled=True)  263 us
    ppermute x48, waiting for transfers between devices, to_partner(): return lax.ppermute(value, 't', [(s, s ^ r) for s in range(HEADS)])  138 us
    reduce_scatter x2, waiting for transfers between devices, rows_home(): part = lax.psum_scatter(grad, order, scatter_dimension=0, tiled=True)  127 us
    all_gather x1, blocking collectives, per_device(): packed = lax.all_gather(packed, WAYS, axis=0)  93.7 us
    unnamed x12, waiting for transfers between devices  80.5 us
    ppermute x4, waiting for transfers between devices, transposed(): return lax.ppermute(value, WAYS, pairs)  64.8 us
    ppermute x48, starting transfers between devices, to_partner(): return lax.ppermute(value, 't', [(s, s ^ r) for s in range(HEADS)])  52.3 us
    dot_general x8, matrix products, dot_nt(): lax.dot_general(a, b, (((1,), (1,)), ((), ())), precision=precision, pref...  46.4 us
  transfers between devices with their start and end apart: 71, of which 42 were waited for; matrix products, arithmetic and copies ran while one was open for 10% of the time, Pallas kernels for 1%

profile of v1, /device:TPU:5, one launch (start us, length us, event | category | flops | bytes accessed | tf_op | source)
XLA Modules:
  0.0 1132.7 jit_solution(14931899494793280163)
XLA Ops:
  7.2 4.8 collective-permute-start.16
  12.0 7.6 collective-permute-done.16
  24.4 3.8 collective-permute-done.23
  29.2 3.8 collective-permute-done.25
  37.0 5.3 collective-permute-done.26
  52.8 5.3 collective-permute-done.10
  58.1 4.1 collective-permute-start.29
  62.3 2.8 collective-permute-start.12
  66.1 31.9 %collective-permute-done.29 = bf16[176,2048]{1,0:T(8,128)(2,1)S(1)} collective-permute-done((bf16[176,2048]{1,0:T(8,128)(2,1)}, bf16[176,2048]{1,0:T(8,128)(2,1)S(1)}, u32[]{:S(2)}, u32[]{:S(2)}) %collective-permute-start.29) | collective-permute-done | bytes 720928 | tf_op jit(solution)/shard_map/ppermute | solution.py:99
  99.0 93.7 %all-gather = bf16[65536]{0:T(1024)(128)(2,1)S(1)} all-gather(bf16[2048]{0:T(1024)(128)(2,1)S(1)} %concatenate.97), channel_id=2, replica_groups=mesh['y'=2,'core'=2,'hi'=2,'t'=4] {'y','core','hi','t'}, dimensions={0}, use_global_device_ids=true | all-gather | bytes 135168 | tf_op jit(solution)/shard_map/all_gather | solution.py:404
  196.0 5.8 collective-permute-start.13
  206.2 10.8 collective-permute-done.13
  218.6 6.8 collective-permute-start.14
  225.4 12.3 %collective-permute-done.7 = bf16[512,768]{1,0:T(8,128)(2,1)S(1)} collective-permute-done((bf16[512,768]{1,0:T(8,128)(2,1)S(1)}, bf16[512,768]{1,0:T(8,128)(2,1)S(1)}, u32[]{:S(2)}, u32[]{:S(2)}) %collective-permute-start.7) | collective-permute-done | bytes 786464 | tf_op jit(solution)/shard_map/ppermute | solution.py:24
  238.2 7.4 collective-permute-start.8
  251.0 4.7 shard_map.279
  255.6 8.4 collective-permute-start.15
  266.4 7.7 collective-permute-done.15.in_ref
  274.1 6.5 shard_map.280
  283.7 3.0 convolution_convert_fusion.6
  289.3 13.5 %collective-permute-start.19 = (bf16[128,2048]{1,0:T(8,128)(2,1)}, bf16[128,2048]{1,0:T(8,128)(2,1)}, u32[]{:S(2)}, u32[]{:S(2)}) collective-permute-start(bf16[128,2048]{1,0:T(8,128)(2,1)} %get-tuple-element.125), channel_id=1, source_target_pairs={{0,3},{1,2},{2,1},{3,0},{4,7},{5,6},{6,5},{7,4},{8,11},{9,10},{10,... | collective-permute-start | bytes 1572872 | tf_op jit(solution)/shard_map/ppermute | solution.py:20
  303.2 12.0 %collective-permute-done.19 = bf16[128,2048]{1,0:T(8,128)(2,1)} collective-permute-done((bf16[128,2048]{1,0:T(8,128)(2,1)}, bf16[128,2048]{1,0:T(8,128)(2,1)}, u32[]{:S(2)}, u32[]{:S(2)}) %collective-permute-start.19) | collective-permute-done | bytes 524320 | tf_op jit(solution)/shard_map/ppermute | solution.py:20
  315.1 10.3 collective-permute-done.18
  330.1 2.4 collective-permute-start.22
  335.2 8.9 collective-permute-done.22
  344.3 10.3 collective-permute-done.21
  357.1 8.3 fusion.35
  365.4 8.3 fusion.34
  373.7 3.5 collective-permute-done.34
  378.7 9.3 multiply_convert_fusion
  388.1 7.1 fusion.46
  395.2 16.5 %add_convert_fusion = bf16[512,2048]{1,0:T(8,128)(2,1)S(1)} fusion(f32[512,2048]{1,0:T(8,128)S(1)} %fusion.46, bf16[512,1408]{1,0:T(8,128)(2,1)S(1)} %get-tuple-element.102, bf16[2048,1408]{1,0:T(8,128)(2,1)S(1)} %copy-done.61), kind=kOutput, calls=%fused_computation.11 | convolution fusion | flops 2954887168 | bytes 13500416 | tf_op jit(solution)/shard_map/dot_general | solution.py:107
  411.8 2.4 collective-permute-start.38
  414.6 3.6 convolution_convert_fusion.7
  420.8 5.1 collective-permute-done.38
  426.0 10.3 collective-permute-done.37
  439.2 9.2 collective-permute-done.32
  448.4 10.5 collective-permute-done.31
  460.4 3.2 fusion.36
  466.3 11.2 collective-permute-done.41
  477.5 10.5 collective-permute-done.40
  490.9 4.4 shard_map.281
  499.5 13.8 %collective-permute-done.42.out_ref = bf16[512,256]{1,0:T(8,128)(2,1)S(1)} collective-permute-done((bf16[512,256]{1,0:T(8,128)(2,1)S(1)}, bf16[512,256]{1,0:T(8,128)(2,1)S(1)}, u32[]{:S(2)}, u32[]{:S(2)}) %collective-permute-start.42) | collective-permute-done | bytes 262176 | tf_op jit(solution)/shard_map/ppermute | solution.py:353
  516.0 7.4 shard_map.282
  531.4 7.9 fusion.3
  542.7 4.3 convolution_convert_fusion.5
  547.0 4.7 convolution_convert_fusion.3
  552.8 3.5 convolution_convert_fusion.4
  558.2 6.9 convolution_convert_fusion.2
  566.5 7.1 convolution_convert_fusion.1
  575.0 7.2 convolution_convert_fusion
  582.2 2.7 fusion.37
  587.5 80.3 %all-reduce.3.cloned.1.call-done = f32[32,2048]{1,0:T(8,128)} async-done(((f32[32,2048]{1,0:T(8,128)}), f32[32,2048]{1,0:T(8,128)}) %all-reduce.3.cloned.1.call-update) | async-done | bytes 262160
  676.5 44.8 %reduce-scatter.11.cloned.1.call-done = bf16[64,2048]{1,0:T(8,128)(2,1)} async-done(((bf16[512,2048]{1,0:T(8,128)(2,1)}), bf16[64,2048]{1,0:T(8,128)(2,1)}) %reduce-scatter.11.cloned.1.call-update) | async-done | bytes 262160 | tf_op jit(solution)/shard_map/reduce_scatter | solution.py:515
  723.2 2.4 fusion.17
  725.6 7.9 collective-permute-done.52
  734.3 49.4 %reduce-scatter.9.cloned.1.call-done = bf16[256,768]{1,0:T(8,128)(2,1)} async-done(((bf16[2048,768]{1,0:T(8,128)(2,1)}), bf16[256,768]{1,0:T(8,128)(2,1)}) %reduce-scatter.9.cloned.1.call-update) | async-done | bytes 393232 | tf_op jit(solution)/shard_map/reduce_scatter | solution.py:502
  784.9 2.4 collective-permute-start.50
  787.5 58.3 %reduce-scatter.7.cloned.1.call-done = bf16[256,768]{1,0:T(8,128)(2,1)} async-done(((bf16[2048,768]{1,0:T(8,128)(2,1)}), bf16[256,768]{1,0:T(8,128)(2,1)}) %reduce-scatter.7.cloned.1.call-update) | async-done | bytes 393232 | tf_op jit(solution)/shard_map/reduce_scatter | solution.py:502
  846.9 2.4 collective-permute-start.47
  857.3 74.2 %reduce-scatter.13.cloned.1.call-done = bf16[256,1408]{1,0:T(8,128)(2,1)} async-done(((bf16[2048,1408]{1,0:T(8,128)(2,1)}), bf16[256,1408]{1,0:T(8,128)(2,1)}) %reduce-scatter.13.cloned.1.call-update) | async-done | bytes 720912 | tf_op jit(solution)/shard_map/reduce_scatter | solution.py:502
  935.6 81.2 %reduce-scatter.15.cloned.1.call-done = bf16[256,1408]{1,0:T(8,128)(2,1)} async-done(((bf16[2048,1408]{1,0:T(8,128)(2,1)}), bf16[256,1408]{1,0:T(8,128)(2,1)}) %reduce-scatter.15.cloned.1.call-update) | async-done | bytes 720912 | tf_op jit(solution)/shard_map/reduce_scatter | solution.py:502
  1020.8 81.7 %reduce-scatter.17.cloned.1.call-done = bf16[176,2048]{1,0:T(8,128)(2,1)} async-done(((bf16[1408,2048]{1,0:T(8,128)(2,1)}), bf16[176,2048]{1,0:T(8,128)(2,1)}) %reduce-scatter.17.cloned.1.call-update) | async-done | bytes 720912 | tf_op jit(solution)/shard_map/reduce_scatter | solution.py:515
  1107.1 17.5 %collective-permute-done.59 = bf16[176,2048]{1,0:T(8,128)(2,1)S(1)} collective-permute-done((bf16[176,2048]{1,0:T(8,128)(2,1)}, bf16[176,2048]{1,0:T(8,128)(2,1)S(1)}, u32[]{:S(2)}, u32[]{:S(2)}) %collective-permute-start.59) | collective-permute-done | bytes 720928 | tf_op jit(solution)/shard_map/ppermute | solution.py:99
  (401 shorter events, 131.8 us)
Async XLA Ops:
  7.2 276.5 %all-gather.6.cloned.1.call-start = ((), (), s32[]{:S(2)}) async-start(), calls=%async_computation.6 | async-start | bytes 2359296 | tf_op jit(solution)/shard_map/all_gather | solution.py:421
  7.2 12.4 %collective-permute-start.16 = (bf16[64,2048]{1,0:T(8,128)(2,1)}, bf16[64,2048]{1,0:T(8,128)(2,1)S(1)}, u32[]{:S(2)}, u32[]{:S(2)}) collective-permute-start(bf16[64,2048]{1,0:T(8,128)(2,1)} %param.26), channel_id=1, source_target_pairs={{0,0},{1,8},{2,16},{3,24},{4,4},{5,12},{6,20},{7,28},{8,1},{9,9},{... | collective-permute-start | bytes 786440 | tf_op jit(solution)/shard_map/ppermute | solution.py:99
  20.3 336.7 %all-gather.8.cloned.1.call-start = ((), (), s32[]{:S(2)}) async-start(), calls=%async_computation.7 | async-start | bytes 6488064 | tf_op jit(solution)/shard_map/all_gather | solution.py:423
  22.8 10.3 collective-permute-start.25
  34.1 331.3 %all-gather.10.cloned.1.call-start = ((), (), s32[]{:S(2)}) async-start(), calls=%async_computation.8 | async-start | bytes 6488064 | tf_op jit(solution)/shard_map/all_gather | solution.py:424
  34.4 8.7 collective-permute-start.27
  34.9 10.3 collective-permute-start.28
  46.2 332.5 %all-gather.12.cloned.1.call-start = ((), (), s32[]{:S(2)}) async-start(), calls=%async_computation.9 | async-start | bytes 6488064 | tf_op jit(solution)/shard_map/all_gather | solution.py:425
  47.0 11.1 collective-permute-start.10
  49.2 13.0 %collective-permute-start.11 = (bf16[64,768]{1,0:T(8,128)(2,1)S(1)}, bf16[64,768]{1,0:T(8,128)(2,1)S(1)}, u32[]{:S(2)}, u32[]{:S(2)}) collective-permute-start(bf16[64,768]{1,0:T(8,128)(2,1)S(1)} %get-tuple-element.202), channel_id=1, source_target_pairs={{0,1},{1,0},{2,3},{3,2},{4,5},{5,4},{6,7},{7,6},{8,9},{9,8},{10,11... | collective-permute-start | bytes 294920 | tf_op jit(solution)/shard_map/ppermute | solution.py:20
  49.5 15.6 %collective-permute-start.3 = (bf16[64,768]{1,0:T(8,128)(2,1)S(1)}, bf16[64,768]{1,0:T(8,128)(2,1)S(1)}, u32[]{:S(2)}, u32[]{:S(2)}) collective-permute-start(bf16[64,768]{1,0:T(8,128)(2,1)S(1)} %broadcast_select_fusion.143), channel_id=1, source_target_pairs={{0,3},{1,2},{2,1},{3,0},{4,7},{5,6},{6,5},{7,4},{8,11},{9,10},{10,... | collective-permute-start | bytes 294920 | tf_op jit(solution)/shard_map/ppermute | solution.py:20
  50.7 14.4 %collective-permute-start.4 = (bf16[64,768]{1,0:T(8,128)(2,1)S(1)}, bf16[64,768]{1,0:T(8,128)(2,1)S(1)}, u32[]{:S(2)}, u32[]{:S(2)}) collective-permute-start(bf16[64,768]{1,0:T(8,128)(2,1)S(1)} %get-tuple-element.99), channel_id=1, source_target_pairs={{0,2},{1,3},{2,0},{3,1},{4,6},{5,7},{6,4},{7,5},{8,10},{9,11},{10,... | collective-permute-start | bytes 294920 | tf_op jit(solution)/shard_map/ppermute | solution.py:20
  52.2 12.9 %collective-permute-start.5 = (bf16[64,768]{1,0:T(8,128)(2,1)S(1)}, bf16[64,768]{1,0:T(8,128)(2,1)S(1)}, u32[]{:S(2)}, u32[]{:S(2)}) collective-permute-start(bf16[64,768]{1,0:T(8,128)(2,1)S(1)} %get-tuple-element.203), channel_id=1, source_target_pairs={{0,1},{1,0},{2,3},{3,2},{4,5},{5,4},{6,7},{7,6},{8,9},{9,8},{10,11... | collective-permute-start | bytes 294920 | tf_op jit(solution)/shard_map/ppermute | solution.py:20
  58.1 40.0 %collective-permute-start.29 = (bf16[176,2048]{1,0:T(8,128)(2,1)}, bf16[176,2048]{1,0:T(8,128)(2,1)S(1)}, u32[]{:S(2)}, u32[]{:S(2)}) collective-permute-start(bf16[176,2048]{1,0:T(8,128)(2,1)} %param.30), channel_id=1, source_target_pairs={{0,0},{1,8},{2,16},{3,24},{4,4},{5,12},{6,20},{7,28},{8,1},{9,9},{... | collective-permute-start | bytes 2162696 | tf_op jit(solution)/shard_map/ppermute | solution.py:99
  62.3 131.4 %collective-permute-start.12 = (bf16[256,768]{1,0:T(8,128)(2,1)S(1)}, bf16[256,768]{1,0:T(8,128)(2,1)}, u32[]{:S(2)}, u32[]{:S(2)}) collective-permute-start(bf16[256,768]{1,0:T(8,128)(2,1)S(1)} %pad_maximum_fusion.17), channel_id=1, source_target_pairs={{0,4},{4,0},{1,5},{5,1},{2,6},{6,2},{3,7},{7,3},{8,12},{12,8},{9,1... | collective-permute-start | bytes 1179656 | tf_op jit(solution)/shard_map/ppermute | solution.py:24
  65.2 128.5 %collective-permute-start.6 = (bf16[256,768]{1,0:T(8,128)(2,1)S(1)}, bf16[256,768]{1,0:T(8,128)(2,1)}, u32[]{:S(2)}, u32[]{:S(2)}) collective-permute-start(bf16[256,768]{1,0:T(8,128)(2,1)S(1)} %pad_maximum_fusion.16), channel_id=1, source_target_pairs={{0,4},{4,0},{1,5},{5,1},{2,6},{6,2},{3,7},{7,3},{8,12},{12,8},{9,1... | collective-permute-start | bytes 1179656 | tf_op jit(solution)/shard_map/ppermute | solution.py:24
  65.3 139.0 %collective-permute-start.2 = (bf16[128,2048]{1,0:T(8,128)(2,1)S(1)}, bf16[128,2048]{1,0:T(8,128)(2,1)S(1)}, u32[]{:S(2)}, u32[]{:S(2)}) collective-permute-start(bf16[128,2048]{1,0:T(8,128)(2,1)S(1)} %bitcast.56), channel_id=1, source_target_pairs={{0,3},{1,2},{2,1},{3,0},{4,7},{5,6},{6,5},{7,4},{8,11},{9,10},{10,... | collective-permute-start | bytes 1572872 | tf_op jit(solution)/shard_map/ppermute | solution.py:20
  65.4 139.0 %collective-permute-start.1 = (bf16[128,2048]{1,0:T(8,128)(2,1)S(1)}, bf16[128,2048]{1,0:T(8,128)(2,1)}, u32[]{:S(2)}, u32[]{:S(2)}) collective-permute-start(bf16[128,2048]{1,0:T(8,128)(2,1)S(1)} %bitcast.57), channel_id=1, source_target_pairs={{0,2},{1,3},{2,0},{3,1},{4,6},{5,7},{6,4},{7,5},{8,10},{9,11},{10,... | collective-permute-start | bytes 1572872 | tf_op jit(solution)/shard_map/ppermute | solution.py:20
  98.0 106.3 %collective-permute-start = (bf16[128,2048]{1,0:T(8,128)(2,1)S(1)}, bf16[128,2048]{1,0:T(8,128)(2,1)}, u32[]{:S(2)}, u32[]{:S(2)}) collective-permute-start(bf16[128,2048]{1,0:T(8,128)(2,1)S(1)} %bitcast.58), channel_id=1, source_target_pairs={{0,1},{1,0},{2,3},{3,2},{4,5},{5,4},{6,7},{7,6},{8,9},{9,8},{10,11... | collective-permute-start | bytes 1572872 | tf_op jit(solution)/shard_map/ppermute | solution.py:20
  98.9 568.9 %all-reduce.3.cloned.1.call-start = ((), (), s32[]{:S(2)}) async-start(), calls=%async_computation.16 | async-start | bytes 524288
  196.0 21.1 %collective-permute-start.13 = (bf16[512,768]{1,0:T(8,128)(2,1)}, bf16[512,768]{1,0:T(8,128)(2,1)}, u32[]{:S(2)}, u32[]{:S(2)}) collective-permute-start(bf16[512,768]{1,0:T(8,128)(2,1)} %pad_maximum_fusion.9), channel_id=1, source_target_pairs={{0,16},{16,0},{1,17},{17,1},{2,18},{18,2},{3,19},{19,3},{4,20},{20... | collective-permute-start | bytes 2359304 | tf_op jit(solution)/shard_map/ppermute | solution.py:24
  204.2 33.5 %collective-permute-start.7 = (bf16[512,768]{1,0:T(8,128)(2,1)S(1)}, bf16[512,768]{1,0:T(8,128)(2,1)S(1)}, u32[]{:S(2)}, u32[]{:S(2)}) collective-permute-start(bf16[512,768]{1,0:T(8,128)(2,1)S(1)} %pad_maximum_fusion.8), channel_id=1, source_target_pairs={{0,16},{16,0},{1,17},{17,1},{2,18},{18,2},{3,19},{19,3},{4,20},{20... | collective-permute-start | bytes 2359304 | tf_op jit(solution)/shard_map/ppermute | solution.py:24
  218.6 30.2 %collective-permute-start.14 = (bf16[1024,768]{1,0:T(8,128)(2,1)S(1)}, bf16[1024,768]{1,0:T(8,128)(2,1)S(1)}, u32[]{:S(2)}, u32[]{:S(2)}) collective-permute-start(bf16[1024,768]{1,0:T(8,128)(2,1)S(1)} %pad_maximum_fusion.7), channel_id=1, source_target_pairs={{0,8},{8,0},{1,9},{9,1},{2,10},{10,2},{3,11},{11,3},{4,12},{12,4},... | collective-permute-start | bytes 4718600 | tf_op jit(solution)/shard_map/ppermute | solution.py:24
  238.2 25.9 %collective-permute-start.8 = (bf16[1024,768]{1,0:T(8,128)(2,1)S(1)}, bf16[1024,768]{1,0:T(8,128)(2,1)S(1)}, u32[]{:S(2)}, u32[]{:S(2)}) collective-permute-start(bf16[1024,768]{1,0:T(8,128)(2,1)S(1)} %pad_maximum_fusion.6), channel_id=1, source_target_pairs={{0,8},{8,0},{1,9},{9,1},{2,10},{10,2},{3,11},{11,3},{4,12},{12,4},... | collective-permute-start | bytes 4718600 | tf_op jit(solution)/shard_map/ppermute | solution.py:24
  255.6 18.4 %collective-permute-start.15 = (bf16[512,256]{1,0:T(8,128)(2,1)S(1)}, bf16[512,256]{1,0:T(8,128)(2,1)S(1)}, u32[]{:S(2)}, u32[]{:S(2)}) collective-permute-start(bf16[512,256]{1,0:T(8,128)(2,1)S(1)} %get-tuple-element.28), channel_id=1, source_target_pairs={{0,4},{1,5},{2,6},{3,7},{8,12},{9,13},{10,14},{11,15},{16,20},{17,... | collective-permute-start | bytes 786440 | tf_op jit(solution)/shard_map/ppermute | solution.py:353
  289.3 25.8 %collective-permute-start.19 = (bf16[128,2048]{1,0:T(8,128)(2,1)}, bf16[128,2048]{1,0:T(8,128)(2,1)}, u32[]{:S(2)}, u32[]{:S(2)}) collective-permute-start(bf16[128,2048]{1,0:T(8,128)(2,1)} %get-tuple-element.125), channel_id=1, source_target_pairs={{0,3},{1,2},{2,1},{3,0},{4,7},{5,6},{6,5},{7,4},{8,11},{9,10},{10,... | collective-permute-start | bytes 1572872 | tf_op jit(solution)/shard_map/ppermute | solution.py:20
  302.8 22.7 %collective-permute-start.18 = (bf16[128,2048]{1,0:T(8,128)(2,1)}, bf16[128,2048]{1,0:T(8,128)(2,1)}, u32[]{:S(2)}, u32[]{:S(2)}) collective-permute-start(bf16[128,2048]{1,0:T(8,128)(2,1)} %get-tuple-element.126), channel_id=1, source_target_pairs={{0,2},{1,3},{2,0},{3,1},{4,6},{5,7},{6,4},{7,5},{8,10},{9,11},{10,... | collective-permute-start | bytes 1572872 | tf_op jit(solution)/shard_map/ppermute | solution.py:20
  302.8 23.9 %collective-permute-start.17 = (bf16[128,2048]{1,0:T(8,128)(2,1)}, bf16[128,2048]{1,0:T(8,128)(2,1)}, u32[]{:S(2)}, u32[]{:S(2)}) collective-permute-start(bf16[128,2048]{1,0:T(8,128)(2,1)} %get-tuple-element.124), channel_id=1, source_target_pairs={{0,1},{1,0},{2,3},{3,2},{4,5},{5,4},{6,7},{7,6},{8,9},{9,8},{10,11... | collective-permute-start | bytes 1572872 | tf_op jit(solution)/shard_map/ppermute | solution.py:20
  330.1 14.0 %collective-permute-start.22 = (bf16[128,2048]{1,0:T(8,128)(2,1)S(1)}, bf16[128,2048]{1,0:T(8,128)(2,1)S(1)}, u32[]{:S(2)}, u32[]{:S(2)}) collective-permute-start(bf16[128,2048]{1,0:T(8,128)(2,1)S(1)} %multiply_convert_fusion.3), channel_id=1, source_target_pairs={{0,3},{1,2},{2,1},{3,0},{4,7},{5,6},{6,5},{7,4},{8,11},{9,10},{10,... | collective-permute-start | bytes 1572872 | tf_op jit(solution)/shard_map/ppermute | solution.py:20
  332.5 22.1 %collective-permute-start.21 = (bf16[128,2048]{1,0:T(8,128)(2,1)S(1)}, bf16[128,2048]{1,0:T(8,128)(2,1)S(1)}, u32[]{:S(2)}, u32[]{:S(2)}) collective-permute-start(bf16[128,2048]{1,0:T(8,128)(2,1)S(1)} %multiply_convert_fusion.3), channel_id=1, source_target_pairs={{0,2},{1,3},{2,0},{3,1},{4,6},{5,7},{6,4},{7,5},{8,10},{9,11},{10,... | collective-permute-start | bytes 1572872 | tf_op jit(solution)/shard_map/ppermute | solution.py:20
  332.5 24.5 %collective-permute-start.20 = (bf16[128,2048]{1,0:T(8,128)(2,1)S(1)}, bf16[128,2048]{1,0:T(8,128)(2,1)}, u32[]{:S(2)}, u32[]{:S(2)}) collective-permute-start(bf16[128,2048]{1,0:T(8,128)(2,1)S(1)} %multiply_convert_fusion.3), channel_id=1, source_target_pairs={{0,1},{1,0},{2,3},{3,2},{4,5},{5,4},{6,7},{7,6},{8,9},{9,8},{10,11... | collective-permute-start | bytes 1572872 | tf_op jit(solution)/shard_map/ppermute | solution.py:20
  332.9 40.8 %collective-permute-start.35 = (bf16[128,2048]{1,0:T(8,128)(2,1)}, bf16[128,2048]{1,0:T(8,128)(2,1)}, u32[]{:S(2)}, u32[]{:S(2)}) collective-permute-start(bf16[128,2048]{1,0:T(8,128)(2,1)} %bitcast.3), channel_id=1, source_target_pairs={{0,3},{1,2},{2,1},{3,0},{4,7},{5,6},{6,5},{7,4},{8,11},{9,10},{10,... | collective-permute-start | bytes 1572872 | tf_op jit(solution)/shard_map/ppermute | solution.py:20
  335.2 42.0 %collective-permute-start.34 = (bf16[128,2048]{1,0:T(8,128)(2,1)}, bf16[128,2048]{1,0:T(8,128)(2,1)}, u32[]{:S(2)}, u32[]{:S(2)}) collective-permute-start(bf16[128,2048]{1,0:T(8,128)(2,1)} %bitcast.3), channel_id=1, source_target_pairs={{0,2},{1,3},{2,0},{3,1},{4,6},{5,7},{6,4},{7,5},{8,10},{9,11},{10,... | collective-permute-start | bytes 1572872 | tf_op jit(solution)/shard_map/ppermute | solution.py:20
  344.1 34.6 %collective-permute-start.33 = (bf16[128,2048]{1,0:T(8,128)(2,1)}, bf16[128,2048]{1,0:T(8,128)(2,1)}, u32[]{:S(2)}, u32[]{:S(2)}) collective-permute-start(bf16[128,2048]{1,0:T(8,128)(2,1)} %bitcast.3), channel_id=1, source_target_pairs={{0,1},{1,0},{2,3},{3,2},{4,5},{5,4},{6,7},{7,6},{8,9},{9,8},{10,11... | collective-permute-start | bytes 1572872 | tf_op jit(solution)/shard_map/ppermute | solution.py:20
  411.8 14.0 %collective-permute-start.38 = (bf16[128,2048]{1,0:T(8,128)(2,1)S(1)}, bf16[128,2048]{1,0:T(8,128)(2,1)S(1)}, u32[]{:S(2)}, u32[]{:S(2)}) collective-permute-start(bf16[128,2048]{1,0:T(8,128)(2,1)S(1)} %get-tuple-element.119), channel_id=1, source_target_pairs={{0,3},{1,2},{2,1},{3,0},{4,7},{5,6},{6,5},{7,4},{8,11},{9,10},{10,... | collective-permute-start | bytes 1572872 | tf_op jit(solution)/shard_map/ppermute | solution.py:20
  414.3 22.1 %collective-permute-start.37 = (bf16[128,2048]{1,0:T(8,128)(2,1)S(1)}, bf16[128,2048]{1,0:T(8,128)(2,1)S(1)}, u32[]{:S(2)}, u32[]{:S(2)}) collective-permute-start(bf16[128,2048]{1,0:T(8,128)(2,1)S(1)} %get-tuple-element.120), channel_id=1, source_target_pairs={{0,2},{1,3},{2,0},{3,1},{4,6},{5,7},{6,4},{7,5},{8,10},{9,11},{10,... | collective-permute-start | bytes 1572872 | tf_op jit(solution)/shard_map/ppermute | solution.py:20
  414.3 24.4 %collective-permute-start.36 = (bf16[128,2048]{1,0:T(8,128)(2,1)S(1)}, bf16[128,2048]{1,0:T(8,128)(2,1)S(1)}, u32[]{:S(2)}, u32[]{:S(2)}) collective-permute-start(bf16[128,2048]{1,0:T(8,128)(2,1)S(1)} %get-tuple-element.118), channel_id=1, source_target_pairs={{0,1},{1,0},{2,3},{3,2},{4,5},{5,4},{6,7},{7,6},{8,9},{9,8},{10,11... | collective-permute-start | bytes 1572872 | tf_op jit(solution)/shard_map/ppermute | solution.py:20
  418.4 30.0 %collective-permute-start.32 = (bf16[128,2048]{1,0:T(8,128)(2,1)S(1)}, bf16[128,2048]{1,0:T(8,128)(2,1)S(1)}, u32[]{:S(2)}, u32[]{:S(2)}) collective-permute-start(bf16[128,2048]{1,0:T(8,128)(2,1)S(1)} %get-tuple-element.122), channel_id=1, source_target_pairs={{0,3},{1,2},{2,1},{3,0},{4,7},{5,6},{6,5},{7,4},{8,11},{9,10},{10,... | collective-permute-start | bytes 1572872 | tf_op jit(solution)/shard_map/ppermute | solution.py:20
  420.8 38.1 %collective-permute-start.31 = (bf16[128,2048]{1,0:T(8,128)(2,1)S(1)}, bf16[128,2048]{1,0:T(8,128)(2,1)S(1)}, u32[]{:S(2)}, u32[]{:S(2)}) collective-permute-start(bf16[128,2048]{1,0:T(8,128)(2,1)S(1)} %get-tuple-element.123), channel_id=1, source_target_pairs={{0,2},{1,3},{2,0},{3,1},{4,6},{5,7},{6,4},{7,5},{8,10},{9,11},{10,... | collective-permute-start | bytes 1572872 | tf_op jit(solution)/shard_map/ppermute | solution.py:20
  425.9 34.5 %collective-permute-start.30 = (bf16[128,2048]{1,0:T(8,128)(2,1)S(1)}, bf16[128,2048]{1,0:T(8,128)(2,1)S(1)}, u32[]{:S(2)}, u32[]{:S(2)}) collective-permute-start(bf16[128,2048]{1,0:T(8,128)(2,1)S(1)} %get-tuple-element.121), channel_id=1, source_target_pairs={{0,1},{1,0},{2,3},{3,2},{4,5},{5,4},{6,7},{7,6},{8,9},{9,8},{10,11... | collective-permute-start | bytes 1572872 | tf_op jit(solution)/shard_map/ppermute | solution.py:20
  463.6 13.9 %collective-permute-start.41 = (bf16[128,2048]{1,0:T(8,128)(2,1)S(1)}, bf16[128,2048]{1,0:T(8,128)(2,1)S(1)}, u32[]{:S(2)}, u32[]{:S(2)}) collective-permute-start(bf16[128,2048]{1,0:T(8,128)(2,1)S(1)} %get-tuple-element.86), channel_id=1, source_target_pairs={{0,3},{1,2},{2,1},{3,0},{4,7},{5,6},{6,5},{7,4},{8,11},{9,10},{10,... | collective-permute-start | bytes 1572872 | tf_op jit(solution)/shard_map/ppermute | solution.py:20
  466.0 22.1 %collective-permute-start.40 = (bf16[128,2048]{1,0:T(8,128)(2,1)S(1)}, bf16[128,2048]{1,0:T(8,128)(2,1)S(1)}, u32[]{:S(2)}, u32[]{:S(2)}) collective-permute-start(bf16[128,2048]{1,0:T(8,128)(2,1)S(1)} %get-tuple-element.86), channel_id=1, source_target_pairs={{0,2},{1,3},{2,0},{3,1},{4,6},{5,7},{6,4},{7,5},{8,10},{9,11},{10,... | collective-permute-start | bytes 1572872 | tf_op jit(solution)/shard_map/ppermute | solution.py:20
  466.0 23.6 %collective-permute-start.39 = (bf16[128,2048]{1,0:T(8,128)(2,1)S(1)}, bf16[128,2048]{1,0:T(8,128)(2,1)S(1)}, u32[]{:S(2)}, u32[]{:S(2)}) collective-permute-start(bf16[128,2048]{1,0:T(8,128)(2,1)S(1)} %get-tuple-element.86), channel_id=1, source_target_pairs={{0,1},{1,0},{2,3},{3,2},{4,5},{5,4},{6,7},{7,6},{8,9},{9,8},{10,11... | collective-permute-start | bytes 1572872 | tf_op jit(solution)/shard_map/ppermute | solution.py:20
  496.9 16.4 %collective-permute-start.42 = (bf16[512,256]{1,0:T(8,128)(2,1)S(1)}, bf16[512,256]{1,0:T(8,128)(2,1)S(1)}, u32[]{:S(2)}, u32[]{:S(2)}) collective-permute-start(bf16[512,256]{1,0:T(8,128)(2,1)S(1)} %get-tuple-element.33), channel_id=1, source_target_pairs={{4,0},{5,1},{6,2},{7,3},{12,8},{13,9},{14,10},{15,11},{20,16},{21,... | collective-permute-start | bytes 786440 | tf_op jit(solution)/shard_map/ppermute | solution.py:353
  542.6 178.7 %reduce-scatter.11.cloned.1.call-start = ((), (), s32[]{:S(2)}) async-start(), calls=%async_computation.12 | async-start | bytes 2359296 | tf_op jit(solution)/shard_map/reduce_scatter | solution.py:515
  547.0 236.8 %reduce-scatter.9.cloned.1.call-start = ((), (), s32[]{:S(2)}) async-start(), calls=%async_computation.11 | async-start | bytes 3538944 | tf_op jit(solution)/shard_map/reduce_scatter | solution.py:502
  551.7 294.0 %reduce-scatter.7.cloned.1.call-start = ((), (), s32[]{:S(2)}) async-start(), calls=%async_computation.10 | async-start | bytes 3538944 | tf_op jit(solution)/shard_map/reduce_scatter | solution.py:502
  556.4 375.1 %reduce-scatter.13.cloned.1.call-start = ((), (), s32[]{:S(2)}) async-start(), calls=%async_computation.13 | async-start | bytes 6488064 | tf_op jit(solution)/shard_map/reduce_scatter | solution.py:502
  565.2 451.6 %reduce-scatter.15.cloned.1.call-start = ((), (), s32[]{:S(2)}) async-start(), calls=%async_computation.14 | async-start | bytes 6488064 | tf_op jit(solution)/shard_map/reduce_scatter | solution.py:502
  573.6 528.8 %reduce-scatter.17.cloned.1.call-start = ((), (), s32[]{:S(2)}) async-start(), calls=%async_computation.15 | async-start | bytes 6488064 | tf_op jit(solution)/shard_map/reduce_scatter | solution.py:515
  584.9 90.1 %collective-permute-start.45 = (bf16[128,2048]{1,0:T(8,128)(2,1)}, bf16[128,2048]{1,0:T(8,128)(2,1)S(1)}, u32[]{:S(2)}, u32[]{:S(2)}) collective-permute-start(bf16[128,2048]{1,0:T(8,128)(2,1)} %get-tuple-element.116), channel_id=1, source_target_pairs={{0,3},{1,2},{2,1},{3,0},{4,7},{5,6},{6,5},{7,4},{8,11},{9,10},{10,... | collective-permute-start | bytes 1572872 | tf_op jit(solution)/shard_map/ppermute | solution.py:20
  584.9 90.1 %collective-permute-start.44 = (bf16[128,2048]{1,0:T(8,128)(2,1)}, bf16[128,2048]{1,0:T(8,128)(2,1)S(1)}, u32[]{:S(2)}, u32[]{:S(2)}) collective-permute-start(bf16[128,2048]{1,0:T(8,128)(2,1)} %get-tuple-element.117), channel_id=1, source_target_pairs={{0,2},{1,3},{2,0},{3,1},{4,6},{5,7},{6,4},{7,5},{8,10},{9,11},{10,... | collective-permute-start | bytes 1572872 | tf_op jit(solution)/shard_map/ppermute | solution.py:20
  586.3 88.7 %collective-permute-start.43 = (bf16[128,2048]{1,0:T(8,128)(2,1)}, bf16[128,2048]{1,0:T(8,128)(2,1)S(1)}, u32[]{:S(2)}, u32[]{:S(2)}) collective-permute-start(bf16[128,2048]{1,0:T(8,128)(2,1)} %get-tuple-element.115), channel_id=1, source_target_pairs={{0,1},{1,0},{2,3},{3,2},{4,5},{5,4},{6,7},{7,6},{8,9},{9,8},{10,11... | collective-permute-start | bytes 1572872 | tf_op jit(solution)/shard_map/ppermute | solution.py:20
  721.3 12.2 %collective-permute-start.52 = (bf16[64,2048]{1,0:T(8,128)(2,1)}, bf16[64,2048]{1,0:T(8,128)(2,1)S(1)}, u32[]{:S(2)}, u32[]{:S(2)}) collective-permute-start(bf16[64,2048]{1,0:T(8,128)(2,1)} %reduce-scatter.11.cloned.1.call-done), channel_id=1, source_target_pairs={{0,0},{1,8},{2,16},{3,24},{4,4},{5,12},{6,20},{7,28},{8,1},{9,9},{... | collective-permute-start | bytes 786440 | tf_op jit(solution)/shard_map/ppermute | solution.py:99
  784.8 64.5 %collective-permute-start.49 = (bf16[64,768]{1,0:T(8,128)(2,1)S(1)}, bf16[64,768]{1,0:T(8,128)(2,1)S(1)}, u32[]{:S(2)}, u32[]{:S(2)}) collective-permute-start(bf16[64,768]{1,0:T(8,128)(2,1)S(1)} %get-tuple-element.193), channel_id=1, source_target_pairs={{0,3},{1,2},{2,1},{3,0},{4,7},{5,6},{6,5},{7,4},{8,11},{9,10},{10,... | collective-permute-start | bytes 294920 | tf_op jit(solution)/shard_map/ppermute | solution.py:20
  784.9 64.7 %collective-permute-start.50 = (bf16[64,768]{1,0:T(8,128)(2,1)S(1)}, bf16[64,768]{1,0:T(8,128)(2,1)S(1)}, u32[]{:S(2)}, u32[]{:S(2)}) collective-permute-start(bf16[64,768]{1,0:T(8,128)(2,1)S(1)} %get-tuple-element.194), channel_id=1, source_target_pairs={{0,2},{1,3},{2,0},{3,1},{4,6},{5,7},{6,4},{7,5},{8,10},{9,11},{10,... | collective-permute-start | bytes 294920 | tf_op jit(solution)/shard_map/ppermute | solution.py:20
  787.2 62.3 %collective-permute-start.51 = (bf16[64,768]{1,0:T(8,128)(2,1)S(1)}, bf16[64,768]{1,0:T(8,128)(2,1)S(1)}, u32[]{:S(2)}, u32[]{:S(2)}) collective-permute-start(bf16[64,768]{1,0:T(8,128)(2,1)S(1)} %get-tuple-element.192), channel_id=1, source_target_pairs={{0,1},{1,0},{2,3},{3,2},{4,5},{5,4},{6,7},{7,6},{8,9},{9,8},{10,11... | collective-permute-start | bytes 294920 | tf_op jit(solution)/shard_map/ppermute | solution.py:20
  932.8 87.6 %collective-permute-start.53 = (bf16[64,1408]{1,0:T(8,128)(2,1)S(1)}, bf16[64,1408]{1,0:T(8,128)(2,1)S(1)}, u32[]{:S(2)}, u32[]{:S(2)}) collective-permute-start(bf16[64,1408]{1,0:T(8,128)(2,1)S(1)} %get-tuple-element.162), channel_id=1, source_target_pairs={{0,3},{1,2},{2,1},{3,0},{4,7},{5,6},{6,5},{7,4},{8,11},{9,10},{10,... | collective-permute-start | bytes 540680 | tf_op jit(solution)/shard_map/ppermute | solution.py:20
  932.9 169.6 %collective-permute-start.54 = (bf16[64,1408]{1,0:T(8,128)(2,1)S(1)}, bf16[64,1408]{1,0:T(8,128)(2,1)S(1)}, u32[]{:S(2)}, u32[]{:S(2)}) collective-permute-start(bf16[64,1408]{1,0:T(8,128)(2,1)S(1)} %get-tuple-element.163), channel_id=1, source_target_pairs={{0,2},{1,3},{2,0},{3,1},{4,6},{5,7},{6,4},{7,5},{8,10},{9,11},{10,... | collective-permute-start | bytes 540680 | tf_op jit(solution)/shard_map/ppermute | solution.py:20
  935.3 169.1 %collective-permute-start.55 = (bf16[64,1408]{1,0:T(8,128)(2,1)S(1)}, bf16[64,1408]{1,0:T(8,128)(2,1)S(1)}, u32[]{:S(2)}, u32[]{:S(2)}) collective-permute-start(bf16[64,1408]{1,0:T(8,128)(2,1)S(1)} %get-tuple-element.161), channel_id=1, source_target_pairs={{0,1},{1,0},{2,3},{3,2},{4,5},{5,4},{6,7},{7,6},{8,9},{9,8},{10,11... | collective-permute-start | bytes 540680 | tf_op jit(solution)/shard_map/ppermute | solution.py:20
  1018.0 87.7 %collective-permute-start.56 = (bf16[64,1408]{1,0:T(8,128)(2,1)S(1)}, bf16[64,1408]{1,0:T(8,128)(2,1)S(1)}, u32[]{:S(2)}, u32[]{:S(2)}) collective-permute-start(bf16[64,1408]{1,0:T(8,128)(2,1)S(1)} %get-tuple-element.157), channel_id=1, source_target_pairs={{0,3},{1,2},{2,1},{3,0},{4,7},{5,6},{6,5},{7,4},{8,11},{9,10},{10,... | collective-permute-start | bytes 540680 | tf_op jit(solution)/shard_map/ppermute | solution.py:20
  1018.1 87.6 %collective-permute-start.57 = (bf16[64,1408]{1,0:T(8,128)(2,1)S(1)}, bf16[64,1408]{1,0:T(8,128)(2,1)S(1)}, u32[]{:S(2)}, u32[]{:S(2)}) collective-permute-start(bf16[64,1408]{1,0:T(8,128)(2,1)S(1)} %get-tuple-element.158), channel_id=1, source_target_pairs={{0,2},{1,3},{2,0},{3,1},{4,6},{5,7},{6,4},{7,5},{8,10},{9,11},{10,... | collective-permute-start | bytes 540680 | tf_op jit(solution)/shard_map/ppermute | solution.py:20
  1020.5 85.3 %collective-permute-start.58 = (bf16[64,1408]{1,0:T(8,128)(2,1)S(1)}, bf16[64,1408]{1,0:T(8,128)(2,1)S(1)}, u32[]{:S(2)}, u32[]{:S(2)}) collective-permute-start(bf16[64,1408]{1,0:T(8,128)(2,1)S(1)} %get-tuple-element.156), channel_id=1, source_target_pairs={{0,1},{1,0},{2,3},{3,2},{4,5},{5,4},{6,7},{7,6},{8,9},{9,8},{10,11... | collective-permute-start | bytes 540680 | tf_op jit(solution)/shard_map/ppermute | solution.py:20
  1102.5 22.0 %collective-permute-start.59 = (bf16[176,2048]{1,0:T(8,128)(2,1)}, bf16[176,2048]{1,0:T(8,128)(2,1)S(1)}, u32[]{:S(2)}, u32[]{:S(2)}) collective-permute-start(bf16[176,2048]{1,0:T(8,128)(2,1)} %reduce-scatter.17.cloned.1.call-done), channel_id=1, source_target_pairs={{0,0},{1,8},{2,16},{3,24},{4,4},{5,12},{6,20},{7,28},{8,1},{9,9},{... | collective-permute-start | bytes 2162696 | tf_op jit(solution)/shard_map/ppermute | solution.py:99
  (85 other events, 956.7 us)
Sparse Core Ops, SparseCore 0:
  20.5 37.9 all-gather.5
  60.9 90.5 all-gather.7
  153.9 66.7 all-gather.9
  222.4 66.4 all-gather.11
  542.7 125.0 all-reduce.2
  671.0 50.2 reduce-scatter.10
  725.1 58.6 reduce-scatter.8
  787.1 58.6 reduce-scatter.6
  849.6 81.8 reduce-scatter.12
  934.8 81.8 reduce-scatter.14
  1020.6 81.8 reduce-scatter.16

commit v2 on v1

--- a/solution.py
+++ b/solution.py
@@ -24,8 +24,8 @@
     return lax.ppermute(value, axis, [(0, 1), (1, 0)])
 
 
-def natural(pieces):
-    t = lax.axis_index("t")
+def natural(pieces, t=None):
+    t = lax.axis_index("t") if t is None else t
     odd, high = (t & 1) == 1, (t & 2) == 2
     a, b, c, d = pieces
     a, b = jnp.where(odd, b, a), jnp.where(odd, a, b)
@@ -51,7 +51,11 @@
     return total
 
 
-def stage(value, axis):
+def after(value, *others):
+    return lax.optimization_barrier((value,) + others)[0]
+
+
+def both(value, axis):
     if lax.axis_size(axis) != 2:
         return lax.all_gather(value, axis, axis=0, tiled=True)
     other = swap(value, axis)
@@ -59,7 +63,7 @@
     return jnp.concatenate([jnp.where(first, value, other), jnp.where(first, other, value)])
 
 
-def stage_core(value):
+def both_cores(value):
     other = swap(value, "core")
     first = lax.axis_index("core") == 0
     half = value.shape[0] // 2
@@ -70,33 +74,59 @@
     return jnp.concatenate(out)
 
 
-def slices_for(parts):
-    four = []
-    for n in range(HEADS):
-        cols = [p[:, n * (p.shape[1] // HEADS) : (n + 1) * (p.shape[1] // HEADS)] for p in parts]
-        four.append(jnp.concatenate(cols, axis=1) if len(cols) > 1 else cols[0])
-    return natural(four)
-
-
-def exchange_columns(parts):
-    sent = slices_for(parts)
+def columns_in(weight):
+    n = weight.shape[1] // HEADS
+    sent = natural([weight[:, i * n : (i + 1) * n] for i in range(HEADS)])
     got = [sent[0]] + [to_partner(sent[r], r) for r in range(1, HEADS)]
     return jnp.concatenate(natural(got))
 
 
-def gather_columns(parts):
-    return stage_core(stage(stage(exchange_columns(parts), "hi"), "y"))
-
-
-def transposed(value):
+def columns_out(part):
+    own = part.shape[0] // HEADS
+    sent = natural([part[n * own : (n + 1) * own] for n in range(HEADS)])
+    back = natural([sent[0]] + [to_partner(sent[r], r) for r in range(1, HEADS)])
+    return jnp.concatenate(back, axis=1).astype(F32)
+
+
+def row_pairs():
     n_hi = lax.axis_size("hi")
-    pairs = [
-        ((i * n_hi + h) * HEADS + t, (t * n_hi + h) * HEADS + i)
+    group = HEADS * n_hi
+    return [
+        (group * t + i * n_hi + h, (i * n_hi + h) * HEADS + t)
         for i in range(HEADS)
         for h in range(n_hi)
         for t in range(HEADS)
     ]
-    return lax.ppermute(value, WAYS, pairs)
+
+
+def rows_in(weight):
+    return lax.ppermute(weight, WAYS, row_pairs())
+
+
+def rows_out(part):
+    return lax.ppermute(part, WAYS, [(b, a) for a, b in row_pairs()]).astype(F32)
+
+
+def cell():
+    return lax.axis_index("y") * 2 + lax.axis_index("core")
+
+
+def add(a, b):
+    return (a.astype(F32) + b.astype(F32)).astype(BF16)
+
+
+def half_hi(total):
+    if lax.axis_size("hi") != 2:
+        return lax.psum_scatter(total, "hi", scatter_dimension=0, tiled=True)
+    first = lax.axis_index("hi") == 0
+    n = total.shape[0] // 2
+    low, high = total[:n], total[n:]
+    return add(jnp.where(first, low, high), swap(jnp.where(first, high, low), "hi"))
+
+
+def rows_in_cells(value):
+    n = value.shape[0] // HEADS
+    return natural([value[i * n : (i + 1) * n] for i in range(HEADS)], cell())
 
 
 def dot(a, b, precision=None):
@@ -401,7 +431,9 @@
     sizes = [s.shape[0] for s in small]
     pad = -sum(sizes) % 1024
     packed = jnp.concatenate(small + (jnp.zeros((pad,), BF16),))
-    packed = lax.all_gather(packed, WAYS, axis=0)
+    packed = packed.reshape(1, 8, -1)
+    packed = jnp.concatenate(natural([packed] + [to_partner(packed, r) for r in range(1, HEADS)]))
+    packed = both_cores(both(both(packed, "hi"), "y")).reshape(devices, -1)
     got, place = [], 0
     for size in sizes:
         got.append(packed[:, place : place + size].reshape(-1))
@@ -414,23 +446,32 @@
     bias_own = lax.dynamic_slice_in_dim(bias_full, t * key_size, key_size, 0)
 
     residual = tokens[0].astype(F32)
+    key_in, value_in = columns_in(key_proj), columns_in(value_proj)
     tokens_all = gather_rows(tokens[0])
-    kv_full = gather_columns((key_proj, value_proj))
-    qs_full = gather_columns((query_proj, swish_proj))
-    order = ("hi", "y", "core")
-    out_full = lax.all_gather(transposed(out_proj), order, axis=0, tiled=True)
-    across = ("y", "core", "hi")
-    gate_full = lax.all_gather(exchange_columns((gate_proj,)), across, axis=0, tiled=True)
-    up_full = lax.all_gather(exchange_columns((up_proj,)), across, axis=0, tiled=True)
-    down_full = lax.all_gather(transposed(down_proj), order, axis=0, tiled=True)
-    cot_all = gather_rows(cotangent[0])
+    query_in = columns_in(after(query_proj, key_in))
+    swish_in_ = columns_in(after(swish_proj, value_in))
+    out_in = rows_in(after(out_proj, query_in))
+    gate_in = columns_in(after(gate_proj, tokens_all, swish_in_))
+    up_in = columns_in(after(up_proj, gate_in))
+    down_in = rows_in(after(down_proj, up_in))
+    cot_all = gather_rows(after(cotangent[0], down_in))
+    key_hi, value_hi = both(key_in, "hi"), both(value_in, "hi")
+    query_hi = both(after(query_in, key_hi), "hi")
+    swish_hi = both(after(swish_in_, value_hi), "hi")
+    out_hi = both(after(out_in, query_hi), "hi")
+    gate_hi = both(after(gate_in, swish_hi), "hi")
+    key_full = both_cores(both(key_hi, "y"))
+    value_full = both_cores(both(value_hi, "y"))
+    query_full = both_cores(both(query_hi, "y"))
+    swish_full = both_cores(both(swish_hi, "y"))
+    out_full = both_cores(both(out_hi, "y"))
+    gate_full = both_cores(both(gate_hi, "y"))
 
     wide_all = tokens_all.astype(F32)
     unit_all = wide_all * inverse(wide_all)
     normed = (unit_all * attn_full).astype(BF16)
-    kv = dot(normed, kv_full)
-    key = kv[:, :key_size].astype(BF16)
-    value = kv[:, key_size:].astype(BF16)
+    key = dot(normed, key_full).astype(BF16)
+    value = dot(normed, value_full).astype(BF16)
     low_rank = dot(normed, rankin_full)
     logits = dot_nt(low_rank, rankout_own, EXACT) + bias_own
     log_decay = jax.nn.log_sigmoid(logits) / 16.0
@@ -441,9 +482,12 @@
     where = t.reshape(1).astype(jnp.int32)
     end_state, end_log = state_call(where, key, value, log_decay)
     in_state = chain(end_state, end_log, True)
-    qs = dot(normed, qs_full)
-    query = qs[:, :key_size].astype(BF16)
-    swish_in = qs[:, key_size:]
+    up_hi = both(after(up_in, in_state), "hi")
+    down_hi = both(after(down_in, gate_hi), "hi")
+    up_full = both_cores(both(up_hi, "y"))
+    down_full = both_cores(both(down_hi, "y"))
+    query = dot(normed, query_full).astype(BF16)
+    swish_in = dot(normed, swish_full)
     gain_row = head_full.reshape(1, value_size)
     gated, mixed, saved = forward_call(
         where, query, key, value, log_decay, swish_in, gain_row, in_state
@@ -457,70 +501,82 @@
     sig = jax.nn.sigmoid(gate_val)
     silu = gate_val * sig
     product = (silu * up_val).astype(BF16)
-    block_out = (hidden + scatter_rows(dot(product, down_full).astype(BF16))).astype(BF16)
 
     back_product = dot_nt(cot_all, down_full)
     back_gate = (back_product * up_val * (sig * (1.0 + gate_val * (1.0 - sig)))).astype(BF16)
     back_up = (back_product * silu).astype(BF16)
-    back_hnorm = scatter_rows(
-        (dot_nt(back_gate, gate_full) + dot_nt(back_up, up_full)).astype(BF16)
-    )
-    grad_down = dot_tn(product, cot_all).astype(BF16)
-    grad_gate = dot_tn(hidden_all, back_gate).astype(BF16)
-    grad_up = dot_tn(hidden_all, back_up).astype(BF16)
-    back_hidden, grad_mlpgain = norm_back(hidden, mlp_full, back_hnorm)
+    back_hnorm = (dot_nt(back_gate, gate_full) + dot_nt(back_up, up_full)).astype(BF16)
+
+    def by_columns(left, right):
+        sent = [swap(dot_tn(left[r], right).astype(BF16), "core") for r in (1, 3)]
+        return [
+            (dot_tn(left[r], right) + got.astype(F32)).astype(BF16)
+            for r, got in zip((0, 2), sent)
+        ]
+
+    def by_rows(left, right):
+        cells = rows_in_cells(dot_tn(left, right).astype(BF16))
+        return [add(cells[r], swap(cells[r + 1], "core")) for r in (0, 2)]
+
+    def over_y(pair):
+        return add(pair[0], swap(pair[1], "y"))
+
+    def cells_of(value):
+        n = value.shape[1] // HEADS
+        return natural([value[:, i * n : (i + 1) * n] for i in range(HEADS)], cell())
+
+    hidden_cells, normed_cells = cells_of(hidden_all), cells_of(normed)
+    back_hnorm_sum = scatter_rows(back_hnorm)
+    up_pair = by_columns(hidden_cells, back_up)
+    gate_pair = by_columns(hidden_cells, back_gate)
+    down_pair = by_rows(product, cot_all)
+    back_hnorm_sum = after(back_hnorm_sum, *up_pair, *gate_pair, *down_pair)
+    back_hidden, grad_mlpgain = norm_back(hidden, mlp_full, back_hnorm_sum)
     back_hidden = back_hidden + cotangent[0].astype(F32)
 
     back_attn = gather_rows(back_hidden.astype(BF16))
+    up_y = over_y(up_pair)
+    back_attn = after(back_attn, up_y)
     back_gated = dot_nt(back_attn, out_full)
-    grad_out = dot_tn(gated, back_attn).astype(BF16)
+    out_pair = by_rows(gated, back_attn)
     back_mixed, back_swish, grad_headgain, direct = gate_back_call(
         where, back_gated, mixed, swish_in, gain_row, query, log_decay
     )
     out_state = chain(direct, end_log, False)
+    block_out = scatter_rows(dot(product, after(down_full, direct)).astype(BF16))
+    block_out = (hidden + block_out).astype(BF16)
+    swish_pair = by_columns(normed_cells, back_swish)
     back_query, back_key, back_value, back_logits = backward_call(
         where, query, key, value, log_decay, decay_slope, back_mixed, saved, out_state
     )
-    back_qs = jnp.concatenate([back_query, back_swish], axis=1)
-    back_kv = jnp.concatenate([back_key, back_value], axis=1)
+    gate_y, down_y = over_y(gate_pair), over_y(down_pair)
     back_rank = dot(back_logits, rankout_own, EXACT)
     back_normed = (
-        dot_nt(back_kv, kv_full)
-        + dot_nt(back_qs, qs_full)
+        dot_nt(back_key, key_full)
+        + dot_nt(back_value, value_full)
+        + dot_nt(back_query, query_full)
+        + dot_nt(back_swish, swish_full)
         + dot_nt(back_rank.astype(BF16), rankin_full)
     )
-    grad_kv = dot_tn(normed, back_kv).astype(BF16)
-    grad_qs = dot_tn(normed, back_qs).astype(BF16)
+    back_tokens = scatter_rows(back_normed.astype(BF16))
+    value_pair = by_columns(normed_cells, back_value)
+    key_pair = by_columns(normed_cells, back_key)
+    query_pair = by_columns(normed_cells, back_query)
     grad_bias = jnp.sum(back_logits, axis=0)
     grad_rankout = dot_tn(back_logits, low_rank, EXACT)
     grad_rankin = dot_tn(normed, back_rank.astype(BF16))
     grad_attngain = jnp.sum(back_normed * unit_all, axis=0)
-    back_tokens, _ = norm_back(residual, attn_full, scatter_rows(back_normed.astype(BF16)))
+    back_tokens, _ = norm_back(residual, attn_full, back_tokens)
     grad_tokens = (back_hidden + back_tokens).astype(BF16)
 
-    def columns_home(grad, widths):
-        part = lax.psum_scatter(grad, across, scatter_dimension=0, tiled=True)
-        own = part.shape[0] // HEADS
-        sent = natural([part[n * own : (n + 1) * own] for n in range(HEADS)])
-        back = natural([sent[0]] + [to_partner(sent[r], r) for r in range(1, HEADS)])
-        outs, place = [], 0
-        for w in widths:
-            outs.append(
-                jnp.concatenate([b[:, place : place + w] for b in back], axis=1).astype(F32)
-            )
-            place += w
-        return outs
-
-    def rows_home(grad):
-        part = lax.psum_scatter(grad, order, scatter_dimension=0, tiled=True)
-        return transposed(part).astype(F32)
-
-    down_home = rows_home(grad_down)
-    (gate_home,) = columns_home(grad_gate, [grad_gate.shape[1]])
-    (up_home,) = columns_home(grad_up, [grad_up.shape[1]])
-    out_home = rows_home(grad_out)
-    query_home, swish_home = columns_home(grad_qs, [key_size, value_size])
-    key_home, value_home = columns_home(grad_kv, [key_size, value_size])
+    up_home = columns_out(half_hi(up_y))
+    gate_home = columns_out(half_hi(gate_y))
+    down_home = rows_out(half_hi(down_y))
+    out_home = rows_out(half_hi(over_y(out_pair)))
+    swish_home = columns_out(half_hi(over_y(swish_pair)))
+    value_home = columns_out(half_hi(over_y(value_pair)))
+    key_home = columns_out(half_hi(over_y(key_pair)))
+    query_home = columns_out(half_hi(over_y(query_pair)))
 
     def own_head(grad):
         full = jnp.zeros((keys_all,) + grad.shape[1:], F32)
@@ -533,7 +589,21 @@
     packed = jnp.concatenate(
         [g.reshape(devices, -1) for g in grads] + [jnp.zeros((devices, pad), F32)], axis=1
     )
-    mine = lax.psum_scatter(packed, WAYS, scatter_dimension=0, tiled=True)[0]
+    eighth = packed.shape[1] // 8
+    cells = rows_in_cells(packed.reshape(devices, 8, eighth))
+    pair = [cells[r] + swap(cells[r + 1], "core") for r in (0, 2)]
+    half = pair[0] + swap(pair[1], "y")
+    if lax.axis_size("hi") == 2:
+        first = lax.axis_index("hi") == 0
+        low, high = half[:HEADS], half[HEADS:]
+        mine = jnp.where(first, low, high) + swap(jnp.where(first, high, low), "hi")
+    else:
+        mine = lax.psum_scatter(half, "hi", scatter_dimension=0, tiled=True)
+    parts = natural([mine[n] for n in range(HEADS)])
+    mine = parts[0]
+    for r in range(1, HEADS):
+        mine = mine + to_partner(parts[r], r)
+    mine = mine.reshape(-1)
     homes, place = [], 0
     for size in sizes:
         homes.append(mine[place : place + size])

time: 1140 us -> 925 us (0.81)
  waiting for transfers between devices: 718 us -> 393 us
  starting transfers between devices: 98.6 us -> 272 us
  blocking collectives: 93.7 us -> 0 us
  other arithmetic: 37.8 us -> 92.4 us
  matrix products: 111 us -> 97.3 us
  between operations: 15.9 us -> 3.88 us
    reduce_scatter x6 -> x0, waiting for transfers between devices: 390 us -> none  [the longest x4 263 us: columns_home(): part = lax.psum_scatter(grad, across, scatter_dimension=0, tiled=True)]
    ppermute x6 -> x63, waiting for transfers between devices: 23.2 us -> 262 us  [swap(): return lax.ppermute(value, axis, [(0, 1), (1, 0)])]
    all_gather x1 -> x0, blocking collectives: 93.7 us -> none  [per_device(): packed = lax.all_gather(packed, WAYS, axis=0)]
    ppermute x6 -> x63, starting transfers between devices: 22.9 us -> 108 us  [swap(): return lax.ppermute(value, axis, [(0, 1), (1, 0)])]
    ppermute x48 -> x66, starting transfers between devices: 52.3 us -> 135 us  [to_partner(): return lax.ppermute(value, 't', [(s, s ^ r) for s in range(HEADS)])]
    unnamed x12 -> x0, waiting for transfers between devices: 80.5 us -> none
    ppermute x4, waiting for transfers between devices: 64.8 us -> 21 us  [the longest x2 20.9 us: rows_in(): return lax.ppermute(weight, WAYS, row_pairs())]
    ppermute x48 -> x66, waiting for transfers between devices: 138 us -> 105 us  [to_partner(): return lax.ppermute(value, 't', [(s, s ^ r) for s in range(HEADS)])]
  transfers between devices with their start and end apart: 71 -> 135, of which waited for: 42 -> 48; matrix products, arithmetic and copies ran while one was open for 10% -> 16% of each run, Pallas kernels for 1% -> 3%
where the time goes in v2:
time: 925 us; the launch traced here: 909 us
  waiting for transfers between devices  393 us (42%)
  starting transfers between devices  272 us (29%)
  matrix products  97.3 us (11%)
  other arithmetic  92.4 us (10%)
  local copies, waits for them, and re-layouts  25.8 us (3%)
  Pallas kernels  23.5 us (3%)
    ppermute x63, waiting for transfers between devices, swap(): return lax.ppermute(value, axis, [(0, 1), (1, 0)])  262 us
    ppermute x66, starting transfers between devices, to_partner(): return lax.ppermute(value, 't', [(s, s ^ r) for s in range(HEADS)])  135 us
    ppermute x63, starting transfers between devices, swap(): return lax.ppermute(value, axis, [(0, 1), (1, 0)])  108 us
    ppermute x66, waiting for transfers between devices, to_partner(): return lax.ppermute(value, 't', [(s, s ^ r) for s in range(HEADS)])  105 us
    dot_general x10, matrix products, dot_nt(): lax.dot_general(a, b, (((1,), (1,)), ((), ())), precision=precision, pref...  35.6 us
    dot_general x28, matrix products, dot_tn(): lax.dot_general(a, b, (((0,), (0,)), ((), ())), precision=precision, pref...  34.8 us
    dot_general x10, matrix products, dot(): return jnp.dot(a, b, precision=precision, preferred_element_type=F32)  26.9 us
    concatenate x2, other arithmetic, both_cores(): return jnp.concatenate(out)  22 us
  transfers between devices with their start and end apart: 135, of which 48 were waited for; matrix products, arithmetic and copies ran while one was open for 16% of the time, Pallas kernels for 3%

profile of v2, /device:TPU:5, one launch (start us, length us, event | category | flops | bytes accessed | tf_op | source)
XLA Modules:
  0.0 908.6 jit_solution(9333443340686989002)
XLA Ops:
  11.2 14.5 %collective-permute-done.3 = bf16[1,8,256]{2,1,0:T(8,128)(2,1)S(1)} collective-permute-done((bf16[1,8,256]{2,1,0:T(8,128)(2,1)S(1)}, bf16[1,8,256]{2,1,0:T(8,128)(2,1)S(1)}, u32[]{:S(2)}, u32[]{:S(2)}) %collective-permute-start.3) | collective-permute-done | bytes 4128 | tf_op jit(solution)/shard_map/ppermute | solution.py:20
  45.7 6.2 collective-permute-start.8
  62.4 15.9 %collective-permute-done.16 = bf16[256,256]{1,0:T(8,128)(2,1)S(1)} collective-permute-done((bf16[256,256]{1,0:T(8,128)(2,1)S(1)}, bf16[256,256]{1,0:T(8,128)(2,1)S(1)}, u32[]{:S(2)}, u32[]{:S(2)}) %collective-permute-start.16) | collective-permute-done | bytes 131104 | tf_op jit(solution)/shard_map/ppermute | solution.py:24
  83.2 8.0 collective-permute-done.34
  91.1 8.6 collective-permute-start.17
  109.6 8.0 collective-permute-start.44
  120.2 5.6 collective-permute-done.35
  126.0 3.7 collective-permute-done.44
  130.2 3.5 collective-permute-done.45
  137.1 3.7 collective-permute-done.50
  148.8 3.9 collective-permute-start.56
  154.0 4.1 collective-permute-start.32
  158.1 5.2 collective-permute-done.36
  166.8 13.0 %collective-permute-done.56 = bf16[176,2048]{1,0:T(8,128)(2,1)S(1)} collective-permute-done((bf16[176,2048]{1,0:T(8,128)(2,1)S(1)}, bf16[176,2048]{1,0:T(8,128)(2,1)S(1)}, u32[]{:S(2)}, u32[]{:S(2)}) %collective-permute-start.56) | collective-permute-done | bytes 720928 | tf_op jit(solution)/shard_map/ppermute | solution.py:103
  179.8 30.2 %collective-permute-start.61 = (bf16[128,2048]{1,0:T(8,128)(2,1)S(1)}, bf16[128,2048]{1,0:T(8,128)(2,1)S(1)}, u32[]{:S(2)}, u32[]{:S(2)}) collective-permute-start(bf16[128,2048]{1,0:T(8,128)(2,1)S(1)} %bitcast.115), channel_id=1, source_target_pairs={{0,2},{1,3},{2,0},{3,1},{4,6},{5,7},{6,4},{7,5},{8,10},{9,11},{10,... | collective-permute-start | bytes 1572872 | tf_op jit(solution)/shard_map/ppermute | solution.py:20
  211.5 4.7 shard_map.279
  216.2 4.6 collective-permute-start.62
  220.8 8.6 collective-permute-start.33
  232.0 3.5 collective-permute-done.33.in_ref
  238.6 6.3 shard_map.280
  247.7 21.2 %collective-permute-start.40 = (bf16[128,2048]{1,0:T(8,128)(2,1)S(1)}, bf16[128,2048]{1,0:T(8,128)(2,1)S(1)}, u32[]{:S(2)}, u32[]{:S(2)}) collective-permute-start(bf16[128,2048]{1,0:T(8,128)(2,1)S(1)} %get-tuple-element.183), channel_id=1, source_target_pairs={{0,3},{1,2},{2,1},{3,0},{4,7},{5,6},{6,5},{7,4},{8,11},{9,10},{10,... | collective-permute-start | bytes 1572872 | tf_op jit(solution)/shard_map/ppermute | solution.py:20
  273.4 21.4 %collective-permute-done.40 = bf16[128,2048]{1,0:T(8,128)(2,1)S(1)} collective-permute-done((bf16[128,2048]{1,0:T(8,128)(2,1)S(1)}, bf16[128,2048]{1,0:T(8,128)(2,1)S(1)}, u32[]{:S(2)}, u32[]{:S(2)}) %collective-permute-start.40) | collective-permute-done | bytes 524320 | tf_op jit(solution)/shard_map/ppermute | solution.py:20
  294.8 10.9 %collective-permute-done.39 = bf16[128,2048]{1,0:T(8,128)(2,1)S(1)} collective-permute-done((bf16[128,2048]{1,0:T(8,128)(2,1)S(1)}, bf16[128,2048]{1,0:T(8,128)(2,1)S(1)}, u32[]{:S(2)}, u32[]{:S(2)}) %collective-permute-start.39) | collective-permute-done | bytes 524320 | tf_op jit(solution)/shard_map/ppermute | solution.py:20
  306.3 4.9 collective-permute-start.48
  313.2 29.5 %collective-permute-done.48 = bf16[512,1408]{1,0:T(8,128)(2,1)S(1)} collective-permute-done((bf16[512,1408]{1,0:T(8,128)(2,1)S(1)}, bf16[512,1408]{1,0:T(8,128)(2,1)S(1)}, u32[]{:S(2)}, u32[]{:S(2)}) %collective-permute-start.48) | collective-permute-done | bytes 1441824 | tf_op jit(solution)/shard_map/ppermute | solution.py:24
  346.4 27.2 %collective-permute-done.58 = bf16[352,2048]{1,0:T(8,128)(2,1)S(1)} collective-permute-done((bf16[352,2048]{1,0:T(8,128)(2,1)S(1)}, bf16[352,2048]{1,0:T(8,128)(2,1)S(1)}, u32[]{:S(2)}, u32[]{:S(2)}) %collective-permute-start.58) | collective-permute-done | bytes 1441824 | tf_op jit(solution)/shard_map/ppermute | solution.py:24
  375.7 10.3 %collective-permute-done.41 = bf16[128,2048]{1,0:T(8,128)(2,1)S(1)} collective-permute-done((bf16[128,2048]{1,0:T(8,128)(2,1)S(1)}, bf16[128,2048]{1,0:T(8,128)(2,1)S(1)}, u32[]{:S(2)}, u32[]{:S(2)}) %collective-permute-start.41) | collective-permute-done | bytes 524320 | tf_op jit(solution)/shard_map/ppermute | solution.py:20
  395.6 5.1 fusion.35
  403.0 22.0 %pad_maximum_fusion.2 = bf16[1408,2048]{1,0:T(8,128)(2,1)S(1)} fusion(bf16[352,2048]{1,0:T(8,128)(2,1)S(1)} %get-tuple-element.151, bf16[352,2048]{1,0:T(8,128)(2,1)S(1)} %get-tuple-element.152, bf16[352,2048]{1,0:T(8,128)(2,1)S(1)} %get-tuple-element.138, bf16[352,2048]{1,0:T(8,128)(2,1)S(1)} %get-tuple-element.137), kind=kLoop, calls=%fused_computation.3 | loop fusion | flops 23068672 | bytes 11534336 | tf_op jit(solution)/shard_map/concatenate | solution.py:74
  425.1 5.1 fusion.79
  430.2 9.9 %multiply_convert_fusion.1 = (bf16[512,1408]{1,0:T(8,128)(2,1)}, bf16[512,1408]{1,0:T(8,128)(2,1)}, bf16[512,1408]{1,0:T(8,128)(2,1)}) fusion(f32[512,1408]{1,0:T(8,128)} %fusion.79, f32[512,1408]{1,0:T(8,128)} %fusion.35, bf16[512,1408]{1,0:T(8,128)(2,1)S(1)} %copy-done.53, bf16[512,1408]{1,0:T(8,128)(2,1)} %get-tuple-element.156, ...), kind=kOutput, calls=%fused_computation.33 | convolution fusion | flops 2995060736 | bytes 17956864 | tf_op jit(solution)/shard_map/dot_general | solution.py:133
  440.1 10.7 %fusion.34 = f32[512,2048]{1,0:T(8,128)} fusion(bf16[512,1408]{1,0:T(8,128)(2,1)} %get-tuple-element.135, bf16[512,1408]{1,0:T(8,128)(2,1)S(1)} %copy-done.59, bf16[512,1408]{1,0:T(8,128)(2,1)S(1)} %copy-done.61, bf16[512,1408]{1,0:T(8,128)(2,1)S(1)} %copy-done.57, bf16[512,1408]{1,0:T(8,128)(2,1)S(1)} %copy-done.55), kind=kOutput, calls=%fused_computation.143 | convolution fusion | flops 2975858688 | bytes 11403264 | tf_op jit(solution)/shard_map/dot_general | solution.py:137
  450.9 3.6 convolution_convert_fusion
  456.8 7.8 add_convert_fusion
  472.6 6.8 collective-permute-done.65
  483.4 6.0 collective-permute-done.64
  503.3 21.3 %collective-permute-done.132 = bf16[352,2048]{1,0:T(8,128)(2,1)S(1)} collective-permute-done((bf16[352,2048]{1,0:T(8,128)(2,1)S(1)}, bf16[352,2048]{1,0:T(8,128)(2,1)S(1)}, u32[]{:S(2)}, u32[]{:S(2)}) %collective-permute-start.132) | collective-permute-done | bytes 1441824 | tf_op jit(solution)/shard_map/ppermute | solution.py:24
  532.4 54.1 %collective-permute-done.123 = bf16[512,1408]{1,0:T(8,128)(2,1)} collective-permute-done((bf16[512,1408]{1,0:T(8,128)(2,1)}, bf16[512,1408]{1,0:T(8,128)(2,1)}, u32[]{:S(2)}, u32[]{:S(2)}) %collective-permute-start.123) | collective-permute-done | bytes 1441824 | tf_op jit(solution)/shard_map/ppermute | solution.py:24
  589.6 4.5 collective-permute-start.124
  603.4 5.1 shard_map.281
  612.9 4.9 convolution_convert_fusion.7
  627.6 34.0 %collective-permute-done.124 = bf16[256,1408]{1,0:T(8,128)(2,1)} collective-permute-done((bf16[256,1408]{1,0:T(8,128)(2,1)}, bf16[256,1408]{1,0:T(8,128)(2,1)}, u32[]{:S(2)}, u32[]{:S(2)}) %collective-permute-start.124) | collective-permute-done | bytes 720928 | tf_op jit(solution)/shard_map/ppermute | solution.py:24
  661.6 3.3 collective-permute-start.119
  667.4 9.7 %collective-permute-done.128 = bf16[256,1408]{1,0:T(8,128)(2,1)} collective-permute-done((bf16[256,1408]{1,0:T(8,128)(2,1)}, bf16[256,1408]{1,0:T(8,128)(2,1)}, u32[]{:S(2)}, u32[]{:S(2)}) %collective-permute-start.128) | collective-permute-done | bytes 720928 | tf_op jit(solution)/shard_map/ppermute | solution.py:24
  678.4 14.1 %collective-permute-done.133 = bf16[176,2048]{1,0:T(8,128)(2,1)} collective-permute-done((bf16[176,2048]{1,0:T(8,128)(2,1)}, bf16[176,2048]{1,0:T(8,128)(2,1)}, u32[]{:S(2)}, u32[]{:S(2)}) %collective-permute-start.133) | collective-permute-done | bytes 720928 | tf_op jit(solution)/shard_map/ppermute | solution.py:24
  698.1 7.4 shard_map.282
  721.4 4.4 fusion.3
  737.5 7.2 collective-permute-done.127
  759.2 4.1 collective-permute-start.84
  774.8 4.1 collective-permute-done.85
  780.5 7.1 collective-permute-start.90
  787.6 5.5 collective-permute-done.80
  798.7 6.6 collective-permute-start.134
  809.1 3.3 fusion.38
  812.9 9.9 %collective-permute-done.86 = bf16[256,256]{1,0:T(8,128)(2,1)S(1)} collective-permute-done((bf16[256,256]{1,0:T(8,128)(2,1)S(1)}, bf16[256,256]{1,0:T(8,128)(2,1)S(1)}, u32[]{:S(2)}, u32[]{:S(2)}) %collective-permute-start.86) | collective-permute-done | bytes 131104 | tf_op jit(solution)/shard_map/ppermute | solution.py:24
  822.9 17.0 %collective-permute-start.87 = (bf16[64,256]{1,0:T(8,128)(2,1)S(1)}, bf16[64,256]{1,0:T(8,128)(2,1)S(1)}, u32[]{:S(2)}, u32[]{:S(2)}) collective-permute-start(bf16[64,256]{1,0:T(8,128)(2,1)S(1)} %get-tuple-element.338), channel_id=1, source_target_pairs={{0,3},{1,2},{2,1},{3,0},{4,7},{5,6},{6,5},{7,4},{8,11},{9,10},{10,... | collective-permute-start | bytes 98312 | tf_op jit(solution)/shard_map/ppermute | solution.py:20
  839.9 3.5 collective-permute-start.88
  844.7 5.2 collective-permute-start.106
  854.8 4.5 collective-permute-start.118
  862.2 10.4 %collective-permute-done.120 = bf16[128,2048]{1,0:T(8,128)(2,1)S(1)} collective-permute-done((bf16[128,2048]{1,0:T(8,128)(2,1)S(1)}, bf16[128,2048]{1,0:T(8,128)(2,1)S(1)}, u32[]{:S(2)}, u32[]{:S(2)}) %collective-permute-start.120) | collective-permute-done | bytes 524320 | tf_op jit(solution)/shard_map/ppermute | solution.py:24
  873.2 10.6 %collective-permute-done.99 = bf16[512,512]{1,0:T(8,128)(2,1)S(1)} collective-permute-done((bf16[512,512]{1,0:T(8,128)(2,1)S(1)}, bf16[512,512]{1,0:T(8,128)(2,1)S(1)}, u32[]{:S(2)}, u32[]{:S(2)}) %collective-permute-start.99) | collective-permute-done | bytes 524320 | tf_op jit(solution)/shard_map/ppermute | solution.py:24
  888.2 6.8 collective-permute-start.122
  895.1 4.2 collective-permute-done.100
  899.5 4.0 collective-permute-start.101
  (751 shorter events, 263.9 us)
Async XLA Ops:
  0.7 99.2 %collective-permute-start.2 = (bf16[128,2048]{1,0:T(8,128)(2,1)}, bf16[128,2048]{1,0:T(8,128)(2,1)S(1)}, u32[]{:S(2)}, u32[]{:S(2)}) collective-permute-start(bf16[128,2048]{1,0:T(8,128)(2,1)} %bitcast.107), channel_id=1, source_target_pairs={{0,3},{1,2},{2,1},{3,0},{4,7},{5,6},{6,5},{7,4},{8,11},{9,10},{10,... | collective-permute-start | bytes 1572872 | tf_op jit(solution)/shard_map/ppermute | solution.py:20
  2.9 97.0 %collective-permute-start.1 = (bf16[128,2048]{1,0:T(8,128)(2,1)}, bf16[128,2048]{1,0:T(8,128)(2,1)}, u32[]{:S(2)}, u32[]{:S(2)}) collective-permute-start(bf16[128,2048]{1,0:T(8,128)(2,1)} %bitcast.108), channel_id=1, source_target_pairs={{0,2},{1,3},{2,0},{3,1},{4,6},{5,7},{6,4},{7,5},{8,10},{9,11},{10,... | collective-permute-start | bytes 1572872 | tf_op jit(solution)/shard_map/ppermute | solution.py:20
  9.0 18.9 %collective-permute-start.4 = (bf16[1,8,256]{2,1,0:T(8,128)(2,1)S(1)}, bf16[1,8,256]{2,1,0:T(8,128)(2,1)S(1)}, u32[]{:S(2)}, u32[]{:S(2)}) collective-permute-start(bf16[1,8,256]{2,1,0:T(8,128)(2,1)S(1)} %reshape.177), channel_id=1, source_target_pairs={{0,2},{1,3},{2,0},{3,1},{4,6},{5,7},{6,4},{7,5},{8,10},{9,11},{10,... | collective-permute-start | bytes 12296 | tf_op jit(solution)/shard_map/ppermute | solution.py:20
  9.1 18.9 %collective-permute-start.5 = (bf16[1,8,256]{2,1,0:T(8,128)(2,1)S(1)}, bf16[1,8,256]{2,1,0:T(8,128)(2,1)S(1)}, u32[]{:S(2)}, u32[]{:S(2)}) collective-permute-start(bf16[1,8,256]{2,1,0:T(8,128)(2,1)S(1)} %reshape.177), channel_id=1, source_target_pairs={{0,1},{1,0},{2,3},{3,2},{4,5},{5,4},{6,7},{7,6},{8,9},{9,8},{10,11... | collective-permute-start | bytes 12296 | tf_op jit(solution)/shard_map/ppermute | solution.py:20
  58.5 43.9 %collective-permute-start = (bf16[128,2048]{1,0:T(8,128)(2,1)S(1)}, bf16[128,2048]{1,0:T(8,128)(2,1)S(1)}, u32[]{:S(2)}, u32[]{:S(2)}) collective-permute-start(bf16[128,2048]{1,0:T(8,128)(2,1)S(1)} %bitcast.109), channel_id=1, source_target_pairs={{0,1},{1,0},{2,3},{3,2},{4,5},{5,4},{6,7},{7,6},{8,9},{9,8},{10,11... | collective-permute-start | bytes 1572872 | tf_op jit(solution)/shard_map/ppermute | solution.py:20
  59.1 21.2 %collective-permute-start.24 = (bf16[256,512]{1,0:T(8,128)(2,1)S(1)}, bf16[256,512]{1,0:T(8,128)(2,1)S(1)}, u32[]{:S(2)}, u32[]{:S(2)}) collective-permute-start(bf16[256,512]{1,0:T(8,128)(2,1)S(1)} %copy-done.125), channel_id=1, source_target_pairs={{0,4},{4,0},{1,5},{5,1},{2,6},{6,2},{3,7},{7,3},{8,12},{12,8},{9,1... | collective-permute-start | bytes 786440 | tf_op jit(solution)/shard_map/ppermute | solution.py:24
  80.3 19.4 %collective-permute-start.19 = (bf16[512,256]{1,0:T(8,128)(2,1)S(1)}, bf16[512,256]{1,0:T(8,128)(2,1)S(1)}, u32[]{:S(2)}, u32[]{:S(2)}) collective-permute-start(bf16[512,256]{1,0:T(8,128)(2,1)S(1)} %pad_maximum_fusion.39), channel_id=1, source_target_pairs={{0,16},{16,0},{1,17},{17,1},{2,18},{18,2},{3,19},{19,3},{4,20},{20... | collective-permute-start | bytes 786440 | tf_op jit(solution)/shard_map/ppermute | solution.py:24
  99.7 36.7 %collective-permute-start.25 = (bf16[512,512]{1,0:T(8,128)(2,1)S(1)}, bf16[512,512]{1,0:T(8,128)(2,1)S(1)}, u32[]{:S(2)}, u32[]{:S(2)}) collective-permute-start(bf16[512,512]{1,0:T(8,128)(2,1)S(1)} %pad_maximum_fusion.28), channel_id=1, source_target_pairs={{0,16},{16,0},{1,17},{17,1},{2,18},{18,2},{3,19},{19,3},{4,20},{20... | collective-permute-start | bytes 1572872 | tf_op jit(solution)/shard_map/ppermute | solution.py:24
  99.9 20.3 %collective-permute-start.30 = (bf16[256,512]{1,0:T(8,128)(2,1)S(1)}, bf16[256,512]{1,0:T(8,128)(2,1)S(1)}, u32[]{:S(2)}, u32[]{:S(2)}) collective-permute-start(bf16[256,512]{1,0:T(8,128)(2,1)S(1)} %pad_maximum_fusion.42), channel_id=1, source_target_pairs={{0,4},{4,0},{1,5},{5,1},{2,6},{6,2},{3,7},{7,3},{8,12},{12,8},{9,1... | collective-permute-start | bytes 786440 | tf_op jit(solution)/shard_map/ppermute | solution.py:24
  100.0 25.9 %collective-permute-start.35 = (bf16[64,2048]{1,0:T(8,128)(2,1)S(1)}, bf16[64,2048]{1,0:T(8,128)(2,1)S(1)}, u32[]{:S(2)}, u32[]{:S(2)}) collective-permute-start(bf16[64,2048]{1,0:T(8,128)(2,1)S(1)} %collective-permute-done.34), channel_id=1, source_target_pairs={{0,4},{4,0},{1,5},{5,1},{2,6},{6,2},{3,7},{7,3},{8,12},{12,8},{9,1... | collective-permute-start | bytes 786440 | tf_op jit(solution)/shard_map/ppermute | solution.py:24
  102.3 43.8 %collective-permute-start.20 = (bf16[1024,256]{1,0:T(8,128)(2,1)S(1)}, bf16[1024,256]{1,0:T(8,128)(2,1)S(1)}, u32[]{:S(2)}, u32[]{:S(2)}) collective-permute-start(bf16[1024,256]{1,0:T(8,128)(2,1)S(1)} %pad_maximum_fusion.27), channel_id=1, source_target_pairs={{0,8},{8,0},{1,9},{9,1},{2,10},{10,2},{3,11},{11,3},{4,12},{12,4},... | collective-permute-start | bytes 1572872 | tf_op jit(solution)/shard_map/ppermute | solution.py:24
  109.6 20.1 %collective-permute-start.44 = (bf16[64,1408]{1,0:T(8,128)(2,1)S(1)}, bf16[64,1408]{1,0:T(8,128)(2,1)S(1)}, u32[]{:S(2)}, u32[]{:S(2)}) collective-permute-start(bf16[64,1408]{1,0:T(8,128)(2,1)S(1)} %get-tuple-element.257), channel_id=1, source_target_pairs={{0,3},{1,2},{2,1},{3,0},{4,7},{5,6},{6,5},{7,4},{8,11},{9,10},{10,... | collective-permute-start | bytes 540680 | tf_op jit(solution)/shard_map/ppermute | solution.py:20
  144.5 18.9 %collective-permute-start.36 = (bf16[128,2048]{1,0:T(8,128)(2,1)S(1)}, bf16[128,2048]{1,0:T(8,128)(2,1)S(1)}, u32[]{:S(2)}, u32[]{:S(2)}) collective-permute-start(bf16[128,2048]{1,0:T(8,128)(2,1)S(1)} %pad_maximum_fusion.30), channel_id=1, source_target_pairs={{0,16},{16,0},{1,17},{17,1},{2,18},{18,2},{3,19},{19,3},{4,20},{20... | collective-permute-start | bytes 1572872 | tf_op jit(solution)/shard_map/ppermute | solution.py:24
  145.4 123.6 %collective-permute-start.47 = (bf16[256,1408]{1,0:T(8,128)(2,1)S(1)}, bf16[256,1408]{1,0:T(8,128)(2,1)S(1)}, u32[]{:S(2)}, u32[]{:S(2)}) collective-permute-start(bf16[256,1408]{1,0:T(8,128)(2,1)S(1)} %pad_maximum_fusion.24), channel_id=1, source_target_pairs={{0,4},{4,0},{1,5},{5,1},{2,6},{6,2},{3,7},{7,3},{8,12},{12,8},{9,1... | collective-permute-start | bytes 2162696 | tf_op jit(solution)/shard_map/ppermute | solution.py:24
  146.2 33.6 %collective-permute-start.26 = (bf16[1024,512]{1,0:T(8,128)(2,1)S(1)}, bf16[1024,512]{1,0:T(8,128)(2,1)S(1)}, u32[]{:S(2)}, u32[]{:S(2)}) collective-permute-start(bf16[1024,512]{1,0:T(8,128)(2,1)S(1)} %pad_maximum_fusion.17), channel_id=1, source_target_pairs={{0,8},{8,0},{1,9},{9,1},{2,10},{10,2},{3,11},{11,3},{4,12},{12,4},... | collective-permute-start | bytes 3145736 | tf_op jit(solution)/shard_map/ppermute | solution.py:24
  148.8 31.0 %collective-permute-start.56 = (bf16[176,2048]{1,0:T(8,128)(2,1)S(1)}, bf16[176,2048]{1,0:T(8,128)(2,1)S(1)}, u32[]{:S(2)}, u32[]{:S(2)}) collective-permute-start(bf16[176,2048]{1,0:T(8,128)(2,1)S(1)} %copy-done.139), channel_id=1, source_target_pairs={{0,0},{8,1},{16,2},{24,3},{1,4},{9,5},{17,6},{25,7},{2,8},{10,9},{... | collective-permute-start | bytes 2162696 | tf_op jit(solution)/shard_map/ppermute | solution.py:103
  154.0 75.4 %collective-permute-start.32 = (bf16[1024,512]{1,0:T(8,128)(2,1)S(1)}, bf16[1024,512]{1,0:T(8,128)(2,1)S(1)}, u32[]{:S(2)}, u32[]{:S(2)}) collective-permute-start(bf16[1024,512]{1,0:T(8,128)(2,1)S(1)} %pad_maximum_fusion.18), channel_id=1, source_target_pairs={{0,8},{8,0},{1,9},{9,1},{2,10},{10,2},{3,11},{11,3},{4,12},{12,4},... | collective-permute-start | bytes 3145736 | tf_op jit(solution)/shard_map/ppermute | solution.py:24
  163.7 65.9 %collective-permute-start.37 = (bf16[256,2048]{1,0:T(8,128)(2,1)S(1)}, bf16[256,2048]{1,0:T(8,128)(2,1)S(1)}, u32[]{:S(2)}, u32[]{:S(2)}) collective-permute-start(bf16[256,2048]{1,0:T(8,128)(2,1)S(1)} %pad_maximum_fusion.19), channel_id=1, source_target_pairs={{0,8},{8,0},{1,9},{9,1},{2,10},{10,2},{3,11},{11,3},{4,12},{12,4},... | collective-permute-start | bytes 3145736 | tf_op jit(solution)/shard_map/ppermute | solution.py:24
  179.8 36.4 %collective-permute-start.60 = (bf16[128,2048]{1,0:T(8,128)(2,1)S(1)}, bf16[128,2048]{1,0:T(8,128)(2,1)S(1)}, u32[]{:S(2)}, u32[]{:S(2)}) collective-permute-start(bf16[128,2048]{1,0:T(8,128)(2,1)S(1)} %bitcast.113), channel_id=1, source_target_pairs={{0,1},{1,0},{2,3},{3,2},{4,5},{5,4},{6,7},{7,6},{8,9},{9,8},{10,11... | collective-permute-start | bytes 1572872 | tf_op jit(solution)/shard_map/ppermute | solution.py:20
  179.8 41.0 %collective-permute-start.61 = (bf16[128,2048]{1,0:T(8,128)(2,1)S(1)}, bf16[128,2048]{1,0:T(8,128)(2,1)S(1)}, u32[]{:S(2)}, u32[]{:S(2)}) collective-permute-start(bf16[128,2048]{1,0:T(8,128)(2,1)S(1)} %bitcast.115), channel_id=1, source_target_pairs={{0,2},{1,3},{2,0},{3,1},{4,6},{5,7},{6,4},{7,5},{8,10},{9,11},{10,... | collective-permute-start | bytes 1572872 | tf_op jit(solution)/shard_map/ppermute | solution.py:20
  216.2 54.4 %collective-permute-start.62 = (bf16[128,2048]{1,0:T(8,128)(2,1)S(1)}, bf16[128,2048]{1,0:T(8,128)(2,1)S(1)}, u32[]{:S(2)}, u32[]{:S(2)}) collective-permute-start(bf16[128,2048]{1,0:T(8,128)(2,1)S(1)} %bitcast.116), channel_id=1, source_target_pairs={{0,3},{1,2},{2,1},{3,0},{4,7},{5,6},{6,5},{7,4},{8,11},{9,10},{10,... | collective-permute-start | bytes 1572872 | tf_op jit(solution)/shard_map/ppermute | solution.py:20
  235.5 34.5 %collective-permute-start.53 = (bf16[256,1408]{1,0:T(8,128)(2,1)S(1)}, bf16[256,1408]{1,0:T(8,128)(2,1)S(1)}, u32[]{:S(2)}, u32[]{:S(2)}) collective-permute-start(bf16[256,1408]{1,0:T(8,128)(2,1)S(1)} %pad_maximum_fusion.25), channel_id=1, source_target_pairs={{0,4},{4,0},{1,5},{5,1},{2,6},{6,2},{3,7},{7,3},{8,12},{12,8},{9,1... | collective-permute-start | bytes 2162696 | tf_op jit(solution)/shard_map/ppermute | solution.py:24
  247.7 47.1 %collective-permute-start.40 = (bf16[128,2048]{1,0:T(8,128)(2,1)S(1)}, bf16[128,2048]{1,0:T(8,128)(2,1)S(1)}, u32[]{:S(2)}, u32[]{:S(2)}) collective-permute-start(bf16[128,2048]{1,0:T(8,128)(2,1)S(1)} %get-tuple-element.183), channel_id=1, source_target_pairs={{0,3},{1,2},{2,1},{3,0},{4,7},{5,6},{6,5},{7,4},{8,11},{9,10},{10,... | collective-permute-start | bytes 1572872 | tf_op jit(solution)/shard_map/ppermute | solution.py:20
  268.9 36.8 %collective-permute-start.39 = (bf16[128,2048]{1,0:T(8,128)(2,1)S(1)}, bf16[128,2048]{1,0:T(8,128)(2,1)S(1)}, u32[]{:S(2)}, u32[]{:S(2)}) collective-permute-start(bf16[128,2048]{1,0:T(8,128)(2,1)S(1)} %get-tuple-element.184), channel_id=1, source_target_pairs={{0,2},{1,3},{2,0},{3,1},{4,6},{5,7},{6,4},{7,5},{8,10},{9,11},{10,... | collective-permute-start | bytes 1572872 | tf_op jit(solution)/shard_map/ppermute | solution.py:20
  268.9 36.8 %collective-permute-start.38 = (bf16[128,2048]{1,0:T(8,128)(2,1)S(1)}, bf16[128,2048]{1,0:T(8,128)(2,1)S(1)}, u32[]{:S(2)}, u32[]{:S(2)}) collective-permute-start(bf16[128,2048]{1,0:T(8,128)(2,1)S(1)} %get-tuple-element.182), channel_id=1, source_target_pairs={{0,1},{1,0},{2,3},{3,2},{4,5},{5,4},{6,7},{7,6},{8,9},{9,8},{10,11... | collective-permute-start | bytes 1572872 | tf_op jit(solution)/shard_map/ppermute | solution.py:20
  270.4 40.8 %collective-permute-start.57 = (bf16[176,2048]{1,0:T(8,128)(2,1)S(1)}, bf16[176,2048]{1,0:T(8,128)(2,1)S(1)}, u32[]{:S(2)}, u32[]{:S(2)}) collective-permute-start(bf16[176,2048]{1,0:T(8,128)(2,1)S(1)} %collective-permute-done.56), channel_id=1, source_target_pairs={{0,4},{4,0},{1,5},{5,1},{2,6},{6,2},{3,7},{7,3},{8,12},{12,8},{9,1... | collective-permute-start | bytes 2162696 | tf_op jit(solution)/shard_map/ppermute | solution.py:24
  270.6 40.9 %collective-permute-start.54 = (bf16[512,1408]{1,0:T(8,128)(2,1)S(1)}, bf16[512,1408]{1,0:T(8,128)(2,1)S(1)}, u32[]{:S(2)}, u32[]{:S(2)}) collective-permute-start(bf16[512,1408]{1,0:T(8,128)(2,1)S(1)} %pad_maximum_fusion.13), channel_id=1, source_target_pairs={{0,16},{16,0},{1,17},{17,1},{2,18},{18,2},{3,19},{19,3},{4,20},{20... | collective-permute-start | bytes 4325384 | tf_op jit(solution)/shard_map/ppermute | solution.py:24
  306.3 36.4 %collective-permute-start.48 = (bf16[512,1408]{1,0:T(8,128)(2,1)S(1)}, bf16[512,1408]{1,0:T(8,128)(2,1)S(1)}, u32[]{:S(2)}, u32[]{:S(2)}) collective-permute-start(bf16[512,1408]{1,0:T(8,128)(2,1)S(1)} %pad_maximum_fusion.12), channel_id=1, source_target_pairs={{0,16},{16,0},{1,17},{17,1},{2,18},{18,2},{3,19},{19,3},{4,20},{20... | collective-permute-start | bytes 4325384 | tf_op jit(solution)/shard_map/ppermute | solution.py:24
  311.4 62.1 %collective-permute-start.58 = (bf16[352,2048]{1,0:T(8,128)(2,1)S(1)}, bf16[352,2048]{1,0:T(8,128)(2,1)S(1)}, u32[]{:S(2)}, u32[]{:S(2)}) collective-permute-start(bf16[352,2048]{1,0:T(8,128)(2,1)S(1)} %pad_maximum_fusion.14), channel_id=1, source_target_pairs={{0,16},{16,0},{1,17},{17,1},{2,18},{18,2},{3,19},{19,3},{4,20},{20... | collective-permute-start | bytes 4325384 | tf_op jit(solution)/shard_map/ppermute | solution.py:24
  312.3 75.9 %collective-permute-start.55 = (bf16[1024,1408]{1,0:T(8,128)(2,1)S(1)}, bf16[1024,1408]{1,0:T(8,128)(2,1)S(1)}, u32[]{:S(2)}, u32[]{:S(2)}) collective-permute-start(bf16[1024,1408]{1,0:T(8,128)(2,1)S(1)} %pad_maximum_fusion.4), channel_id=1, source_target_pairs={{0,8},{8,0},{1,9},{9,1},{2,10},{10,2},{3,11},{11,3},{4,12},{12,4},... | collective-permute-start | bytes 8650760 | tf_op jit(solution)/shard_map/ppermute | solution.py:24
  343.5 47.2 %collective-permute-start.49 = (bf16[1024,1408]{1,0:T(8,128)(2,1)S(1)}, bf16[1024,1408]{1,0:T(8,128)(2,1)S(1)}, u32[]{:S(2)}, u32[]{:S(2)}) collective-permute-start(bf16[1024,1408]{1,0:T(8,128)(2,1)S(1)} %pad_maximum_fusion.3), channel_id=1, source_target_pairs={{0,8},{8,0},{1,9},{9,1},{2,10},{10,2},{3,11},{11,3},{4,12},{12,4},... | collective-permute-start | bytes 8650760 | tf_op jit(solution)/shard_map/ppermute | solution.py:24
  345.3 29.2 %collective-permute-start.43 = (bf16[128,2048]{1,0:T(8,128)(2,1)S(1)}, bf16[128,2048]{1,0:T(8,128)(2,1)S(1)}, u32[]{:S(2)}, u32[]{:S(2)}) collective-permute-start(bf16[128,2048]{1,0:T(8,128)(2,1)S(1)} %multiply_convert_fusion.3), channel_id=1, source_target_pairs={{0,3},{1,2},{2,1},{3,0},{4,7},{5,6},{6,5},{7,4},{8,11},{9,10},{10,... | collective-permute-start | bytes 1572872 | tf_op jit(solution)/shard_map/ppermute | solution.py:20
  345.4 30.3 %collective-permute-start.42 = (bf16[128,2048]{1,0:T(8,128)(2,1)S(1)}, bf16[128,2048]{1,0:T(8,128)(2,1)S(1)}, u32[]{:S(2)}, u32[]{:S(2)}) collective-permute-start(bf16[128,2048]{1,0:T(8,128)(2,1)S(1)} %multiply_convert_fusion.3), channel_id=1, source_target_pairs={{0,2},{1,3},{2,0},{3,1},{4,6},{5,7},{6,4},{7,5},{8,10},{9,11},{10,... | collective-permute-start | bytes 1572872 | tf_op jit(solution)/shard_map/ppermute | solution.py:20
  374.5 26.2 %collective-permute-start.59 = (bf16[704,2048]{1,0:T(8,128)(2,1)S(1)}, bf16[704,2048]{1,0:T(8,128)(2,1)}, u32[]{:S(2)}, u32[]{:S(2)}) collective-permute-start(bf16[704,2048]{1,0:T(8,128)(2,1)S(1)} %pad_maximum_fusion.5), channel_id=1, source_target_pairs={{0,8},{8,0},{1,9},{9,1},{2,10},{10,2},{3,11},{11,3},{4,12},{12,4},... | collective-permute-start | bytes 8650760 | tf_op jit(solution)/shard_map/ppermute | solution.py:24
  454.8 25.7 %collective-permute-start.71 = (bf16[352,2048]{1,0:T(8,128)(2,1)S(1)}, bf16[352,2048]{1,0:T(8,128)(2,1)}, u32[]{:S(2)}, u32[]{:S(2)}) collective-permute-start(bf16[352,2048]{1,0:T(8,128)(2,1)S(1)} %get-tuple-element.133), channel_id=1, source_target_pairs={{0,8},{8,0},{1,9},{9,1},{2,10},{10,2},{3,11},{11,3},{4,12},{12,4},... | collective-permute-start | bytes 4325384 | tf_op jit(solution)/shard_map/ppermute | solution.py:24
  464.9 24.5 %collective-permute-start.64 = (bf16[128,2048]{1,0:T(8,128)(2,1)S(1)}, bf16[128,2048]{1,0:T(8,128)(2,1)S(1)}, u32[]{:S(2)}, u32[]{:S(2)}) collective-permute-start(bf16[128,2048]{1,0:T(8,128)(2,1)S(1)} %get-tuple-element.181), channel_id=1, source_target_pairs={{0,2},{1,3},{2,0},{3,1},{4,6},{5,7},{6,4},{7,5},{8,10},{9,11},{10,... | collective-permute-start | bytes 1572872 | tf_op jit(solution)/shard_map/ppermute | solution.py:20
  466.1 24.8 %collective-permute-start.63 = (bf16[128,2048]{1,0:T(8,128)(2,1)S(1)}, bf16[128,2048]{1,0:T(8,128)(2,1)S(1)}, u32[]{:S(2)}, u32[]{:S(2)}) collective-permute-start(bf16[128,2048]{1,0:T(8,128)(2,1)S(1)} %get-tuple-element.179), channel_id=1, source_target_pairs={{0,1},{1,0},{2,3},{3,2},{4,5},{5,4},{6,7},{7,6},{8,9},{9,8},{10,11... | collective-permute-start | bytes 1572872 | tf_op jit(solution)/shard_map/ppermute | solution.py:20
  468.6 22.8 %collective-permute-start.67 = (bf16[512,1408]{1,0:T(8,128)(2,1)S(1)}, bf16[512,1408]{1,0:T(8,128)(2,1)S(1)}, u32[]{:S(2)}, u32[]{:S(2)}) collective-permute-start(bf16[512,1408]{1,0:T(8,128)(2,1)S(1)} %convolution_convert_fusion.3), channel_id=1, source_target_pairs={{0,8},{8,0},{1,9},{9,1},{2,10},{10,2},{3,11},{11,3},{4,12},{12,4},... | collective-permute-start | bytes 4325384 | tf_op jit(solution)/shard_map/ppermute | solution.py:24
  491.3 33.2 %collective-permute-start.132 = (bf16[352,2048]{1,0:T(8,128)(2,1)S(1)}, bf16[352,2048]{1,0:T(8,128)(2,1)S(1)}, u32[]{:S(2)}, u32[]{:S(2)}) collective-permute-start(bf16[352,2048]{1,0:T(8,128)(2,1)S(1)} %add_convert_fusion.4), channel_id=1, source_target_pairs={{0,16},{16,0},{1,17},{17,1},{2,18},{18,2},{3,19},{19,3},{4,20},{20... | collective-permute-start | bytes 4325384 | tf_op jit(solution)/shard_map/ppermute | solution.py:24
  495.0 99.1 %collective-permute-start.75 = (bf16[512,1408]{1,0:T(8,128)(2,1)}, bf16[512,1408]{1,0:T(8,128)(2,1)}, u32[]{:S(2)}, u32[]{:S(2)}) collective-permute-start(bf16[512,1408]{1,0:T(8,128)(2,1)} %add_convert_fusion.8), channel_id=1, source_target_pairs={{0,16},{16,0},{1,17},{17,1},{2,18},{18,2},{3,19},{19,3},{4,20},{20... | collective-permute-start | bytes 4325384 | tf_op jit(solution)/shard_map/ppermute | solution.py:24
  497.4 89.0 %collective-permute-start.123 = (bf16[512,1408]{1,0:T(8,128)(2,1)}, bf16[512,1408]{1,0:T(8,128)(2,1)}, u32[]{:S(2)}, u32[]{:S(2)}) collective-permute-start(bf16[512,1408]{1,0:T(8,128)(2,1)} %add_convert_fusion.6), channel_id=1, source_target_pairs={{0,16},{16,0},{1,17},{17,1},{2,18},{18,2},{3,19},{19,3},{4,20},{20... | collective-permute-start | bytes 4325384 | tf_op jit(solution)/shard_map/ppermute | solution.py:24
  529.7 69.3 %collective-permute-start.74 = (bf16[128,2048]{1,0:T(8,128)(2,1)}, bf16[128,2048]{1,0:T(8,128)(2,1)}, u32[]{:S(2)}, u32[]{:S(2)}) collective-permute-start(bf16[128,2048]{1,0:T(8,128)(2,1)} %fusion.72), channel_id=1, source_target_pairs={{0,3},{1,2},{2,1},{3,0},{4,7},{5,6},{6,5},{7,4},{8,11},{9,10},{10,... | collective-permute-start | bytes 1572872 | tf_op jit(solution)/shard_map/ppermute | solution.py:20
  529.7 70.5 %collective-permute-start.73 = (bf16[128,2048]{1,0:T(8,128)(2,1)}, bf16[128,2048]{1,0:T(8,128)(2,1)}, u32[]{:S(2)}, u32[]{:S(2)}) collective-permute-start(bf16[128,2048]{1,0:T(8,128)(2,1)} %fusion.72), channel_id=1, source_target_pairs={{0,2},{1,3},{2,0},{3,1},{4,6},{5,7},{6,4},{7,5},{8,10},{9,11},{10,... | collective-permute-start | bytes 1572872 | tf_op jit(solution)/shard_map/ppermute | solution.py:20
  530.7 69.4 %collective-permute-start.72 = (bf16[128,2048]{1,0:T(8,128)(2,1)}, bf16[128,2048]{1,0:T(8,128)(2,1)}, u32[]{:S(2)}, u32[]{:S(2)}) collective-permute-start(bf16[128,2048]{1,0:T(8,128)(2,1)} %fusion.72), channel_id=1, source_target_pairs={{0,1},{1,0},{2,3},{3,2},{4,5},{5,4},{6,7},{7,6},{8,9},{9,8},{10,11... | collective-permute-start | bytes 1572872 | tf_op jit(solution)/shard_map/ppermute | solution.py:20
  589.6 72.0 %collective-permute-start.124 = (bf16[256,1408]{1,0:T(8,128)(2,1)}, bf16[256,1408]{1,0:T(8,128)(2,1)}, u32[]{:S(2)}, u32[]{:S(2)}) collective-permute-start(bf16[256,1408]{1,0:T(8,128)(2,1)} %broadcast_select_fusion.28), channel_id=1, source_target_pairs={{0,4},{4,0},{1,5},{5,1},{2,6},{6,2},{3,7},{7,3},{8,12},{12,8},{9,1... | collective-permute-start | bytes 2162696 | tf_op jit(solution)/shard_map/ppermute | solution.py:24
  596.8 80.3 %collective-permute-start.128 = (bf16[256,1408]{1,0:T(8,128)(2,1)}, bf16[256,1408]{1,0:T(8,128)(2,1)}, u32[]{:S(2)}, u32[]{:S(2)}) collective-permute-start(bf16[256,1408]{1,0:T(8,128)(2,1)} %broadcast_select_fusion.27), channel_id=1, source_target_pairs={{0,4},{4,0},{1,5},{5,1},{2,6},{6,2},{3,7},{7,3},{8,12},{12,8},{9,1... | collective-permute-start | bytes 2162696 | tf_op jit(solution)/shard_map/ppermute | solution.py:24
  598.9 93.6 %collective-permute-start.133 = (bf16[176,2048]{1,0:T(8,128)(2,1)}, bf16[176,2048]{1,0:T(8,128)(2,1)}, u32[]{:S(2)}, u32[]{:S(2)}) collective-permute-start(bf16[176,2048]{1,0:T(8,128)(2,1)} %broadcast_select_fusion.24), channel_id=1, source_target_pairs={{0,4},{4,0},{1,5},{5,1},{2,6},{6,2},{3,7},{7,3},{8,12},{12,8},{9,1... | collective-permute-start | bytes 2162696 | tf_op jit(solution)/shard_map/ppermute | solution.py:24
  608.6 89.5 %collective-permute-start.79 = (bf16[512,256]{1,0:T(8,128)(2,1)}, bf16[512,256]{1,0:T(8,128)(2,1)S(1)}, u32[]{:S(2)}, u32[]{:S(2)}) collective-permute-start(bf16[512,256]{1,0:T(8,128)(2,1)} %get-tuple-element.62), channel_id=1, source_target_pairs={{4,0},{5,1},{6,2},{7,3},{12,8},{13,9},{14,10},{15,11},{20,16},{21,... | collective-permute-start | bytes 786440 | tf_op jit(solution)/shard_map/ppermute | solution.py:383
  619.0 152.0 %collective-permute-start.105 = (bf16[512,512]{1,0:T(8,128)(2,1)}, bf16[512,512]{1,0:T(8,128)(2,1)}, u32[]{:S(2)}, u32[]{:S(2)}) collective-permute-start(bf16[512,512]{1,0:T(8,128)(2,1)} %convolution_convert_fusion.8), channel_id=1, source_target_pairs={{0,8},{8,0},{1,9},{9,1},{2,10},{10,2},{3,11},{11,3},{4,12},{12,4},... | collective-permute-start | bytes 1572872 | tf_op jit(solution)/shard_map/ppermute | solution.py:24
  661.6 104.9 %collective-permute-start.119 = (bf16[128,2048]{1,0:T(8,128)(2,1)}, bf16[128,2048]{1,0:T(8,128)(2,1)}, u32[]{:S(2)}, u32[]{:S(2)}) collective-permute-start(bf16[128,2048]{1,0:T(8,128)(2,1)} %get-tuple-element.164), channel_id=1, source_target_pairs={{0,8},{8,0},{1,9},{9,1},{2,10},{10,2},{3,11},{11,3},{4,12},{12,4},... | collective-permute-start | bytes 1572872 | tf_op jit(solution)/shard_map/ppermute | solution.py:24
  677.0 58.9 %collective-permute-start.125 = (bf16[64,1408]{1,0:T(8,128)(2,1)}, bf16[64,1408]{1,0:T(8,128)(2,1)}, u32[]{:S(2)}, u32[]{:S(2)}) collective-permute-start(bf16[64,1408]{1,0:T(8,128)(2,1)} %get-tuple-element.247), channel_id=1, source_target_pairs={{0,3},{1,2},{2,1},{3,0},{4,7},{5,6},{6,5},{7,4},{8,11},{9,10},{10,... | collective-permute-start | bytes 540680 | tf_op jit(solution)/shard_map/ppermute | solution.py:20
  692.5 44.3 %collective-permute-start.126 = (bf16[64,1408]{1,0:T(8,128)(2,1)}, bf16[64,1408]{1,0:T(8,128)(2,1)}, u32[]{:S(2)}, u32[]{:S(2)}) collective-permute-start(bf16[64,1408]{1,0:T(8,128)(2,1)} %get-tuple-element.248), channel_id=1, source_target_pairs={{0,2},{1,3},{2,0},{3,1},{4,6},{5,7},{6,4},{7,5},{8,10},{9,11},{10,... | collective-permute-start | bytes 540680 | tf_op jit(solution)/shard_map/ppermute | solution.py:20
  757.1 22.8 %collective-permute-start.82 = (bf16[128,2048]{1,0:T(8,128)(2,1)}, bf16[128,2048]{1,0:T(8,128)(2,1)S(1)}, u32[]{:S(2)}, u32[]{:S(2)}) collective-permute-start(bf16[128,2048]{1,0:T(8,128)(2,1)} %get-tuple-element.170), channel_id=1, source_target_pairs={{0,3},{1,2},{2,1},{3,0},{4,7},{5,6},{6,5},{7,4},{8,11},{9,10},{10,... | collective-permute-start | bytes 1572872 | tf_op jit(solution)/shard_map/ppermute | solution.py:20
  758.6 21.9 %collective-permute-start.81 = (bf16[128,2048]{1,0:T(8,128)(2,1)}, bf16[128,2048]{1,0:T(8,128)(2,1)S(1)}, u32[]{:S(2)}, u32[]{:S(2)}) collective-permute-start(bf16[128,2048]{1,0:T(8,128)(2,1)} %get-tuple-element.171), channel_id=1, source_target_pairs={{0,2},{1,3},{2,0},{3,1},{4,6},{5,7},{6,4},{7,5},{8,10},{9,11},{10,... | collective-permute-start | bytes 1572872 | tf_op jit(solution)/shard_map/ppermute | solution.py:20
  768.7 24.5 %collective-permute-start.80 = (bf16[128,2048]{1,0:T(8,128)(2,1)}, bf16[128,2048]{1,0:T(8,128)(2,1)S(1)}, u32[]{:S(2)}, u32[]{:S(2)}) collective-permute-start(bf16[128,2048]{1,0:T(8,128)(2,1)} %get-tuple-element.169), channel_id=1, source_target_pairs={{0,1},{1,0},{2,3},{3,2},{4,5},{5,4},{6,7},{7,6},{8,9},{9,8},{10,11... | collective-permute-start | bytes 1572872 | tf_op jit(solution)/shard_map/ppermute | solution.py:20
  773.7 32.0 %collective-permute-start.78 = (bf16[128,2048]{1,0:T(8,128)(2,1)S(1)}, bf16[128,2048]{1,0:T(8,128)(2,1)S(1)}, u32[]{:S(2)}, u32[]{:S(2)}) collective-permute-start(bf16[128,2048]{1,0:T(8,128)(2,1)S(1)} %copy-done.116), channel_id=1, source_target_pairs={{0,3},{1,2},{2,1},{3,0},{4,7},{5,6},{6,5},{7,4},{8,11},{9,10},{10,... | collective-permute-start | bytes 1572872 | tf_op jit(solution)/shard_map/ppermute | solution.py:20
  778.9 27.8 %collective-permute-start.77 = (bf16[128,2048]{1,0:T(8,128)(2,1)S(1)}, bf16[128,2048]{1,0:T(8,128)(2,1)S(1)}, u32[]{:S(2)}, u32[]{:S(2)}) collective-permute-start(bf16[128,2048]{1,0:T(8,128)(2,1)S(1)} %copy-done.115), channel_id=1, source_target_pairs={{0,2},{1,3},{2,0},{3,1},{4,6},{5,7},{6,4},{7,5},{8,10},{9,11},{10,... | collective-permute-start | bytes 1572872 | tf_op jit(solution)/shard_map/ppermute | solution.py:20
  779.9 27.5 %collective-permute-start.76 = (bf16[128,2048]{1,0:T(8,128)(2,1)S(1)}, bf16[128,2048]{1,0:T(8,128)(2,1)S(1)}, u32[]{:S(2)}, u32[]{:S(2)}) collective-permute-start(bf16[128,2048]{1,0:T(8,128)(2,1)S(1)} %copy-done.114), channel_id=1, source_target_pairs={{0,1},{1,0},{2,3},{3,2},{4,5},{5,4},{6,7},{7,6},{8,9},{9,8},{10,11... | collective-permute-start | bytes 1572872 | tf_op jit(solution)/shard_map/ppermute | solution.py:20
  794.8 65.3 %collective-permute-start.104 = (bf16[512,512]{1,0:T(8,128)(2,1)S(1)}, bf16[512,512]{1,0:T(8,128)(2,1)S(1)}, u32[]{:S(2)}, u32[]{:S(2)}) collective-permute-start(bf16[512,512]{1,0:T(8,128)(2,1)S(1)} %copy-done.140), channel_id=1, source_target_pairs={{0,8},{8,0},{1,9},{9,1},{2,10},{10,2},{3,11},{11,3},{4,12},{12,4},... | collective-permute-start | bytes 1572872 | tf_op jit(solution)/shard_map/ppermute | solution.py:24
  798.7 46.0 %collective-permute-start.134 = (bf16[176,2048]{1,0:T(8,128)(2,1)S(1)}, bf16[176,2048]{1,0:T(8,128)(2,1)S(1)}, u32[]{:S(2)}, u32[]{:S(2)}) collective-permute-start(bf16[176,2048]{1,0:T(8,128)(2,1)S(1)} %copy-done.80), channel_id=1, source_target_pairs={{0,0},{1,8},{2,16},{3,24},{4,1},{5,9},{6,17},{7,25},{8,2},{9,10},{... | collective-permute-start | bytes 2162696 | tf_op jit(solution)/shard_map/ppermute | solution.py:107
  807.4 36.0 %collective-permute-start.93 = (bf16[256,256]{1,0:T(8,128)(2,1)S(1)}, bf16[256,256]{1,0:T(8,128)(2,1)S(1)}, u32[]{:S(2)}, u32[]{:S(2)}) collective-permute-start(bf16[256,256]{1,0:T(8,128)(2,1)S(1)} %broadcast_select_fusion.174), channel_id=1, source_target_pairs={{0,4},{4,0},{1,5},{5,1},{2,6},{6,2},{3,7},{7,3},{8,12},{12,8},{9,1... | collective-permute-start | bytes 393224 | tf_op jit(solution)/shard_map/ppermute | solution.py:24
  822.9 28.2 %collective-permute-start.87 = (bf16[64,256]{1,0:T(8,128)(2,1)S(1)}, bf16[64,256]{1,0:T(8,128)(2,1)S(1)}, u32[]{:S(2)}, u32[]{:S(2)}) collective-permute-start(bf16[64,256]{1,0:T(8,128)(2,1)S(1)} %get-tuple-element.338), channel_id=1, source_target_pairs={{0,3},{1,2},{2,1},{3,0},{4,7},{5,6},{6,5},{7,4},{8,11},{9,10},{10,... | collective-permute-start | bytes 98312 | tf_op jit(solution)/shard_map/ppermute | solution.py:20
  860.1 23.7 %collective-permute-start.99 = (bf16[512,512]{1,0:T(8,128)(2,1)S(1)}, bf16[512,512]{1,0:T(8,128)(2,1)S(1)}, u32[]{:S(2)}, u32[]{:S(2)}) collective-permute-start(bf16[512,512]{1,0:T(8,128)(2,1)S(1)} %fusion.10), channel_id=1, source_target_pairs={{0,16},{16,0},{1,17},{17,1},{2,18},{18,2},{3,19},{19,3},{4,20},{20... | collective-permute-start | bytes 1572872 | tf_op jit(solution)/shard_map/ppermute | solution.py:24
  862.1 22.3 %collective-permute-start.107 = (bf16[256,512]{1,0:T(8,128)(2,1)S(1)}, bf16[256,512]{1,0:T(8,128)(2,1)S(1)}, u32[]{:S(2)}, u32[]{:S(2)}) collective-permute-start(bf16[256,512]{1,0:T(8,128)(2,1)S(1)} %broadcast_select_fusion.76), channel_id=1, source_target_pairs={{0,4},{4,0},{1,5},{5,1},{2,6},{6,2},{3,7},{7,3},{8,12},{12,8},{9,1... | collective-permute-start | bytes 786440 | tf_op jit(solution)/shard_map/ppermute | solution.py:24
  (223 other events, 2410.3 us)

commit v3 on v2

--- a/solution.py
+++ b/solution.py
@@ -16,12 +16,23 @@
 WAYS = ("y", "core", "hi", "t")
 
 
-def to_partner(value, r):
-    return lax.ppermute(value, "t", [(s, s ^ r) for s in range(HEADS)])
+def after(value, *others):
+    return lax.optimization_barrier((value,) + others)[0]
+
+
+def all_after(values, *others):
+    return lax.optimization_barrier(tuple(values) + others)[: len(values)]
 
 
 def swap(value, axis):
     return lax.ppermute(value, axis, [(0, 1), (1, 0)])
+
+
+def partners(values):
+    return tuple(
+        lax.ppermute(v, "t", [(s, s ^ (r + 1)) for s in range(HEADS)])
+        for r, v in enumerate(values)
+    )
 
 
 def natural(pieces, t=None):
@@ -39,20 +50,16 @@
 
 
 def gather_rows(value):
-    return jnp.concatenate([value] + [to_partner(value, r) for r in range(1, HEADS)])
+    return jnp.concatenate((value,) + partners((value,) * 3))
 
 
 def scatter_rows(value):
     rows = value.shape[0] // HEADS
     parts = [value[r * rows : (r + 1) * rows] for r in range(HEADS)]
     total = parts[0].astype(F32)
-    for r in range(1, HEADS):
-        total = total + to_partner(parts[r], r).astype(F32)
+    for got in partners(parts[1:]):
+        total = total + got.astype(F32)
     return total
-
-
-def after(value, *others):
-    return lax.optimization_barrier((value,) + others)[0]
 
 
 def both(value, axis):
@@ -74,18 +81,31 @@
     return jnp.concatenate(out)
 
 
-def columns_in(weight):
-    n = weight.shape[1] // HEADS
-    sent = natural([weight[:, i * n : (i + 1) * n] for i in range(HEADS)])
-    got = [sent[0]] + [to_partner(sent[r], r) for r in range(1, HEADS)]
-    return jnp.concatenate(natural(got))
-
-
-def columns_out(part):
+def columns_of(weights):
+    four = []
+    for i in range(HEADS):
+        cols = []
+        for w in weights:
+            n = w.shape[1] // HEADS
+            cols.append(w[:, i * n : (i + 1) * n])
+        four.append(jnp.concatenate(cols, axis=1) if len(cols) > 1 else cols[0])
+    return natural(four)
+
+
+def columns_in(sent, *others):
+    got = partners(all_after(sent[1:], *others))
+    return jnp.concatenate(natural((sent[0],) + got))
+
+
+def columns_out(part, widths):
     own = part.shape[0] // HEADS
     sent = natural([part[n * own : (n + 1) * own] for n in range(HEADS)])
-    back = natural([sent[0]] + [to_partner(sent[r], r) for r in range(1, HEADS)])
-    return jnp.concatenate(back, axis=1).astype(F32)
+    back = natural((sent[0],) + partners(sent[1:]))
+    outs, place = [], 0
+    for w in widths:
+        outs.append(jnp.concatenate([b[:, place : place + w] for b in back], axis=1).astype(F32))
+        place += w
+    return outs
 
 
 def row_pairs():
@@ -124,9 +144,30 @@
     return add(jnp.where(first, low, high), swap(jnp.where(first, high, low), "hi"))
 
 
+def over_y(pair):
+    return add(pair[0], swap(pair[1], "y"))
+
+
 def rows_in_cells(value):
     n = value.shape[0] // HEADS
     return natural([value[i * n : (i + 1) * n] for i in range(HEADS)], cell())
+
+
+def columns_in_cells(value):
+    n = value.shape[1] // HEADS
+    return natural([value[:, i * n : (i + 1) * n] for i in range(HEADS)], cell())
+
+
+def by_columns(left, right):
+    sent = [swap(dot_tn(left[r], right).astype(BF16), "core") for r in (1, 3)]
+    return tuple(
+        (dot_tn(left[r], right) + got.astype(F32)).astype(BF16) for r, got in zip((0, 2), sent)
+    )
+
+
+def by_rows(left, right):
+    cells = rows_in_cells(dot_tn(left, right).astype(BF16))
+    return tuple(add(cells[r], swap(cells[r + 1], "core")) for r in (0, 2))
 
 
 def dot(a, b, precision=None):
@@ -432,8 +473,32 @@
     pad = -sum(sizes) % 1024
     packed = jnp.concatenate(small + (jnp.zeros((pad,), BF16),))
     packed = packed.reshape(1, 8, -1)
-    packed = jnp.concatenate(natural([packed] + [to_partner(packed, r) for r in range(1, HEADS)]))
-    packed = both_cores(both(both(packed, "hi"), "y")).reshape(devices, -1)
+    kv_cols = columns_of((key_proj, value_proj))
+    qs_cols = columns_of((query_proj, swish_proj))
+    gate_cols, up_cols = columns_of((gate_proj,)), columns_of((up_proj,))
+    across = ("y", "core", "hi")
+
+    packed = jnp.concatenate(natural((packed,) + partners((packed,) * 3)))
+    kv_in = columns_in(kv_cols, packed)
+    packed = both(packed, "hi")
+    kv_in, packed = lax.optimization_barrier((kv_in, packed))
+    kv_hi = both(kv_in, "hi")
+    qs_in = columns_in(qs_cols, kv_in)
+    packed = both(packed, "y")
+    out_in = rows_in(after(out_proj, qs_in))
+    kv_hi, qs_in, packed = lax.optimization_barrier((kv_hi, qs_in, packed))
+    packed = both_cores(packed).reshape(devices, -1)
+    kv_y, qs_hi = both(kv_hi, "y"), both(qs_in, "hi")
+    tokens_all = gather_rows(after(tokens[0], qs_in))
+    kv_y, qs_hi, tokens_all, out_in = lax.optimization_barrier((kv_y, qs_hi, tokens_all, out_in))
+    kv_full = both_cores(kv_y)
+    gate_in = columns_in(gate_cols, tokens_all)
+    gate_full = lax.all_gather(gate_in, across, axis=0, tiled=True)
+    qs_y, out_hi = both(qs_hi, "y"), both(out_in, "hi")
+    up_in = columns_in(up_cols, gate_in)
+    up_full = lax.all_gather(up_in, across, axis=0, tiled=True)
+    down_in = rows_in(after(down_proj, up_in))
+    down_full = lax.all_gather(down_in, across, axis=0, tiled=True)
     got, place = [], 0
     for size in sizes:
         got.append(packed[:, place : place + size].reshape(-1))
@@ -446,32 +511,13 @@
     bias_own = lax.dynamic_slice_in_dim(bias_full, t * key_size, key_size, 0)
 
     residual = tokens[0].astype(F32)
-    key_in, value_in = columns_in(key_proj), columns_in(value_proj)
-    tokens_all = gather_rows(tokens[0])
-    query_in = columns_in(after(query_proj, key_in))
-    swish_in_ = columns_in(after(swish_proj, value_in))
-    out_in = rows_in(after(out_proj, query_in))
-    gate_in = columns_in(after(gate_proj, tokens_all, swish_in_))
-    up_in = columns_in(after(up_proj, gate_in))
-    down_in = rows_in(after(down_proj, up_in))
-    cot_all = gather_rows(after(cotangent[0], down_in))
-    key_hi, value_hi = both(key_in, "hi"), both(value_in, "hi")
-    query_hi = both(after(query_in, key_hi), "hi")
-    swish_hi = both(after(swish_in_, value_hi), "hi")
-    out_hi = both(after(out_in, query_hi), "hi")
-    gate_hi = both(after(gate_in, swish_hi), "hi")
-    key_full = both_cores(both(key_hi, "y"))
-    value_full = both_cores(both(value_hi, "y"))
-    query_full = both_cores(both(query_hi, "y"))
-    swish_full = both_cores(both(swish_hi, "y"))
-    out_full = both_cores(both(out_hi, "y"))
-    gate_full = both_cores(both(gate_hi, "y"))
 
     wide_all = tokens_all.astype(F32)
     unit_all = wide_all * inverse(wide_all)
     normed = (unit_all * attn_full).astype(BF16)
-    key = dot(normed, key_full).astype(BF16)
-    value = dot(normed, value_full).astype(BF16)
+    kv = dot(normed, kv_full)
+    key = kv[:, :key_size].astype(BF16)
+    value = kv[:, key_size:].astype(BF16)
     low_rank = dot(normed, rankin_full)
     logits = dot_nt(low_rank, rankout_own, EXACT) + bias_own
     log_decay = jax.nn.log_sigmoid(logits) / 16.0
@@ -481,21 +527,27 @@
     )
     where = t.reshape(1).astype(jnp.int32)
     end_state, end_log = state_call(where, key, value, log_decay)
+    end_state, qs_y, out_hi = lax.optimization_barrier((end_state, qs_y, out_hi))
     in_state = chain(end_state, end_log, True)
-    up_hi = both(after(up_in, in_state), "hi")
-    down_hi = both(after(down_in, gate_hi), "hi")
-    up_full = both_cores(both(up_hi, "y"))
-    down_full = both_cores(both(down_hi, "y"))
-    query = dot(normed, query_full).astype(BF16)
-    swish_in = dot(normed, swish_full)
+    out_y = both(out_hi, "y")
+    qs_full = both_cores(qs_y)
+    qs = dot(normed, qs_full)
+    query = qs[:, :key_size].astype(BF16)
+    swish_in = qs[:, key_size:]
+    in_state, out_y, query, swish_in, down_in = lax.optimization_barrier(
+        (in_state, out_y, query, swish_in, down_in)
+    )
+    out_full = both_cores(out_y)
     gain_row = head_full.reshape(1, value_size)
     gated, mixed, saved = forward_call(
         where, query, key, value, log_decay, swish_in, gain_row, in_state
     )
-    hidden = residual + scatter_rows(dot(gated, out_full).astype(BF16))
+    attended = scatter_rows(dot(gated, out_full).astype(BF16))
+    hidden = residual + attended
 
     hidden_norm = (hidden * inverse(hidden) * mlp_full).astype(BF16)
     hidden_all = gather_rows(hidden_norm)
+    cot_all = gather_rows(after(cotangent[0], hidden_all))
     gate_val = dot(hidden_all, gate_full)
     up_val = dot(hidden_all, up_full)
     sig = jax.nn.sigmoid(gate_val)
@@ -507,38 +559,23 @@
     back_up = (back_product * silu).astype(BF16)
     back_hnorm = (dot_nt(back_gate, gate_full) + dot_nt(back_up, up_full)).astype(BF16)
 
-    def by_columns(left, right):
-        sent = [swap(dot_tn(left[r], right).astype(BF16), "core") for r in (1, 3)]
-        return [
-            (dot_tn(left[r], right) + got.astype(F32)).astype(BF16)
-            for r, got in zip((0, 2), sent)
-        ]
-
-    def by_rows(left, right):
-        cells = rows_in_cells(dot_tn(left, right).astype(BF16))
-        return [add(cells[r], swap(cells[r + 1], "core")) for r in (0, 2)]
-
-    def over_y(pair):
-        return add(pair[0], swap(pair[1], "y"))
-
-    def cells_of(value):
-        n = value.shape[1] // HEADS
-        return natural([value[:, i * n : (i + 1) * n] for i in range(HEADS)], cell())
-
-    hidden_cells, normed_cells = cells_of(hidden_all), cells_of(normed)
+    normed_cells = columns_in_cells(normed)
     back_hnorm_sum = scatter_rows(back_hnorm)
-    up_pair = by_columns(hidden_cells, back_up)
-    gate_pair = by_columns(hidden_cells, back_gate)
+    grad_gate = dot_tn(hidden_all, back_gate).astype(BF16)
+    gate_mine = lax.psum_scatter(grad_gate, across, scatter_dimension=0, tiled=True)
+    grad_up = dot_tn(hidden_all, back_up).astype(BF16)
+    up_mine = lax.psum_scatter(grad_up, across, scatter_dimension=0, tiled=True)
     down_pair = by_rows(product, cot_all)
-    back_hnorm_sum = after(back_hnorm_sum, *up_pair, *gate_pair, *down_pair)
+    back_hnorm_sum, down_0, down_1, grad_gate, grad_up = lax.optimization_barrier(
+        (back_hnorm_sum,) + down_pair + (grad_gate, grad_up)
+    )
     back_hidden, grad_mlpgain = norm_back(hidden, mlp_full, back_hnorm_sum)
     back_hidden = back_hidden + cotangent[0].astype(F32)
 
+    down_y = over_y((down_0, down_1))
     back_attn = gather_rows(back_hidden.astype(BF16))
-    up_y = over_y(up_pair)
-    back_attn = after(back_attn, up_y)
+    back_attn, down_y = lax.optimization_barrier((back_attn, down_y))
     back_gated = dot_nt(back_attn, out_full)
-    out_pair = by_rows(gated, back_attn)
     back_mixed, back_swish, grad_headgain, direct = gate_back_call(
         where, back_gated, mixed, swish_in, gain_row, query, log_decay
     )
@@ -546,37 +583,52 @@
     block_out = scatter_rows(dot(product, after(down_full, direct)).astype(BF16))
     block_out = (hidden + block_out).astype(BF16)
     swish_pair = by_columns(normed_cells, back_swish)
+    out_pair = by_rows(gated, back_attn)
+    out_state, out_0, out_1, swish_0, swish_1, down_y = lax.optimization_barrier(
+        (out_state,) + out_pair + swish_pair + (down_y,)
+    )
+    down_mine = half_hi(down_y)
+    out_y = over_y((out_0, out_1))
     back_query, back_key, back_value, back_logits = backward_call(
         where, query, key, value, log_decay, decay_slope, back_mixed, saved, out_state
     )
-    gate_y, down_y = over_y(gate_pair), over_y(down_pair)
+    back_qkv = jnp.concatenate([back_query, back_key, back_value], axis=1)
+    qkv_0, qkv_1 = by_columns(normed_cells, back_qkv)
+    qkv_0, qkv_1, out_y, back_qkv, back_logits = lax.optimization_barrier(
+        (qkv_0, qkv_1, out_y, back_qkv, back_logits)
+    )
+    qkv_y = over_y((qkv_0, qkv_1))
     back_rank = dot(back_logits, rankout_own, EXACT)
+    back_query, back_kv = back_qkv[:, :key_size], back_qkv[:, key_size:]
+    back_qs = jnp.concatenate([back_query, back_swish], axis=1)
     back_normed = (
-        dot_nt(back_key, key_full)
-        + dot_nt(back_value, value_full)
-        + dot_nt(back_query, query_full)
-        + dot_nt(back_swish, swish_full)
+        dot_nt(back_kv, kv_full)
+        + dot_nt(back_qs, qs_full)
         + dot_nt(back_rank.astype(BF16), rankin_full)
     )
     back_tokens = scatter_rows(back_normed.astype(BF16))
-    value_pair = by_columns(normed_cells, back_value)
-    key_pair = by_columns(normed_cells, back_key)
-    query_pair = by_columns(normed_cells, back_query)
     grad_bias = jnp.sum(back_logits, axis=0)
     grad_rankout = dot_tn(back_logits, low_rank, EXACT)
     grad_rankin = dot_tn(normed, back_rank.astype(BF16))
     grad_attngain = jnp.sum(back_normed * unit_all, axis=0)
+    out_mine = half_hi(after(out_y, down_mine))
+    back_tokens, qkv_y, down_mine, out_mine, grad_attngain = lax.optimization_barrier(
+        (back_tokens, qkv_y, down_mine, out_mine, grad_attngain)
+    )
     back_tokens, _ = norm_back(residual, attn_full, back_tokens)
     grad_tokens = (back_hidden + back_tokens).astype(BF16)
 
-    up_home = columns_out(half_hi(up_y))
-    gate_home = columns_out(half_hi(gate_y))
-    down_home = rows_out(half_hi(down_y))
-    out_home = rows_out(half_hi(over_y(out_pair)))
-    swish_home = columns_out(half_hi(over_y(swish_pair)))
-    value_home = columns_out(half_hi(over_y(value_pair)))
-    key_home = columns_out(half_hi(over_y(key_pair)))
-    query_home = columns_out(half_hi(over_y(query_pair)))
+    qkv_mine = half_hi(qkv_y)
+    swish_y = over_y((swish_0, after(swish_1, qkv_y)))
+    (gate_home,) = columns_out(after(gate_mine, qkv_y), [gate_mine.shape[1]])
+    (up_home,) = columns_out(after(up_mine, gate_home), [up_mine.shape[1]])
+    swish_mine = half_hi(after(swish_y, qkv_mine))
+    down_home = rows_out(after(down_mine, up_home))
+    out_home = rows_out(after(out_mine, down_home))
+    query_home, key_home, value_home = columns_out(
+        after(qkv_mine, up_home), [key_size, key_size, value_size]
+    )
+    (swish_home,) = columns_out(after(swish_mine, query_home), [value_size])
 
     def own_head(grad):
         full = jnp.zeros((keys_all,) + grad.shape[1:], F32)
@@ -595,14 +647,14 @@
     half = pair[0] + swap(pair[1], "y")
     if lax.axis_size("hi") == 2:
         first = lax.axis_index("hi") == 0
-        low, high = half[:HEADS], half[HEADS:]
-        mine = jnp.where(first, low, high) + swap(jnp.where(first, high, low), "hi")
+        one, two = half[:HEADS], half[HEADS:]
+        mine = jnp.where(first, one, two) + swap(jnp.where(first, two, one), "hi")
     else:
         mine = lax.psum_scatter(half, "hi", scatter_dimension=0, tiled=True)
     parts = natural([mine[n] for n in range(HEADS)])
     mine = parts[0]
-    for r in range(1, HEADS):
-        mine = mine + to_partner(parts[r], r)
+    for got in partners(parts[1:]):
+        mine = mine + got
     mine = mine.reshape(-1)
     homes, place = [], 0
     for size in sizes:

time: 925 us -> 798 us (0.86)
  starting transfers between devices: 272 us -> 134 us
  other arithmetic: 92.4 us -> 68.6 us
  local copies, waits for them, and re-layouts: 25.8 us -> 47.6 us
  between operations: 3.88 us -> 16.4 us
    ppermute x63 -> x32, waiting for transfers between devices: 262 us -> 129 us  [swap(): return lax.ppermute(value, axis, [(0, 1), (1, 0)])]
    ppermute x66 -> x54, waiting for transfers between devices: 105 us -> 222 us  [partners(): lax.ppermute(v, 't', [(s, s ^ r + 1) for s in range(HEADS)])]
    ppermute x66 -> x54, starting transfers between devices: 135 us -> 54.3 us  [partners(): lax.ppermute(v, 't', [(s, s ^ r + 1) for s in range(HEADS)])]
    ppermute x63 -> x32, starting transfers between devices: 108 us -> 59.4 us  [swap(): return lax.ppermute(value, axis, [(0, 1), (1, 0)])]
    ppermute x2, waiting for transfers between devices: 0.01 us -> 35.8 us  [rows_out(): lax.ppermute(part, WAYS, [(b, a) for a, b in row_pairs()]).astype(F32)]
    concatenate x2 -> x1, other arithmetic: 22 us -> 0.02 us  [both_cores(): return jnp.concatenate(out)]
    ppermute x2, waiting for transfers between devices: 20.9 us -> 4.98 us  [rows_in(): return lax.ppermute(weight, WAYS, row_pairs())]
    unnamed x313 -> x223, local copies, waits for them, and re-layouts: 15 us -> 21.6 us
  transfers between devices with their start and end apart: 135 -> 97, of which waited for: 48 -> 45; matrix products, arithmetic and copies ran while one was open for 16% -> 22% of each run, Pallas kernels for 3% -> 3%
where the time goes in v3:
time: 798 us; the launch traced here: 785 us
  waiting for transfers between devices  401 us (50%)
  starting transfers between devices  134 us (17%)
  matrix products  94.6 us (12%)
  other arithmetic  68.6 us (9%)
  local copies, waits for them, and re-layouts  47.6 us (6%)
  Pallas kernels  23.4 us (3%)
  between operations  16.4 us (2%)
    ppermute x54, waiting for transfers between devices, partners(): lax.ppermute(v, 't', [(s, s ^ r + 1) for s in range(HEADS)])  222 us
    ppermute x32, waiting for transfers between devices, swap(): return lax.ppermute(value, axis, [(0, 1), (1, 0)])  129 us
    ppermute x32, starting transfers between devices, swap(): return lax.ppermute(value, axis, [(0, 1), (1, 0)])  59.4 us
    ppermute x54, starting transfers between devices, partners(): lax.ppermute(v, 't', [(s, s ^ r + 1) for s in range(HEADS)])  54.3 us
    ppermute x2, waiting for transfers between devices, rows_out(): lax.ppermute(part, WAYS, [(b, a) for a, b in row_pairs()]).astype(F32)  35.8 us
    dot_general x14, matrix products, dot_tn(): lax.dot_general(a, b, (((0,), (0,)), ((), ())), precision=precision, pref...  34.7 us
    dot_general x8, matrix products, dot_nt(): lax.dot_general(a, b, (((1,), (1,)), ((), ())), precision=precision, pref...  32.7 us
    dot_general x8, matrix products, dot(): return jnp.dot(a, b, precision=precision, preferred_element_type=F32)  27.3 us
  transfers between devices with their start and end apart: 97, of which 45 were waited for; matrix products, arithmetic and copies ran while one was open for 22% of the time, Pallas kernels for 3%

profile of v3, /device:TPU:5, one launch (start us, length us, event | category | flops | bytes accessed | tf_op | source)
XLA Modules:
  0.0 785.1 jit_solution(6087585005848435699)
XLA Ops:
  9.0 2.8 concatenate.121
  31.1 4.6 collective-permute-done.8
  37.9 10.0 %collective-permute-done.7 = bf16[256,768]{1,0:T(8,128)(2,1)S(1)} collective-permute-done((bf16[256,768]{1,0:T(8,128)(2,1)S(1)}, bf16[256,768]{1,0:T(8,128)(2,1)S(1)}, u32[]{:S(2)}, u32[]{:S(2)}) %collective-permute-start.7) | collective-permute-done | bytes 393248 | tf_op jit(solution)/shard_map/ppermute | solution.py:28
  52.2 15.3 %collective-permute-done.13 = bf16[256,768]{1,0:T(8,128)(2,1)S(1)} collective-permute-done((bf16[256,768]{1,0:T(8,128)(2,1)S(1)}, bf16[256,768]{1,0:T(8,128)(2,1)S(1)}, u32[]{:S(2)}, u32[]{:S(2)}) %collective-permute-start.13) | collective-permute-done | bytes 393248 | tf_op jit(solution)/shard_map/ppermute | solution.py:28
  67.5 2.6 collective-permute-start.17
  70.2 11.3 %collective-permute-done.15 = bf16[128,2048]{1,0:T(8,128)(2,1)S(1)} collective-permute-done((bf16[128,2048]{1,0:T(8,128)(2,1)S(1)}, bf16[128,2048]{1,0:T(8,128)(2,1)S(1)}, u32[]{:S(2)}, u32[]{:S(2)}) %collective-permute-start.15) | collective-permute-done | bytes 524320 | tf_op jit(solution)/shard_map/ppermute | solution.py:33
  83.2 5.0 collective-permute-done.17
  90.9 4.5 collective-permute-done.25
  104.0 3.9 collective-permute-done.28
  107.9 3.1 collective-permute-done.29
  121.0 13.6 %collective-permute-start.20 = (bf16[512,768]{1,0:T(8,128)(2,1)S(1)}, bf16[512,768]{1,0:T(8,128)(2,1)}, u32[]{:S(2)}, u32[]{:S(2)}) collective-permute-start(bf16[512,768]{1,0:T(8,128)(2,1)S(1)} %pad_maximum_fusion.10), channel_id=1, source_target_pairs={{0,16},{16,0},{1,17},{17,1},{2,18},{18,2},{3,19},{19,3},{4,20},{20... | collective-permute-start | bytes 2359304 | tf_op jit(solution)/shard_map/ppermute | solution.py:28
  137.3 4.6 collective-permute-start.31
  143.5 38.8 %collective-permute-done.21 = bf16[64,2048]{1,0:T(8,128)(2,1)S(1)} collective-permute-done((bf16[64,2048]{1,0:T(8,128)(2,1)}, bf16[64,2048]{1,0:T(8,128)(2,1)S(1)}, u32[]{:S(2)}, u32[]{:S(2)}) %collective-permute-start.21) | collective-permute-done | bytes 262176 | tf_op jit(solution)/shard_map/ppermute | solution.py:28
  190.4 4.7 shard_map.279
  195.1 28.3 %collective-permute-start.24 = (bf16[1024,768]{1,0:T(8,128)(2,1)S(1)}, bf16[1024,768]{1,0:T(8,128)(2,1)S(1)}, u32[]{:S(2)}, u32[]{:S(2)}) collective-permute-start(bf16[1024,768]{1,0:T(8,128)(2,1)S(1)} %pad_maximum_fusion.7), channel_id=1, source_target_pairs={{0,8},{8,0},{1,9},{9,1},{2,10},{10,2},{3,11},{11,3},{4,12},{12,4},... | collective-permute-start | bytes 4718600 | tf_op jit(solution)/shard_map/ppermute | solution.py:28
  225.7 11.6 %collective-permute-done.23 = bf16[128,2048]{1,0:T(8,128)(2,1)S(1)} collective-permute-done((bf16[128,2048]{1,0:T(8,128)(2,1)S(1)}, bf16[128,2048]{1,0:T(8,128)(2,1)S(1)}, u32[]{:S(2)}, u32[]{:S(2)}) %collective-permute-start.23) | collective-permute-done | bytes 524320 | tf_op jit(solution)/shard_map/ppermute | solution.py:28
  243.9 6.3 shard_map.280
  250.2 3.1 broadcast_select_fusion.37
  256.0 3.7 collective-permute-start.35
  264.6 15.6 %collective-permute-done.35 = bf16[128,2048]{1,0:T(8,128)(2,1)} collective-permute-done((bf16[128,2048]{1,0:T(8,128)(2,1)}, bf16[128,2048]{1,0:T(8,128)(2,1)}, u32[]{:S(2)}, u32[]{:S(2)}) %collective-permute-start.35) | collective-permute-done | bytes 524320 | tf_op jit(solution)/shard_map/ppermute | solution.py:33
  282.2 14.5 %collective-permute-done.34 = bf16[128,2048]{1,0:T(8,128)(2,1)} collective-permute-done((bf16[128,2048]{1,0:T(8,128)(2,1)}, bf16[128,2048]{1,0:T(8,128)(2,1)}, u32[]{:S(2)}, u32[]{:S(2)}) %collective-permute-start.34) | collective-permute-done | bytes 524320 | tf_op jit(solution)/shard_map/ppermute | solution.py:33
  303.1 12.6 %collective-permute-done.40 = bf16[128,2048]{1,0:T(8,128)(2,1)} collective-permute-done((bf16[128,2048]{1,0:T(8,128)(2,1)}, bf16[128,2048]{1,0:T(8,128)(2,1)}, u32[]{:S(2)}, u32[]{:S(2)}) %collective-permute-start.40) | collective-permute-done | bytes 524320 | tf_op jit(solution)/shard_map/ppermute | solution.py:33
  316.8 15.2 %collective-permute-done.41 = bf16[128,2048]{1,0:T(8,128)(2,1)S(1)} collective-permute-done((bf16[128,2048]{1,0:T(8,128)(2,1)}, bf16[128,2048]{1,0:T(8,128)(2,1)S(1)}, u32[]{:S(2)}, u32[]{:S(2)}) %collective-permute-start.41) | collective-permute-done | bytes 524320 | tf_op jit(solution)/shard_map/ppermute | solution.py:33
  332.1 22.3 %collective-permute-done.38 = bf16[128,2048]{1,0:T(8,128)(2,1)S(1)} collective-permute-done((bf16[128,2048]{1,0:T(8,128)(2,1)S(1)}, bf16[128,2048]{1,0:T(8,128)(2,1)S(1)}, u32[]{:S(2)}, u32[]{:S(2)}) %collective-permute-start.38) | collective-permute-done | bytes 524320 | tf_op jit(solution)/shard_map/ppermute | solution.py:33
  354.4 10.4 %collective-permute-done.37 = bf16[128,2048]{1,0:T(8,128)(2,1)S(1)} collective-permute-done((bf16[128,2048]{1,0:T(8,128)(2,1)S(1)}, bf16[128,2048]{1,0:T(8,128)(2,1)S(1)}, u32[]{:S(2)}, u32[]{:S(2)}) %collective-permute-start.37) | collective-permute-done | bytes 524320 | tf_op jit(solution)/shard_map/ppermute | solution.py:33
  365.5 8.3 %fusion.44 = f32[512,1408]{1,0:T(8,128)} fusion(bf16[2048,1408]{1,0:T(8,128)(2,1)} %all-gather.4.cloned.1.call-done, bf16[128,2048]{1,0:T(8,128)(2,1)} %copy-done.91, bf16[128,2048]{1,0:T(8,128)(2,1)} %copy-done.94, bf16[128,2048]{1,0:T(8,128)(2,1)} %collective-permute-done.36, bf16[128,2048]{1,0:T(8,128)(2,1)} %copy-done.71), kind=kOutput, calls=%fused_computation.358 | convolution fusion | flops 2961178624 | bytes 10747904 | tf_op jit(solution)/shard_map/dot_general | solution.py:174
  373.9 8.3 %fusion.43 = f32[512,1408]{1,0:T(8,128)} fusion(bf16[2048,1408]{1,0:T(8,128)(2,1)} %all-gather.6.cloned.1.call-done, bf16[128,2048]{1,0:T(8,128)(2,1)} %copy-done.91, bf16[128,2048]{1,0:T(8,128)(2,1)} %copy-done.94, bf16[128,2048]{1,0:T(8,128)(2,1)} %collective-permute-done.36, bf16[128,2048]{1,0:T(8,128)(2,1)} %copy-done.71), kind=kOutput, calls=%fused_computation.357 | convolution fusion | flops 2961178624 | bytes 10747904 | tf_op jit(solution)/shard_map/dot_general | solution.py:174
  382.2 10.9 %multiply_convert_fusion = (bf16[512,1408]{1,0:T(8,128)(2,1)}, bf16[512,1408]{1,0:T(8,128)(2,1)S(1)}, bf16[512,1408]{1,0:T(8,128)(2,1)}) fusion(f32[512,1408]{1,0:T(8,128)} %fusion.44, f32[512,1408]{1,0:T(8,128)} %fusion.43, bf16[512,2048]{1,0:T(8,128)(2,1)} %copy-done.78, bf16[1408,2048]{1,0:T(8,128)(2,1)} %all-gather.8.cloned.1.call-done), kind=kOutput, calls=%fused_computation.20 | convolution fusion | flops 2963603456 | bytes 17956864 | tf_op jit(solution)/shard_map/dot_general | solution.py:178
  394.3 7.5 convolution_convert_fusion.1
  401.8 5.2 convolution_convert_fusion.2
  411.7 5.9 fusion.59
  417.6 3.9 add_convert_fusion
  424.0 2.4 collective-permute-start.43
  426.7 7.1 convolution_convert_fusion
  433.8 7.9 %collective-permute-done.44 = bf16[128,2048]{1,0:T(8,128)(2,1)} collective-permute-done((bf16[128,2048]{1,0:T(8,128)(2,1)}, bf16[128,2048]{1,0:T(8,128)(2,1)}, u32[]{:S(2)}, u32[]{:S(2)}) %collective-permute-start.44) | collective-permute-done | bytes 524320 | tf_op jit(solution)/shard_map/ppermute | solution.py:33
  441.7 23.1 %collective-permute-done.43 = bf16[128,2048]{1,0:T(8,128)(2,1)} collective-permute-done((bf16[128,2048]{1,0:T(8,128)(2,1)}, bf16[128,2048]{1,0:T(8,128)(2,1)}, u32[]{:S(2)}, u32[]{:S(2)}) %collective-permute-start.43) | collective-permute-done | bytes 524320 | tf_op jit(solution)/shard_map/ppermute | solution.py:33
  466.7 7.7 add_convert_fusion.2
  484.3 15.3 %collective-permute-done.49 = bf16[128,2048]{1,0:T(8,128)(2,1)} collective-permute-done((bf16[128,2048]{1,0:T(8,128)(2,1)}, bf16[128,2048]{1,0:T(8,128)(2,1)}, u32[]{:S(2)}, u32[]{:S(2)}) %collective-permute-start.49) | collective-permute-done | bytes 524320 | tf_op jit(solution)/shard_map/ppermute | solution.py:33
  499.5 9.3 %collective-permute-done.48 = bf16[128,2048]{1,0:T(8,128)(2,1)} collective-permute-done((bf16[128,2048]{1,0:T(8,128)(2,1)}, bf16[128,2048]{1,0:T(8,128)(2,1)}, u32[]{:S(2)}, u32[]{:S(2)}) %collective-permute-start.48) | collective-permute-done | bytes 524320 | tf_op jit(solution)/shard_map/ppermute | solution.py:33
  510.7 3.2 add_convert_fusion.1
  516.6 5.0 shard_map.281
  529.7 3.9 convolution_convert_fusion.5
  541.8 2.5 add_convert_fusion.11
  544.2 9.4 %collective-permute-done.54.out_ref = bf16[512,256]{1,0:T(8,128)(2,1)S(1)} collective-permute-done((bf16[512,256]{1,0:T(8,128)(2,1)}, bf16[512,256]{1,0:T(8,128)(2,1)S(1)}, u32[]{:S(2)}, u32[]{:S(2)}) %collective-permute-start.54) | collective-permute-done | bytes 262176 | tf_op jit(solution)/shard_map/ppermute | solution.py:424
  553.6 7.4 shard_map.282
  565.1 11.6 %collective-permute-done.61 = bf16[128,2048]{1,0:T(8,128)(2,1)S(1)} collective-permute-done((bf16[128,2048]{1,0:T(8,128)(2,1)S(1)}, bf16[128,2048]{1,0:T(8,128)(2,1)S(1)}, u32[]{:S(2)}, u32[]{:S(2)}) %collective-permute-start.61) | collective-permute-done | bytes 524320 | tf_op jit(solution)/shard_map/ppermute | solution.py:28
  576.8 28.5 %collective-permute-done.66 = bf16[176,2048]{1,0:T(8,128)(2,1)S(1)} collective-permute-done((bf16[176,2048]{1,0:T(8,128)(2,1)S(1)}, bf16[176,2048]{1,0:T(8,128)(2,1)S(1)}, u32[]{:S(2)}, u32[]{:S(2)}) %collective-permute-start.66) | collective-permute-done | bytes 720928 | tf_op jit(solution)/shard_map/ppermute | solution.py:28
  615.9 6.5 fusion.3
  634.6 6.0 collective-permute-done.64
  641.0 10.9 %collective-permute-done.63 = bf16[128,2048]{1,0:T(8,128)(2,1)} collective-permute-done((bf16[128,2048]{1,0:T(8,128)(2,1)}, bf16[128,2048]{1,0:T(8,128)(2,1)}, u32[]{:S(2)}, u32[]{:S(2)}) %collective-permute-start.63) | collective-permute-done | bytes 524320 | tf_op jit(solution)/shard_map/ppermute | solution.py:33
  665.0 2.7 collective-permute-start.86
  667.8 3.9 collective-permute-done.86
  671.8 5.3 collective-permute-start.89
  677.1 3.6 collective-permute-done.52
  680.7 3.6 fusion.21
  687.5 5.4 collective-permute-done.68
  700.9 3.1 collective-permute-done.70
  707.3 3.0 collective-permute-start.73
  711.9 9.3 %collective-permute-done.73 = bf16[64,1408]{1,0:T(8,128)(2,1)S(1)} collective-permute-done((bf16[64,1408]{1,0:T(8,128)(2,1)S(1)}, bf16[64,1408]{1,0:T(8,128)(2,1)S(1)}, u32[]{:S(2)}, u32[]{:S(2)}) %collective-permute-start.73) | collective-permute-done | bytes 180256 | tf_op jit(solution)/shard_map/ppermute | solution.py:33
  722.7 2.6 collective-permute-start.77
  725.4 6.8 collective-permute-start.90
  733.4 2.4 collective-permute-start.82
  737.4 17.5 %collective-permute-done.90 = bf16[176,2048]{1,0:T(8,128)(2,1)S(1)} collective-permute-done((bf16[176,2048]{1,0:T(8,128)(2,1)S(1)}, bf16[176,2048]{1,0:T(8,128)(2,1)S(1)}, u32[]{:S(2)}, u32[]{:S(2)}) %collective-permute-start.90) | collective-permute-done | bytes 720928 | tf_op jit(solution)/shard_map/ppermute | solution.py:127
  759.0 18.3 %collective-permute-done.91 = bf16[64,2048]{1,0:T(8,128)(2,1)S(1)} collective-permute-done((bf16[64,2048]{1,0:T(8,128)(2,1)S(1)}, bf16[64,2048]{1,0:T(8,128)(2,1)S(1)}, u32[]{:S(2)}, u32[]{:S(2)}) %collective-permute-start.91) | collective-permute-done | bytes 262176 | tf_op jit(solution)/shard_map/ppermute | solution.py:127
  (549 shorter events, 195.3 us)
Async XLA Ops:
  7.2 358.4 %all-gather.4.cloned.1.call-start = ((), (), s32[]{:S(2)}) async-start(), calls=%async_computation.2 | async-start | bytes 6488064 | tf_op jit(solution)/shard_map/all_gather | solution.py:496
  28.3 19.7 %collective-permute-start.7 = (bf16[256,768]{1,0:T(8,128)(2,1)S(1)}, bf16[256,768]{1,0:T(8,128)(2,1)S(1)}, u32[]{:S(2)}, u32[]{:S(2)}) collective-permute-start(bf16[256,768]{1,0:T(8,128)(2,1)S(1)} %pad_maximum_fusion.18), channel_id=1, source_target_pairs={{0,4},{4,0},{1,5},{5,1},{2,6},{6,2},{3,7},{7,3},{8,12},{12,8},{9,1... | collective-permute-start | bytes 1179656 | tf_op jit(solution)/shard_map/ppermute | solution.py:28
  48.1 19.4 %collective-permute-start.13 = (bf16[256,768]{1,0:T(8,128)(2,1)S(1)}, bf16[256,768]{1,0:T(8,128)(2,1)S(1)}, u32[]{:S(2)}, u32[]{:S(2)}) collective-permute-start(bf16[256,768]{1,0:T(8,128)(2,1)S(1)} %pad_maximum_fusion.19), channel_id=1, source_target_pairs={{0,4},{4,0},{1,5},{5,1},{2,6},{6,2},{3,7},{7,3},{8,12},{12,8},{9,1... | collective-permute-start | bytes 1179656 | tf_op jit(solution)/shard_map/ppermute | solution.py:28
  48.1 22.1 %collective-permute-start.16 = (bf16[128,2048]{1,0:T(8,128)(2,1)S(1)}, bf16[128,2048]{1,0:T(8,128)(2,1)S(1)}, u32[]{:S(2)}, u32[]{:S(2)}) collective-permute-start(bf16[128,2048]{1,0:T(8,128)(2,1)S(1)} %bitcast.75), channel_id=1, source_target_pairs={{0,3},{1,2},{2,1},{3,0},{4,7},{5,6},{6,5},{7,4},{8,11},{9,10},{10,... | collective-permute-start | bytes 1572872 | tf_op jit(solution)/shard_map/ppermute | solution.py:33
  49.6 31.9 %collective-permute-start.15 = (bf16[128,2048]{1,0:T(8,128)(2,1)S(1)}, bf16[128,2048]{1,0:T(8,128)(2,1)S(1)}, u32[]{:S(2)}, u32[]{:S(2)}) collective-permute-start(bf16[128,2048]{1,0:T(8,128)(2,1)S(1)} %bitcast.76), channel_id=1, source_target_pairs={{0,2},{1,3},{2,0},{3,1},{4,6},{5,7},{6,4},{7,5},{8,10},{9,11},{10,... | collective-permute-start | bytes 1572872 | tf_op jit(solution)/shard_map/ppermute | solution.py:33
  50.6 30.9 %collective-permute-start.14 = (bf16[128,2048]{1,0:T(8,128)(2,1)S(1)}, bf16[128,2048]{1,0:T(8,128)(2,1)S(1)}, u32[]{:S(2)}, u32[]{:S(2)}) collective-permute-start(bf16[128,2048]{1,0:T(8,128)(2,1)S(1)} %bitcast.77), channel_id=1, source_target_pairs={{0,1},{1,0},{2,3},{3,2},{4,5},{5,4},{6,7},{7,6},{8,9},{9,8},{10,11... | collective-permute-start | bytes 1572872 | tf_op jit(solution)/shard_map/ppermute | solution.py:33
  50.9 30.7 %collective-permute-start.12 = (bf16[512,768]{1,0:T(8,128)(2,1)S(1)}, bf16[512,768]{1,0:T(8,128)(2,1)S(1)}, u32[]{:S(2)}, u32[]{:S(2)}) collective-permute-start(bf16[512,768]{1,0:T(8,128)(2,1)S(1)} %pad_maximum_fusion.9), channel_id=1, source_target_pairs={{0,16},{16,0},{1,17},{17,1},{2,18},{18,2},{3,19},{19,3},{4,20},{20... | collective-permute-start | bytes 2359304 | tf_op jit(solution)/shard_map/ppermute | solution.py:28
  67.5 20.7 %collective-permute-start.17 = (bf16[64,2048]{1,0:T(8,128)(2,1)S(1)}, bf16[64,2048]{1,0:T(8,128)(2,1)S(1)}, u32[]{:S(2)}, u32[]{:S(2)}) collective-permute-start(bf16[64,2048]{1,0:T(8,128)(2,1)S(1)} %copy-done.97), channel_id=1, source_target_pairs={{0,0},{8,1},{16,2},{24,3},{1,4},{9,5},{17,6},{25,7},{2,8},{10,9},{... | collective-permute-start | bytes 786440 | tf_op jit(solution)/shard_map/ppermute | solution.py:123
  100.0 273.9 %all-gather.6.cloned.1.call-start = ((), (), s32[]{:S(2)}) async-start(), calls=%async_computation.3 | async-start | bytes 6488064 | tf_op jit(solution)/shard_map/all_gather | solution.py:499
  113.7 268.6 %all-gather.8.cloned.1.call-start = ((), (), s32[]{:S(2)}) async-start(), calls=%async_computation.4 | async-start | bytes 6488064 | tf_op jit(solution)/shard_map/all_gather | solution.py:501
  120.6 64.9 %collective-permute-start.19 = (bf16[1024,768]{1,0:T(8,128)(2,1)}, bf16[1024,768]{1,0:T(8,128)(2,1)}, u32[]{:S(2)}, u32[]{:S(2)}) collective-permute-start(bf16[1024,768]{1,0:T(8,128)(2,1)} %pad_maximum_fusion.6), channel_id=1, source_target_pairs={{0,8},{8,0},{1,9},{9,1},{2,10},{10,2},{3,11},{11,3},{4,12},{12,4},... | collective-permute-start | bytes 4718600 | tf_op jit(solution)/shard_map/ppermute | solution.py:28
  121.0 63.2 %collective-permute-start.20 = (bf16[512,768]{1,0:T(8,128)(2,1)S(1)}, bf16[512,768]{1,0:T(8,128)(2,1)}, u32[]{:S(2)}, u32[]{:S(2)}) collective-permute-start(bf16[512,768]{1,0:T(8,128)(2,1)S(1)} %pad_maximum_fusion.10), channel_id=1, source_target_pairs={{0,16},{16,0},{1,17},{17,1},{2,18},{18,2},{3,19},{19,3},{4,20},{20... | collective-permute-start | bytes 2359304 | tf_op jit(solution)/shard_map/ppermute | solution.py:28
  134.5 47.8 %collective-permute-start.21 = (bf16[64,2048]{1,0:T(8,128)(2,1)}, bf16[64,2048]{1,0:T(8,128)(2,1)S(1)}, u32[]{:S(2)}, u32[]{:S(2)}) collective-permute-start(bf16[64,2048]{1,0:T(8,128)(2,1)} %copy-done.75), channel_id=1, source_target_pairs={{0,4},{4,0},{1,5},{5,1},{2,6},{6,2},{3,7},{7,3},{8,12},{12,8},{9,1... | collective-permute-start | bytes 786440 | tf_op jit(solution)/shard_map/ppermute | solution.py:28
  137.3 45.9 %collective-permute-start.31 = (bf16[176,2048]{1,0:T(8,128)(2,1)S(1)}, bf16[176,2048]{1,0:T(8,128)(2,1)S(1)}, u32[]{:S(2)}, u32[]{:S(2)}) collective-permute-start(bf16[176,2048]{1,0:T(8,128)(2,1)S(1)} %copy-done.90), channel_id=1, source_target_pairs={{0,0},{8,1},{16,2},{24,3},{1,4},{9,5},{17,6},{25,7},{2,8},{10,9},{... | collective-permute-start | bytes 2162696 | tf_op jit(solution)/shard_map/ppermute | solution.py:123
  184.1 510.1 %reduce-scatter.5.cloned.1.call-start = ((), (), s32[]{:S(2)}) async-start(), calls=%async_computation.6 | async-start | bytes 6488064 | tf_op jit(solution)/shard_map/reduce_scatter | solution.py:565
  195.1 43.4 %collective-permute-start.24 = (bf16[1024,768]{1,0:T(8,128)(2,1)S(1)}, bf16[1024,768]{1,0:T(8,128)(2,1)S(1)}, u32[]{:S(2)}, u32[]{:S(2)}) collective-permute-start(bf16[1024,768]{1,0:T(8,128)(2,1)S(1)} %pad_maximum_fusion.7), channel_id=1, source_target_pairs={{0,8},{8,0},{1,9},{9,1},{2,10},{10,2},{3,11},{11,3},{4,12},{12,4},... | collective-permute-start | bytes 4718600 | tf_op jit(solution)/shard_map/ppermute | solution.py:28
  223.4 13.9 %collective-permute-start.23 = (bf16[128,2048]{1,0:T(8,128)(2,1)S(1)}, bf16[128,2048]{1,0:T(8,128)(2,1)S(1)}, u32[]{:S(2)}, u32[]{:S(2)}) collective-permute-start(bf16[128,2048]{1,0:T(8,128)(2,1)S(1)} %copy-done.32), channel_id=1, source_target_pairs={{0,16},{16,0},{1,17},{17,1},{2,18},{18,2},{3,19},{19,3},{4,20},{20... | collective-permute-start | bytes 1572872 | tf_op jit(solution)/shard_map/ppermute | solution.py:28
  223.4 18.4 %collective-permute-start.22 = (bf16[512,256]{1,0:T(8,128)(2,1)S(1)}, bf16[512,256]{1,0:T(8,128)(2,1)S(1)}, u32[]{:S(2)}, u32[]{:S(2)}) collective-permute-start(bf16[512,256]{1,0:T(8,128)(2,1)S(1)} %get-tuple-element.109), channel_id=1, source_target_pairs={{0,4},{1,5},{2,6},{3,7},{8,12},{9,13},{10,14},{11,15},{16,20},{17,... | collective-permute-start | bytes 786440 | tf_op jit(solution)/shard_map/ppermute | solution.py:424
  256.0 24.1 %collective-permute-start.35 = (bf16[128,2048]{1,0:T(8,128)(2,1)}, bf16[128,2048]{1,0:T(8,128)(2,1)}, u32[]{:S(2)}, u32[]{:S(2)}) collective-permute-start(bf16[128,2048]{1,0:T(8,128)(2,1)} %get-tuple-element.245), channel_id=1, source_target_pairs={{0,3},{1,2},{2,1},{3,0},{4,7},{5,6},{6,5},{7,4},{8,11},{9,10},{10,... | collective-permute-start | bytes 1572872 | tf_op jit(solution)/shard_map/ppermute | solution.py:33
  259.7 37.0 %collective-permute-start.34 = (bf16[128,2048]{1,0:T(8,128)(2,1)}, bf16[128,2048]{1,0:T(8,128)(2,1)}, u32[]{:S(2)}, u32[]{:S(2)}) collective-permute-start(bf16[128,2048]{1,0:T(8,128)(2,1)} %get-tuple-element.246), channel_id=1, source_target_pairs={{0,2},{1,3},{2,0},{3,1},{4,6},{5,7},{6,4},{7,5},{8,10},{9,11},{10,... | collective-permute-start | bytes 1572872 | tf_op jit(solution)/shard_map/ppermute | solution.py:33
  259.7 37.0 %collective-permute-start.33 = (bf16[128,2048]{1,0:T(8,128)(2,1)}, bf16[128,2048]{1,0:T(8,128)(2,1)}, u32[]{:S(2)}, u32[]{:S(2)}) collective-permute-start(bf16[128,2048]{1,0:T(8,128)(2,1)} %get-tuple-element.244), channel_id=1, source_target_pairs={{0,1},{1,0},{2,3},{3,2},{4,5},{5,4},{6,7},{7,6},{8,9},{9,8},{10,11... | collective-permute-start | bytes 1572872 | tf_op jit(solution)/shard_map/ppermute | solution.py:33
  260.0 41.9 %collective-permute-start.39 = (bf16[128,2048]{1,0:T(8,128)(2,1)}, bf16[128,2048]{1,0:T(8,128)(2,1)}, u32[]{:S(2)}, u32[]{:S(2)}) collective-permute-start(bf16[128,2048]{1,0:T(8,128)(2,1)} %bitcast.2), channel_id=1, source_target_pairs={{0,1},{1,0},{2,3},{3,2},{4,5},{5,4},{6,7},{7,6},{8,9},{9,8},{10,11... | collective-permute-start | bytes 1572872 | tf_op jit(solution)/shard_map/ppermute | solution.py:33
  261.1 54.5 %collective-permute-start.40 = (bf16[128,2048]{1,0:T(8,128)(2,1)}, bf16[128,2048]{1,0:T(8,128)(2,1)}, u32[]{:S(2)}, u32[]{:S(2)}) collective-permute-start(bf16[128,2048]{1,0:T(8,128)(2,1)} %bitcast.2), channel_id=1, source_target_pairs={{0,2},{1,3},{2,0},{3,1},{4,6},{5,7},{6,4},{7,5},{8,10},{9,11},{10,... | collective-permute-start | bytes 1572872 | tf_op jit(solution)/shard_map/ppermute | solution.py:33
  280.2 51.8 %collective-permute-start.41 = (bf16[128,2048]{1,0:T(8,128)(2,1)}, bf16[128,2048]{1,0:T(8,128)(2,1)S(1)}, u32[]{:S(2)}, u32[]{:S(2)}) collective-permute-start(bf16[128,2048]{1,0:T(8,128)(2,1)} %bitcast.2), channel_id=1, source_target_pairs={{0,3},{1,2},{2,1},{3,0},{4,7},{5,6},{6,5},{7,4},{8,11},{9,10},{10,... | collective-permute-start | bytes 1572872 | tf_op jit(solution)/shard_map/ppermute | solution.py:33
  299.3 55.1 %collective-permute-start.38 = (bf16[128,2048]{1,0:T(8,128)(2,1)S(1)}, bf16[128,2048]{1,0:T(8,128)(2,1)S(1)}, u32[]{:S(2)}, u32[]{:S(2)}) collective-permute-start(bf16[128,2048]{1,0:T(8,128)(2,1)S(1)} %multiply_convert_fusion.3), channel_id=1, source_target_pairs={{0,3},{1,2},{2,1},{3,0},{4,7},{5,6},{6,5},{7,4},{8,11},{9,10},{10,... | collective-permute-start | bytes 1572872 | tf_op jit(solution)/shard_map/ppermute | solution.py:33
  299.7 65.1 %collective-permute-start.37 = (bf16[128,2048]{1,0:T(8,128)(2,1)S(1)}, bf16[128,2048]{1,0:T(8,128)(2,1)S(1)}, u32[]{:S(2)}, u32[]{:S(2)}) collective-permute-start(bf16[128,2048]{1,0:T(8,128)(2,1)S(1)} %multiply_convert_fusion.3), channel_id=1, source_target_pairs={{0,2},{1,3},{2,0},{3,1},{4,6},{5,7},{6,4},{7,5},{8,10},{9,11},{10,... | collective-permute-start | bytes 1572872 | tf_op jit(solution)/shard_map/ppermute | solution.py:33
  301.9 63.7 %collective-permute-start.36 = (bf16[128,2048]{1,0:T(8,128)(2,1)S(1)}, bf16[128,2048]{1,0:T(8,128)(2,1)}, u32[]{:S(2)}, u32[]{:S(2)}) collective-permute-start(bf16[128,2048]{1,0:T(8,128)(2,1)S(1)} %multiply_convert_fusion.3), channel_id=1, source_target_pairs={{0,1},{1,0},{2,3},{3,2},{4,5},{5,4},{6,7},{7,6},{8,9},{9,8},{10,11... | collective-permute-start | bytes 1572872 | tf_op jit(solution)/shard_map/ppermute | solution.py:33
  401.8 303.5 %reduce-scatter.3.cloned.1.call-start = ((), (), s32[]{:S(2)}) async-start(), calls=%async_computation.5 | async-start | bytes 6488064 | tf_op jit(solution)/shard_map/reduce_scatter | solution.py:567
  410.5 56.2 %collective-permute-start.46 = (bf16[352,2048]{1,0:T(8,128)(2,1)}, bf16[352,2048]{1,0:T(8,128)(2,1)}, u32[]{:S(2)}, u32[]{:S(2)}) collective-permute-start(bf16[352,2048]{1,0:T(8,128)(2,1)} %get-tuple-element.212), channel_id=1, source_target_pairs={{0,8},{8,0},{1,9},{9,1},{2,10},{10,2},{3,11},{11,3},{4,12},{12,4},... | collective-permute-start | bytes 4325384 | tf_op jit(solution)/shard_map/ppermute | solution.py:28
  411.6 55.1 %collective-permute-start.45 = (bf16[352,2048]{1,0:T(8,128)(2,1)}, bf16[352,2048]{1,0:T(8,128)(2,1)}, u32[]{:S(2)}, u32[]{:S(2)}) collective-permute-start(bf16[352,2048]{1,0:T(8,128)(2,1)} %get-tuple-element.213), channel_id=1, source_target_pairs={{0,8},{8,0},{1,9},{9,1},{2,10},{10,2},{3,11},{11,3},{4,12},{12,4},... | collective-permute-start | bytes 4325384 | tf_op jit(solution)/shard_map/ppermute | solution.py:28
  424.0 17.7 %collective-permute-start.44 = (bf16[128,2048]{1,0:T(8,128)(2,1)}, bf16[128,2048]{1,0:T(8,128)(2,1)}, u32[]{:S(2)}, u32[]{:S(2)}) collective-permute-start(bf16[128,2048]{1,0:T(8,128)(2,1)} %get-tuple-element.242), channel_id=1, source_target_pairs={{0,3},{1,2},{2,1},{3,0},{4,7},{5,6},{6,5},{7,4},{8,11},{9,10},{10,... | collective-permute-start | bytes 1572872 | tf_op jit(solution)/shard_map/ppermute | solution.py:33
  424.0 40.8 %collective-permute-start.43 = (bf16[128,2048]{1,0:T(8,128)(2,1)}, bf16[128,2048]{1,0:T(8,128)(2,1)}, u32[]{:S(2)}, u32[]{:S(2)}) collective-permute-start(bf16[128,2048]{1,0:T(8,128)(2,1)} %get-tuple-element.243), channel_id=1, source_target_pairs={{0,2},{1,3},{2,0},{3,1},{4,6},{5,7},{6,4},{7,5},{8,10},{9,11},{10,... | collective-permute-start | bytes 1572872 | tf_op jit(solution)/shard_map/ppermute | solution.py:33
  426.5 38.3 %collective-permute-start.42 = (bf16[128,2048]{1,0:T(8,128)(2,1)}, bf16[128,2048]{1,0:T(8,128)(2,1)}, u32[]{:S(2)}, u32[]{:S(2)}) collective-permute-start(bf16[128,2048]{1,0:T(8,128)(2,1)} %get-tuple-element.241), channel_id=1, source_target_pairs={{0,1},{1,0},{2,3},{3,2},{4,5},{5,4},{6,7},{7,6},{8,9},{9,8},{10,11... | collective-permute-start | bytes 1572872 | tf_op jit(solution)/shard_map/ppermute | solution.py:33
  474.4 36.3 %collective-permute-start.50 = (bf16[352,2048]{1,0:T(8,128)(2,1)}, bf16[352,2048]{1,0:T(8,128)(2,1)}, u32[]{:S(2)}, u32[]{:S(2)}) collective-permute-start(bf16[352,2048]{1,0:T(8,128)(2,1)} %get-tuple-element.127), channel_id=1, source_target_pairs={{0,16},{16,0},{1,17},{17,1},{2,18},{18,2},{3,19},{19,3},{4,20},{20... | collective-permute-start | bytes 4325384 | tf_op jit(solution)/shard_map/ppermute | solution.py:28
  479.0 20.6 %collective-permute-start.49 = (bf16[128,2048]{1,0:T(8,128)(2,1)}, bf16[128,2048]{1,0:T(8,128)(2,1)}, u32[]{:S(2)}, u32[]{:S(2)}) collective-permute-start(bf16[128,2048]{1,0:T(8,128)(2,1)} %fusion.42), channel_id=1, source_target_pairs={{0,3},{1,2},{2,1},{3,0},{4,7},{5,6},{6,5},{7,4},{8,11},{9,10},{10,... | collective-permute-start | bytes 1572872 | tf_op jit(solution)/shard_map/ppermute | solution.py:33
  479.0 29.8 %collective-permute-start.48 = (bf16[128,2048]{1,0:T(8,128)(2,1)}, bf16[128,2048]{1,0:T(8,128)(2,1)}, u32[]{:S(2)}, u32[]{:S(2)}) collective-permute-start(bf16[128,2048]{1,0:T(8,128)(2,1)} %fusion.42), channel_id=1, source_target_pairs={{0,2},{1,3},{2,0},{3,1},{4,6},{5,7},{6,4},{7,5},{8,10},{9,11},{10,... | collective-permute-start | bytes 1572872 | tf_op jit(solution)/shard_map/ppermute | solution.py:33
  479.9 28.9 %collective-permute-start.47 = (bf16[128,2048]{1,0:T(8,128)(2,1)}, bf16[128,2048]{1,0:T(8,128)(2,1)}, u32[]{:S(2)}, u32[]{:S(2)}) collective-permute-start(bf16[128,2048]{1,0:T(8,128)(2,1)} %fusion.42), channel_id=1, source_target_pairs={{0,1},{1,0},{2,3},{3,2},{4,5},{5,4},{6,7},{7,6},{8,9},{9,8},{10,11... | collective-permute-start | bytes 1572872 | tf_op jit(solution)/shard_map/ppermute | solution.py:33
  524.2 29.3 %collective-permute-start.54 = (bf16[512,256]{1,0:T(8,128)(2,1)}, bf16[512,256]{1,0:T(8,128)(2,1)S(1)}, u32[]{:S(2)}, u32[]{:S(2)}) collective-permute-start(bf16[512,256]{1,0:T(8,128)(2,1)} %get-tuple-element.130), channel_id=1, source_target_pairs={{4,0},{5,1},{6,2},{7,3},{12,8},{13,9},{14,10},{15,11},{20,16},{21,... | collective-permute-start | bytes 786440 | tf_op jit(solution)/shard_map/ppermute | solution.py:424
  526.8 13.0 %collective-permute-start.56 = (bf16[128,2048]{1,0:T(8,128)(2,1)}, bf16[128,2048]{1,0:T(8,128)(2,1)}, u32[]{:S(2)}, u32[]{:S(2)}) collective-permute-start(bf16[128,2048]{1,0:T(8,128)(2,1)} %get-tuple-element.236), channel_id=1, source_target_pairs={{0,8},{8,0},{1,9},{9,1},{2,10},{10,2},{3,11},{11,3},{4,12},{12,4},... | collective-permute-start | bytes 1572872 | tf_op jit(solution)/shard_map/ppermute | solution.py:28
  529.2 10.7 %collective-permute-start.55 = (bf16[128,2048]{1,0:T(8,128)(2,1)}, bf16[128,2048]{1,0:T(8,128)(2,1)}, u32[]{:S(2)}, u32[]{:S(2)}) collective-permute-start(bf16[128,2048]{1,0:T(8,128)(2,1)} %get-tuple-element.237), channel_id=1, source_target_pairs={{0,8},{8,0},{1,9},{9,1},{2,10},{10,2},{3,11},{11,3},{4,12},{12,4},... | collective-permute-start | bytes 1572872 | tf_op jit(solution)/shard_map/ppermute | solution.py:28
  529.7 12.1 %collective-permute-start.58 = (bf16[512,512]{1,0:T(8,128)(2,1)}, bf16[512,512]{1,0:T(8,128)(2,1)}, u32[]{:S(2)}, u32[]{:S(2)}) collective-permute-start(bf16[512,512]{1,0:T(8,128)(2,1)} %convolution_convert_fusion.9), channel_id=1, source_target_pairs={{0,8},{8,0},{1,9},{9,1},{2,10},{10,2},{3,11},{11,3},{4,12},{12,4},... | collective-permute-start | bytes 1572872 | tf_op jit(solution)/shard_map/ppermute | solution.py:28
  562.9 43.6 %collective-permute-start.59 = (bf16[512,1024]{1,0:T(8,128)(2,1)S(1)}, bf16[512,1024]{1,0:T(8,128)(2,1)S(1)}, u32[]{:S(2)}, u32[]{:S(2)}) collective-permute-start(bf16[512,1024]{1,0:T(8,128)(2,1)S(1)} %convolution_convert_fusion.7), channel_id=1, source_target_pairs={{0,8},{8,0},{1,9},{9,1},{2,10},{10,2},{3,11},{11,3},{4,12},{12,4},... | collective-permute-start | bytes 3145736 | tf_op jit(solution)/shard_map/ppermute | solution.py:28
  563.3 13.4 %collective-permute-start.61 = (bf16[128,2048]{1,0:T(8,128)(2,1)S(1)}, bf16[128,2048]{1,0:T(8,128)(2,1)S(1)}, u32[]{:S(2)}, u32[]{:S(2)}) collective-permute-start(bf16[128,2048]{1,0:T(8,128)(2,1)S(1)} %get-tuple-element.141), channel_id=1, source_target_pairs={{0,16},{16,0},{1,17},{17,1},{2,18},{18,2},{3,19},{19,3},{4,20},{20... | collective-permute-start | bytes 1572872 | tf_op jit(solution)/shard_map/ppermute | solution.py:28
  563.6 41.7 %collective-permute-start.66 = (bf16[176,2048]{1,0:T(8,128)(2,1)S(1)}, bf16[176,2048]{1,0:T(8,128)(2,1)S(1)}, u32[]{:S(2)}, u32[]{:S(2)}) collective-permute-start(bf16[176,2048]{1,0:T(8,128)(2,1)S(1)} %broadcast_select_fusion.18), channel_id=1, source_target_pairs={{0,4},{4,0},{1,5},{5,1},{2,6},{6,2},{3,7},{7,3},{8,12},{12,8},{9,1... | collective-permute-start | bytes 2162696 | tf_op jit(solution)/shard_map/ppermute | solution.py:28
  564.5 43.8 %collective-permute-start.60 = (bf16[512,1024]{1,0:T(8,128)(2,1)S(1)}, bf16[512,1024]{1,0:T(8,128)(2,1)S(1)}, u32[]{:S(2)}, u32[]{:S(2)}) collective-permute-start(bf16[512,1024]{1,0:T(8,128)(2,1)S(1)} %convolution_convert_fusion.6), channel_id=1, source_target_pairs={{0,8},{8,0},{1,9},{9,1},{2,10},{10,2},{3,11},{11,3},{4,12},{12,4},... | collective-permute-start | bytes 3145736 | tf_op jit(solution)/shard_map/ppermute | solution.py:28
  615.8 17.1 %collective-permute-start.67 = (bf16[64,2048]{1,0:T(8,128)(2,1)}, bf16[64,2048]{1,0:T(8,128)(2,1)S(1)}, u32[]{:S(2)}, u32[]{:S(2)}) collective-permute-start(bf16[64,2048]{1,0:T(8,128)(2,1)} %broadcast_select_fusion.45), channel_id=1, source_target_pairs={{0,4},{4,0},{1,5},{5,1},{2,6},{6,2},{3,7},{7,3},{8,12},{12,8},{9,1... | collective-permute-start | bytes 786440 | tf_op jit(solution)/shard_map/ppermute | solution.py:28
  626.1 14.6 %collective-permute-start.64 = (bf16[128,2048]{1,0:T(8,128)(2,1)}, bf16[128,2048]{1,0:T(8,128)(2,1)}, u32[]{:S(2)}, u32[]{:S(2)}) collective-permute-start(bf16[128,2048]{1,0:T(8,128)(2,1)} %get-tuple-element.228), channel_id=1, source_target_pairs={{0,3},{1,2},{2,1},{3,0},{4,7},{5,6},{6,5},{7,4},{8,11},{9,10},{10,... | collective-permute-start | bytes 1572872 | tf_op jit(solution)/shard_map/ppermute | solution.py:33
  626.2 25.7 %collective-permute-start.63 = (bf16[128,2048]{1,0:T(8,128)(2,1)}, bf16[128,2048]{1,0:T(8,128)(2,1)}, u32[]{:S(2)}, u32[]{:S(2)}) collective-permute-start(bf16[128,2048]{1,0:T(8,128)(2,1)} %get-tuple-element.229), channel_id=1, source_target_pairs={{0,2},{1,3},{2,0},{3,1},{4,6},{5,7},{6,4},{7,5},{8,10},{9,11},{10,... | collective-permute-start | bytes 1572872 | tf_op jit(solution)/shard_map/ppermute | solution.py:33
  628.5 24.5 %collective-permute-start.62 = (bf16[128,2048]{1,0:T(8,128)(2,1)}, bf16[128,2048]{1,0:T(8,128)(2,1)}, u32[]{:S(2)}, u32[]{:S(2)}) collective-permute-start(bf16[128,2048]{1,0:T(8,128)(2,1)} %get-tuple-element.227), channel_id=1, source_target_pairs={{0,1},{1,0},{2,3},{3,2},{4,5},{5,4},{6,7},{7,6},{8,9},{9,8},{10,11... | collective-permute-start | bytes 1572872 | tf_op jit(solution)/shard_map/ppermute | solution.py:33
  628.8 26.1 %collective-permute-start.65 = (bf16[512,1024]{1,0:T(8,128)(2,1)}, bf16[512,1024]{1,0:T(8,128)(2,1)}, u32[]{:S(2)}, u32[]{:S(2)}) collective-permute-start(bf16[512,1024]{1,0:T(8,128)(2,1)} %add_convert_fusion.5), channel_id=1, source_target_pairs={{0,16},{16,0},{1,17},{17,1},{2,18},{18,2},{3,19},{19,3},{4,20},{20... | collective-permute-start | bytes 3145736 | tf_op jit(solution)/shard_map/ppermute | solution.py:28
  632.9 38.9 %collective-permute-start.53 = (bf16[128,2048]{1,0:T(8,128)(2,1)}, bf16[128,2048]{1,0:T(8,128)(2,1)}, u32[]{:S(2)}, u32[]{:S(2)}) collective-permute-start(bf16[128,2048]{1,0:T(8,128)(2,1)} %get-tuple-element.239), channel_id=1, source_target_pairs={{0,3},{1,2},{2,1},{3,0},{4,7},{5,6},{6,5},{7,4},{8,11},{9,10},{10,... | collective-permute-start | bytes 1572872 | tf_op jit(solution)/shard_map/ppermute | solution.py:33
  640.6 40.0 %collective-permute-start.52 = (bf16[128,2048]{1,0:T(8,128)(2,1)}, bf16[128,2048]{1,0:T(8,128)(2,1)}, u32[]{:S(2)}, u32[]{:S(2)}) collective-permute-start(bf16[128,2048]{1,0:T(8,128)(2,1)} %get-tuple-element.240), channel_id=1, source_target_pairs={{0,2},{1,3},{2,0},{3,1},{4,6},{5,7},{6,4},{7,5},{8,10},{9,11},{10,... | collective-permute-start | bytes 1572872 | tf_op jit(solution)/shard_map/ppermute | solution.py:33
  651.9 28.8 %collective-permute-start.51 = (bf16[128,2048]{1,0:T(8,128)(2,1)}, bf16[128,2048]{1,0:T(8,128)(2,1)}, u32[]{:S(2)}, u32[]{:S(2)}) collective-permute-start(bf16[128,2048]{1,0:T(8,128)(2,1)} %get-tuple-element.238), channel_id=1, source_target_pairs={{0,1},{1,0},{2,3},{3,2},{4,5},{5,4},{6,7},{7,6},{8,9},{9,8},{10,11... | collective-permute-start | bytes 1572872 | tf_op jit(solution)/shard_map/ppermute | solution.py:33
  667.7 25.1 %collective-permute-start.68 = (bf16[256,1024]{1,0:T(8,128)(2,1)}, bf16[256,1024]{1,0:T(8,128)(2,1)}, u32[]{:S(2)}, u32[]{:S(2)}) collective-permute-start(bf16[256,1024]{1,0:T(8,128)(2,1)} %broadcast_select_fusion.19), channel_id=1, source_target_pairs={{0,4},{4,0},{1,5},{5,1},{2,6},{6,2},{3,7},{7,3},{8,12},{12,8},{9,1... | collective-permute-start | bytes 1572872 | tf_op jit(solution)/shard_map/ppermute | solution.py:28
  671.8 26.5 %collective-permute-start.78 = (bf16[512,512]{1,0:T(8,128)(2,1)}, bf16[512,512]{1,0:T(8,128)(2,1)}, u32[]{:S(2)}, u32[]{:S(2)}) collective-permute-start(bf16[512,512]{1,0:T(8,128)(2,1)} %add_convert_fusion.11), channel_id=1, source_target_pairs={{0,16},{16,0},{1,17},{17,1},{2,18},{18,2},{3,19},{19,3},{4,20},{20... | collective-permute-start | bytes 1572872 | tf_op jit(solution)/shard_map/ppermute | solution.py:28
  671.8 12.6 %collective-permute-start.89 = (f32[8,256]{1,0:T(8,128)S(1)}, f32[8,256]{1,0:T(8,128)S(1)}, u32[]{:S(2)}, u32[]{:S(2)}) collective-permute-start(f32[8,256]{1,0:T(8,128)S(1)} %get-tuple-element.361), channel_id=1, source_target_pairs={{0,3},{1,2},{2,1},{3,0},{4,7},{5,6},{6,5},{7,4},{8,11},{9,10},{10,... | collective-permute-start | bytes 24584 | tf_op jit(solution)/shard_map/ppermute | solution.py:33
  707.3 13.8 %collective-permute-start.73 = (bf16[64,1408]{1,0:T(8,128)(2,1)S(1)}, bf16[64,1408]{1,0:T(8,128)(2,1)S(1)}, u32[]{:S(2)}, u32[]{:S(2)}) collective-permute-start(bf16[64,1408]{1,0:T(8,128)(2,1)S(1)} %get-tuple-element.281), channel_id=1, source_target_pairs={{0,2},{1,3},{2,0},{3,1},{4,6},{5,7},{6,4},{7,5},{8,10},{9,11},{10,... | collective-permute-start | bytes 540680 | tf_op jit(solution)/shard_map/ppermute | solution.py:33
  710.4 10.8 %collective-permute-start.74 = (bf16[64,1408]{1,0:T(8,128)(2,1)S(1)}, bf16[64,1408]{1,0:T(8,128)(2,1)S(1)}, u32[]{:S(2)}, u32[]{:S(2)}) collective-permute-start(bf16[64,1408]{1,0:T(8,128)(2,1)S(1)} %get-tuple-element.279), channel_id=1, source_target_pairs={{0,1},{1,0},{2,3},{3,2},{4,5},{5,4},{6,7},{7,6},{8,9},{9,8},{10,11... | collective-permute-start | bytes 540680 | tf_op jit(solution)/shard_map/ppermute | solution.py:33
  710.4 14.9 %collective-permute-start.79 = (bf16[256,512]{1,0:T(8,128)(2,1)S(1)}, bf16[256,512]{1,0:T(8,128)(2,1)S(1)}, u32[]{:S(2)}, u32[]{:S(2)}) collective-permute-start(bf16[256,512]{1,0:T(8,128)(2,1)S(1)} %broadcast_select_fusion.44), channel_id=1, source_target_pairs={{0,4},{4,0},{1,5},{5,1},{2,6},{6,2},{3,7},{7,3},{8,12},{12,8},{9,1... | collective-permute-start | bytes 786440 | tf_op jit(solution)/shard_map/ppermute | solution.py:28
  725.4 29.5 %collective-permute-start.90 = (bf16[176,2048]{1,0:T(8,128)(2,1)S(1)}, bf16[176,2048]{1,0:T(8,128)(2,1)S(1)}, u32[]{:S(2)}, u32[]{:S(2)}) collective-permute-start(bf16[176,2048]{1,0:T(8,128)(2,1)S(1)} %copy-done.56), channel_id=1, source_target_pairs={{0,0},{1,8},{2,16},{3,24},{4,1},{5,9},{6,17},{7,25},{8,2},{9,10},{... | collective-permute-start | bytes 2162696 | tf_op jit(solution)/shard_map/ppermute | solution.py:127
  733.1 25.0 %collective-permute-start.80 = (bf16[64,512]{1,0:T(8,128)(2,1)S(1)}, bf16[64,512]{1,0:T(8,128)(2,1)S(1)}, u32[]{:S(2)}, u32[]{:S(2)}) collective-permute-start(bf16[64,512]{1,0:T(8,128)(2,1)S(1)} %get-tuple-element.327), channel_id=1, source_target_pairs={{0,3},{1,2},{2,1},{3,0},{4,7},{5,6},{6,5},{7,4},{8,11},{9,10},{10,... | collective-permute-start | bytes 196616 | tf_op jit(solution)/shard_map/ppermute | solution.py:33
  733.2 24.9 %collective-permute-start.81 = (bf16[64,512]{1,0:T(8,128)(2,1)S(1)}, bf16[64,512]{1,0:T(8,128)(2,1)S(1)}, u32[]{:S(2)}, u32[]{:S(2)}) collective-permute-start(bf16[64,512]{1,0:T(8,128)(2,1)S(1)} %get-tuple-element.184), channel_id=1, source_target_pairs={{0,2},{1,3},{2,0},{3,1},{4,6},{5,7},{6,4},{7,5},{8,10},{9,11},{10,... | collective-permute-start | bytes 196616 | tf_op jit(solution)/shard_map/ppermute | solution.py:33
  733.4 24.7 %collective-permute-start.82 = (bf16[64,512]{1,0:T(8,128)(2,1)S(1)}, bf16[64,512]{1,0:T(8,128)(2,1)S(1)}, u32[]{:S(2)}, u32[]{:S(2)}) collective-permute-start(bf16[64,512]{1,0:T(8,128)(2,1)S(1)} %get-tuple-element.326), channel_id=1, source_target_pairs={{0,1},{1,0},{2,3},{3,2},{4,5},{5,4},{6,7},{7,6},{8,9},{9,8},{10,11... | collective-permute-start | bytes 196616 | tf_op jit(solution)/shard_map/ppermute | solution.py:33
  756.2 21.1 %collective-permute-start.91 = (bf16[64,2048]{1,0:T(8,128)(2,1)S(1)}, bf16[64,2048]{1,0:T(8,128)(2,1)S(1)}, u32[]{:S(2)}, u32[]{:S(2)}) collective-permute-start(bf16[64,2048]{1,0:T(8,128)(2,1)S(1)} %copy-done.74), channel_id=1, source_target_pairs={{0,0},{1,8},{2,16},{3,24},{4,1},{5,9},{6,17},{7,25},{8,2},{9,10},{... | collective-permute-start | bytes 786440 | tf_op jit(solution)/shard_map/ppermute | solution.py:127
  (139 other events, 1281.2 us)
Sparse Core Ops, SparseCore 0:
  100.1 109.7 all-gather.3
  212.3 75.8 all-gather.5
  290.1 65.5 all-gather.7
  401.9 88.8 reduce-scatter.4
  494.5 115.3 reduce-scatter.2

commit v4 on v3

--- a/solution.py
+++ b/solution.py
@@ -3,6 +3,7 @@
 import jax
 import jax.numpy as jnp
 from jax import lax
+from jax.experimental.layout import Layout, with_layout_constraint
 from jax.experimental import pallas as pl
 from jax.experimental.pallas import tpu as pltpu
 from jax.sharding import Mesh, PartitionSpec as P
@@ -13,15 +14,26 @@
 F32 = jnp.float32
 BF16 = jnp.bfloat16
 EXACT = lax.Precision.HIGHEST
+SMALL = pl.CostEstimate(flops=1, transcendentals=0, bytes_accessed=1)
 WAYS = ("y", "core", "hi", "t")
 
 
 def after(value, *others):
+    if not others:
+        return value
     return lax.optimization_barrier((value,) + others)[0]
+
+
+def meet(*values):
+    return lax.optimization_barrier(values)
 
 
 def all_after(values, *others):
     return lax.optimization_barrier(tuple(values) + others)[: len(values)]
+
+
+def by_rows_in_memory(value):
+    return with_layout_constraint(value, Layout(tuple(range(value.ndim))))
 
 
 def swap(value, axis):
@@ -49,29 +61,40 @@
     )
 
 
-def gather_rows(value):
-    return jnp.concatenate((value,) + partners((value,) * 3))
-
-
-def scatter_rows(value):
+def gather_rows(value, until=()):
+    return jnp.concatenate((after(value, *until),) + partners((value,) * 3))
+
+
+def scatter_rows(value, until=()):
     rows = value.shape[0] // HEADS
     parts = [value[r * rows : (r + 1) * rows] for r in range(HEADS)]
-    total = parts[0].astype(F32)
+    total = after(parts[0], *until).astype(F32)
     for got in partners(parts[1:]):
         total = total + got.astype(F32)
     return total
 
 
-def both(value, axis):
+def over_t(value):
+    t = lax.axis_index("t")
+    for bit in (1, 2):
+        other = lax.ppermute(value, "t", [(n, n ^ bit) for n in range(HEADS)])
+        first = (t & bit) == 0
+        value = jnp.concatenate([jnp.where(first, value, other), jnp.where(first, other, value)])
+    return value
+
+
+def both(value, axis, until=()):
     if lax.axis_size(axis) != 2:
         return lax.all_gather(value, axis, axis=0, tiled=True)
     other = swap(value, axis)
+    value = after(value, *until)
     first = lax.axis_index(axis) == 0
     return jnp.concatenate([jnp.where(first, value, other), jnp.where(first, other, value)])
 
 
-def both_cores(value):
+def both_cores(value, until=()):
     other = swap(value, "core")
+    value = after(value, *until)
     first = lax.axis_index("core") == 0
     half = value.shape[0] // 2
     out = []
@@ -92,15 +115,16 @@
     return natural(four)
 
 
-def columns_in(sent, *others):
+def columns_in(sent, *others, until=()):
+    sent = [by_rows_in_memory(part) for part in sent]
     got = partners(all_after(sent[1:], *others))
-    return jnp.concatenate(natural((sent[0],) + got))
-
-
-def columns_out(part, widths):
+    return jnp.concatenate(natural((after(sent[0], *until),) + got))
+
+
+def columns_out(part, widths, until=()):
     own = part.shape[0] // HEADS
     sent = natural([part[n * own : (n + 1) * own] for n in range(HEADS)])
-    back = natural((sent[0],) + partners(sent[1:]))
+    back = natural((after(sent[0], *until),) + partners(sent[1:]))
     outs, place = [], 0
     for w in widths:
         outs.append(jnp.concatenate([b[:, place : place + w] for b in back], axis=1).astype(F32))
@@ -127,6 +151,94 @@
     return lax.ppermute(part, WAYS, [(b, a) for a, b in row_pairs()]).astype(F32)
 
 
+def whole_lanes(width):
+    return width + -width % 128
+
+
+def blocks_of(weights, width):
+    n_hi = lax.axis_size("hi")
+    four = []
+    for t in range(HEADS):
+        cols = []
+        for h in range(n_hi):
+            for w in weights:
+                for i in range(HEADS):
+                    start = ((i * n_hi + h) * HEADS + t) * width
+                    cols.append(w[:, start : start + width])
+                cols.append(jnp.zeros((w.shape[0], -HEADS * width % 128), w.dtype))
+        four.append(jnp.concatenate(cols, axis=1))
+    return natural(four)
+
+
+def blocks_back(part):
+    own = part.shape[0] // HEADS
+    sent = natural([part[n * own : (n + 1) * own] for n in range(HEADS)])
+    return natural((sent[0],) + partners(sent[1:]))
+
+
+def blocks_joined(back, width, count):
+    n_hi = lax.axis_size("hi")
+    outs = []
+    for k in range(count):
+        cols = []
+        for i in range(HEADS):
+            for h in range(n_hi):
+                for t in range(HEADS):
+                    start = (h * count + k) * whole_lanes(HEADS * width) + i * width
+                    cols.append(back[t][:, start : start + width])
+        outs.append(jnp.concatenate(cols, axis=1).astype(F32))
+    return outs
+
+
+def halves_in(value, until=()):
+    n_hi = lax.axis_size("hi")
+    width = value.shape[1] // n_hi
+    cols = [value[:, n * width : (n + 1) * width] for n in range(n_hi)]
+    if n_hi != 2:
+        return lax.all_to_all(jnp.stack(cols), "hi", 0, 0).reshape(-1, width)
+    first = lax.axis_index("hi") == 0
+    kept = jnp.where(first, cols[0], cols[1])
+    got = swap(jnp.where(first, cols[1], cols[0]), "hi")
+    kept = after(kept, *until)
+    return jnp.concatenate([jnp.where(first, kept, got), jnp.where(first, got, kept)])
+
+
+def halves_out(value):
+    n_hi = lax.axis_size("hi")
+    rows = value.shape[0] // n_hi
+    if n_hi != 2:
+        got = lax.all_to_all(value.reshape(n_hi, rows, -1), "hi", 0, 0)
+        return jnp.concatenate([got[n] for n in range(n_hi)], axis=1)
+    first = lax.axis_index("hi") == 0
+    low, high = value[:rows], value[rows:]
+    kept = jnp.where(first, low, high)
+    got = swap(jnp.where(first, high, low), "hi")
+    return jnp.concatenate(
+        [jnp.where(first, kept, got), jnp.where(first, got, kept)], axis=1
+    )
+
+
+def from_other(value):
+    n_hi = lax.axis_size("hi")
+    if n_hi == 2:
+        return swap(value, "hi")
+    turns = [[(s, (s + k) % n_hi) for s in range(n_hi)] for k in range(1, n_hi)]
+    return jnp.concatenate([lax.ppermute(value, "hi", turn) for turn in turns])
+
+
+def to_other(value):
+    n_hi = lax.axis_size("hi")
+    if n_hi == 2:
+        return swap(value, "hi").astype(F32)
+    rows = value.shape[0] // (n_hi - 1)
+    total = 0.0
+    for k in range(1, n_hi):
+        part = value[(k - 1) * rows : k * rows]
+        back = [((s + k) % n_hi, s) for s in range(n_hi)]
+        total = total + lax.ppermute(part, "hi", back).astype(F32)
+    return total
+
+
 def cell():
     return lax.axis_index("y") * 2 + lax.axis_index("core")
 
@@ -135,17 +247,18 @@
     return (a.astype(F32) + b.astype(F32)).astype(BF16)
 
 
-def half_hi(total):
+def half_hi(total, until=()):
     if lax.axis_size("hi") != 2:
         return lax.psum_scatter(total, "hi", scatter_dimension=0, tiled=True)
     first = lax.axis_index("hi") == 0
     n = total.shape[0] // 2
     low, high = total[:n], total[n:]
-    return add(jnp.where(first, low, high), swap(jnp.where(first, high, low), "hi"))
-
-
-def over_y(pair):
-    return add(pair[0], swap(pair[1], "y"))
+    kept, sent = jnp.where(first, low, high), jnp.where(first, high, low)
+    return add(after(kept, *until), swap(sent, "hi"))
+
+
+def over_y(pair, until=()):
+    return add(after(pair[0], *until), swap(pair[1], "y"))
 
 
 def rows_in_cells(value):
@@ -158,16 +271,19 @@
     return natural([value[:, i * n : (i + 1) * n] for i in range(HEADS)], cell())
 
 
-def by_columns(left, right):
-    sent = [swap(dot_tn(left[r], right).astype(BF16), "core") for r in (1, 3)]
-    return tuple(
-        (dot_tn(left[r], right) + got.astype(F32)).astype(BF16) for r, got in zip((0, 2), sent)
-    )
+def by_columns(cells, right):
+    theirs = jnp.concatenate([cells[1], cells[3]], axis=1)
+    mine = jnp.concatenate([cells[0], cells[2]], axis=1)
+    total = gradient(mine, right, swap(gradient(theirs, right), "core"))
+    half = total.shape[0] // 2
+    return total[:half], total[half:]
 
 
 def by_rows(left, right):
     cells = rows_in_cells(dot_tn(left, right).astype(BF16))
-    return tuple(add(cells[r], swap(cells[r + 1], "core")) for r in (0, 2))
+    got = swap(jnp.concatenate([cells[1], cells[3]]), "core")
+    half = cells[0].shape[0]
+    return add(cells[0], got[:half]), add(cells[2], got[half:])
 
 
 def dot(a, b, precision=None):
@@ -364,9 +480,7 @@
             ),
             out_shape=out_shape,
             compiler_params=params,
-            cost_estimate=pl.CostEstimate(
-                flops=flops, transcendentals=rows * k * 4, bytes_accessed=moved
-            ),
+            cost_estimate=SMALL,
         )
 
     unit = 2 * rows * k * v
@@ -410,6 +524,151 @@
         rows * (16 * k + 8 * v),
     )
     return state, forward, gate_back, backward
+
+
+def kernel_call(body, grid, ins, outs, out_shape):
+    return pl.pallas_call(
+        body,
+        grid=grid,
+        in_specs=ins,
+        out_specs=outs,
+        out_shape=out_shape,
+        compiler_params=pltpu.CompilerParams(
+            dimension_semantics=("arbitrary",), vmem_limit_bytes=50 * 1024 * 1024
+        ),
+        cost_estimate=SMALL,
+    )
+
+
+def whole_block(*shape):
+    return pl.BlockSpec(shape, lambda i: (0,) * len(shape), pipeline_mode=pl.Buffered(1))
+
+
+def row_block(rows, width):
+    return pl.BlockSpec((rows, width), lambda i: (i, 0))
+
+
+def column_block(rows, width):
+    return pl.BlockSpec((rows, width), lambda i: (0, i))
+
+
+def project(tokens, gain, weights, rank_in, rank_out, bias, key_size, value_size):
+    rows, width = tokens.shape
+    rank = rank_in.shape[1]
+    tile = 128
+    k, v = key_size, value_size
+
+    def body(
+        x_ref, gain_ref, w_ref, in_ref, out_ref, bias_ref,
+        normed_ref, inv_ref, key_ref, value_ref, query_ref, swish_ref, low_ref, ld_ref, slope_ref,
+    ):
+        x = x_ref[...].astype(F32)
+        inv = lax.rsqrt(jnp.mean(x * x, axis=-1, keepdims=True) + EPS)
+        inv_ref[...] = inv
+        normed = (x * inv * gain_ref[...]).astype(BF16)
+        normed_ref[...] = normed
+        key_ref[...] = dot(normed, w_ref[:, :k]).astype(BF16)
+        value_ref[...] = dot(normed, w_ref[:, k : k + v]).astype(BF16)
+        query_ref[...] = dot(normed, w_ref[:, k + v : 2 * k + v]).astype(BF16)
+        swish_ref[...] = dot(normed, w_ref[:, 2 * k + v :])
+        low = dot(normed, in_ref[...])
+        low_ref[...] = low
+        logits = dot_nt(low, out_ref[...], EXACT) + bias_ref[...]
+        small = jnp.exp(-jnp.abs(logits))
+        ld_ref[...] = (jnp.minimum(logits, 0.0) - jnp.log1p(small)) / 16.0
+        slope_ref[...] = jnp.where(logits > 0, small, 1.0) / (1.0 + small) / 16.0
+
+    def out(n, kind):
+        return jax.ShapeDtypeStruct((rows, n), kind)
+
+    widths = [(width, BF16), (1, F32), (k, BF16), (v, BF16), (k, BF16), (v, F32), (rank, F32)]
+    widths += [(k, F32), (k, F32)]
+    return kernel_call(
+        body,
+        (rows // tile,),
+        [
+            row_block(tile, width), whole_block(1, width), whole_block(width, 2 * (k + v)),
+            whole_block(width, rank), whole_block(k, rank), whole_block(1, k),
+        ],
+        [row_block(tile, n) for n, _ in widths],
+        [out(n, kind) for n, kind in widths],
+    )(tokens, gain, weights, rank_in, rank_out, bias)
+
+
+def feed(hidden, cot, weights, down):
+    rows, width = hidden.shape
+    lanes = down.shape[0]
+    tile = 512
+
+    def body(h_ref, c_ref, w_ref, d_ref, product_ref, back_ref, hnorm_ref, low_ref):
+        values = dot(h_ref[...], w_ref[...])
+        gate, up = values[:, :lanes], values[:, lanes:]
+        sig = 1.0 / (1.0 + jnp.exp(-gate))
+        silu = gate * sig
+        product = (silu * up).astype(BF16)
+        product_ref[...] = product
+        back = dot_nt(c_ref[...], d_ref[...])
+        back_ref[:, :lanes] = (back * up * (sig * (1.0 + gate * (1.0 - sig)))).astype(BF16)
+        back_ref[:, lanes:] = (back * silu).astype(BF16)
+        hnorm_ref[...] = dot_nt(back_ref[...], w_ref[...]).astype(BF16)
+        low_ref[...] = dot(product, d_ref[...]).astype(BF16)
+
+    widths = [lanes, 2 * lanes, width, width]
+    return kernel_call(
+        body,
+        (rows // tile,),
+        [
+            row_block(tile, width), row_block(tile, width), whole_block(*weights.shape),
+            whole_block(*down.shape),
+        ],
+        [row_block(tile, n) for n in widths],
+        [jax.ShapeDtypeStruct((rows, n), BF16) for n in widths],
+    )(hidden, cot, weights, down)
+
+
+def gradient(left, right, addend=None, rows=None):
+    depth, width = right.shape
+    rows = left.shape[1] if rows is None else rows
+    tile = 512 if rows % 512 == 0 else 256
+
+    def body(l_ref, r_ref, *refs):
+        total = dot_tn(l_ref[...], r_ref[...])
+        if addend is not None:
+            total = total + refs[0][...].astype(F32)
+        refs[-1][...] = total.astype(BF16)
+
+    more = [] if addend is None else [addend]
+    return kernel_call(
+        body,
+        (pl.cdiv(rows, tile),),
+        [column_block(depth, tile), whole_block(depth, width)] + [row_block(tile, width) for _ in more],
+        row_block(tile, width),
+        jax.ShapeDtypeStruct((rows, width), BF16),
+    )(left, right, *more)
+
+
+def back_to_norm(back, weights, back_rank, rank_in, tokens, inv):
+    rows, depth = back.shape
+    width = tokens.shape[1]
+    rank = rank_in.shape[1]
+    tile = 512
+
+    def body(b_ref, w_ref, br_ref, in_ref, x_ref, inv_ref, out_ref, gain_ref):
+        total = dot_nt(b_ref[...], w_ref[...]) + dot_nt(br_ref[...], in_ref[...])
+        out_ref[...] = total.astype(BF16)
+        unit = x_ref[...].astype(F32) * inv_ref[...]
+        gain_ref[...] = jnp.sum(total * unit, axis=0, keepdims=True)
+
+    return kernel_call(
+        body,
+        (width // tile,),
+        [
+            whole_block(rows, depth), row_block(tile, depth), whole_block(rows, rank),
+            row_block(tile, rank), column_block(rows, tile), whole_block(rows, 1),
+        ],
+        [column_block(rows, tile), column_block(1, tile)],
+        [jax.ShapeDtypeStruct((rows, width), BF16), jax.ShapeDtypeStruct((1, width), F32)],
+    )(back, weights, back_rank, rank_in, tokens, inv)
 
 
 def chain(local, total, upward):
@@ -473,37 +732,44 @@
     pad = -sum(sizes) % 1024
     packed = jnp.concatenate(small + (jnp.zeros((pad,), BF16),))
     packed = packed.reshape(1, 8, -1)
-    kv_cols = columns_of((key_proj, value_proj))
-    qs_cols = columns_of((query_proj, swish_proj))
-    gate_cols, up_cols = columns_of((gate_proj,)), columns_of((up_proj,))
-    across = ("y", "core", "hi")
-
-    packed = jnp.concatenate(natural((packed,) + partners((packed,) * 3)))
-    kv_in = columns_in(kv_cols, packed)
-    packed = both(packed, "hi")
-    kv_in, packed = lax.optimization_barrier((kv_in, packed))
-    kv_hi = both(kv_in, "hi")
-    qs_in = columns_in(qs_cols, kv_in)
-    packed = both(packed, "y")
-    out_in = rows_in(after(out_proj, qs_in))
-    kv_hi, qs_in, packed = lax.optimization_barrier((kv_hi, qs_in, packed))
-    packed = both_cores(packed).reshape(devices, -1)
-    kv_y, qs_hi = both(kv_hi, "y"), both(qs_in, "hi")
-    tokens_all = gather_rows(after(tokens[0], qs_in))
-    kv_y, qs_hi, tokens_all, out_in = lax.optimization_barrier((kv_y, qs_hi, tokens_all, out_in))
-    kv_full = both_cores(kv_y)
-    gate_in = columns_in(gate_cols, tokens_all)
-    gate_full = lax.all_gather(gate_in, across, axis=0, tiled=True)
-    qs_y, out_hi = both(qs_hi, "y"), both(out_in, "hi")
-    up_in = columns_in(up_cols, gate_in)
-    up_full = lax.all_gather(up_in, across, axis=0, tiled=True)
-    down_in = rows_in(after(down_proj, up_in))
-    down_full = lax.all_gather(down_in, across, axis=0, tiled=True)
+    kvqs_cols = columns_of((key_proj, value_proj, query_proj, swish_proj))
+    block = down_proj.shape[0]
+    gate_up_cols = blocks_of((gate_proj, up_proj), block)
+    across, pair = ("y", "core", "hi"), ("y", "core")
+
+    kvqs_in = columns_in(kvqs_cols)
+    out_in = rows_in(out_proj)
+    out_in = jnp.concatenate(
+        [out_in[:, n * value_size : (n + 1) * value_size] for n in range(HEADS)]
+    )
+    attn_in = by_rows_in_memory(jnp.concatenate([kvqs_in, out_in], axis=1))
+    attn_in, packed, local_tokens = meet(attn_in, packed, tokens[0])
+
+    attn_full = lax.all_gather(attn_in, across, axis=0, tiled=True)
+    tokens_all = gather_rows(local_tokens)
+    packed = both_cores(both(both(over_t(packed), "hi"), "y")).reshape(devices, -1)
+    tokens_all, local_cot = meet(tokens_all, cotangent[0])
+    cot_own = gather_rows(local_cot)
+    attn_full, tokens_all, cot_own, packed, *gate_up_cols = meet(
+        attn_full, tokens_all, cot_own, packed, *gate_up_cols
+    )
+
+    gate_up_in = columns_in(gate_up_cols)
+    cot_other = from_other(after(cotangent[0], tokens_all))
+    kvqs_width = kvqs_in.shape[1]
+    out_full = attn_full[:, kvqs_width:].reshape(-1, HEADS, out_proj.shape[0], value_size)
+    out_full = jnp.concatenate(
+        [out_full[:, n].reshape(value_size, value_size) for n in range(HEADS)], axis=1
+    )
+    down_full = jnp.pad(
+        lax.all_gather(down_proj, pair, axis=0, tiled=True),
+        ((0, -HEADS * block % 128), (0, 0)),
+    )
     got, place = [], 0
     for size in sizes:
         got.append(packed[:, place : place + size].reshape(-1))
         place += size
-    attn_full, mlp_full, head_full, bias_full = [g.astype(F32) for g in got[:4]]
+    attngain_full, mlp_full, head_full, bias_full = [g.astype(F32) for g in got[:4]]
     rankin_full = got[4].reshape(width, rank)
     rankout_own = lax.dynamic_slice_in_dim(
         got[5].reshape(keys_all, rank), t * key_size, key_size, 0
@@ -512,123 +778,98 @@
 
     residual = tokens[0].astype(F32)
 
-    wide_all = tokens_all.astype(F32)
-    unit_all = wide_all * inverse(wide_all)
-    normed = (unit_all * attn_full).astype(BF16)
-    kv = dot(normed, kv_full)
-    key = kv[:, :key_size].astype(BF16)
-    value = kv[:, key_size:].astype(BF16)
-    low_rank = dot(normed, rankin_full)
-    logits = dot_nt(low_rank, rankout_own, EXACT) + bias_own
-    log_decay = jax.nn.log_sigmoid(logits) / 16.0
-    decay_slope = jax.nn.sigmoid(-logits) / 16.0
+    each = HEADS * block
+    lanes = whole_lanes(each)
+    n_hi = lax.axis_size("hi")
+    normed, inv_all, key, value, query, swish_in, low_rank, log_decay, decay_slope = project(
+        tokens_all, attngain_full.reshape(1, width), attn_full, rankin_full, rankout_own,
+        bias_own.reshape(1, key_size), key_size, value_size,
+    )
     state_call, forward_call, gate_back_call, backward_call = recurrence_calls(
         rows, local, key_size, value_size
     )
     where = t.reshape(1).astype(jnp.int32)
     end_state, end_log = state_call(where, key, value, log_decay)
-    end_state, qs_y, out_hi = lax.optimization_barrier((end_state, qs_y, out_hi))
+    end_state, cot_other, gate_up_in = meet(end_state, cot_other, gate_up_in)
+
     in_state = chain(end_state, end_log, True)
-    out_y = both(out_hi, "y")
-    qs_full = both_cores(qs_y)
-    qs = dot(normed, qs_full)
-    query = qs[:, :key_size].astype(BF16)
-    swish_in = qs[:, key_size:]
-    in_state, out_y, query, swish_in, down_in = lax.optimization_barrier(
-        (in_state, out_y, query, swish_in, down_in)
-    )
-    out_full = both_cores(out_y)
+    cot_other = gather_rows(cot_other)
+    in_state, cot_other, gate_up_in, out_full = meet(in_state, cot_other, gate_up_in, out_full)
+
+    gate_up_in = halves_in(gate_up_in)
     gain_row = head_full.reshape(1, value_size)
     gated, mixed, saved = forward_call(
         where, query, key, value, log_decay, swish_in, gain_row, in_state
     )
     attended = scatter_rows(dot(gated, out_full).astype(BF16))
+    attended, gate_up_in = meet(attended, gate_up_in)
+    gate_up_full = lax.all_gather(gate_up_in, pair, axis=0, tiled=True)
+
     hidden = residual + attended
-
     hidden_norm = (hidden * inverse(hidden) * mlp_full).astype(BF16)
-    hidden_all = gather_rows(hidden_norm)
-    cot_all = gather_rows(after(cotangent[0], hidden_all))
-    gate_val = dot(hidden_all, gate_full)
-    up_val = dot(hidden_all, up_full)
-    sig = jax.nn.sigmoid(gate_val)
-    silu = gate_val * sig
-    product = (silu * up_val).astype(BF16)
-
-    back_product = dot_nt(cot_all, down_full)
-    back_gate = (back_product * up_val * (sig * (1.0 + gate_val * (1.0 - sig)))).astype(BF16)
-    back_up = (back_product * silu).astype(BF16)
-    back_hnorm = (dot_nt(back_gate, gate_full) + dot_nt(back_up, up_full)).astype(BF16)
-
+    hidden_other, hidden_own = from_other(hidden_norm), gather_rows(hidden_norm)
+    hidden_other = gather_rows(after(hidden_other, hidden_own))
+    hidden_all = jnp.concatenate([hidden_own, hidden_other])
+    cot_all = jnp.concatenate([cot_own, cot_other])
+    product, back_gate_up, back_hnorm, out_low = feed(
+        hidden_all, cot_all, gate_up_full, down_full
+    )
+    back_hnorm, back_gate_up, product, out_low = meet(back_hnorm, back_gate_up, product, out_low)
+
+    other_sum = scatter_rows(back_hnorm[rows:]).astype(BF16)
+    other_sum, back_hnorm, product = meet(other_sum, back_hnorm, product)
+
+    own_sum, other_sum = scatter_rows(back_hnorm[:rows]), to_other(other_sum)
+    own_sum, other_sum, product = meet(own_sum, other_sum, product)
+
+    grad_down = gradient(product, cot_all, rows=each)
     normed_cells = columns_in_cells(normed)
-    back_hnorm_sum = scatter_rows(back_hnorm)
-    grad_gate = dot_tn(hidden_all, back_gate).astype(BF16)
-    gate_mine = lax.psum_scatter(grad_gate, across, scatter_dimension=0, tiled=True)
-    grad_up = dot_tn(hidden_all, back_up).astype(BF16)
-    up_mine = lax.psum_scatter(grad_up, across, scatter_dimension=0, tiled=True)
-    down_pair = by_rows(product, cot_all)
-    back_hnorm_sum, down_0, down_1, grad_gate, grad_up = lax.optimization_barrier(
-        (back_hnorm_sum,) + down_pair + (grad_gate, grad_up)
-    )
-    back_hidden, grad_mlpgain = norm_back(hidden, mlp_full, back_hnorm_sum)
+    back_hidden, grad_mlpgain = norm_back(hidden, mlp_full, own_sum + other_sum)
     back_hidden = back_hidden + cotangent[0].astype(F32)
 
-    down_y = over_y((down_0, down_1))
     back_attn = gather_rows(back_hidden.astype(BF16))
-    back_attn, down_y = lax.optimization_barrier((back_attn, down_y))
+    back_attn, out_low, grad_down = meet(back_attn, out_low, grad_down)
+    down_mine = lax.psum_scatter(grad_down, pair, scatter_dimension=0, tiled=True)
+
     back_gated = dot_nt(back_attn, out_full)
     back_mixed, back_swish, grad_headgain, direct = gate_back_call(
         where, back_gated, mixed, swish_in, gain_row, query, log_decay
     )
     out_state = chain(direct, end_log, False)
-    block_out = scatter_rows(dot(product, after(down_full, direct)).astype(BF16))
-    block_out = (hidden + block_out).astype(BF16)
-    swish_pair = by_columns(normed_cells, back_swish)
+    hidden_all, direct = meet(hidden_all, direct)
+    grad_gate_up = gradient(hidden_all, back_gate_up)
+    gate_up_mine = lax.psum_scatter(grad_gate_up, pair, scatter_dimension=0, tiled=True)
+    other_out = scatter_rows(out_low[rows:]).astype(BF16)
     out_pair = by_rows(gated, back_attn)
-    out_state, out_0, out_1, swish_0, swish_1, down_y = lax.optimization_barrier(
-        (out_state,) + out_pair + swish_pair + (down_y,)
-    )
-    down_mine = half_hi(down_y)
-    out_y = over_y((out_0, out_1))
+    out_state, out_low, other_out, out_0, out_1, grad_gate_up, down_mine = meet(
+        out_state, out_low, other_out, *out_pair, grad_gate_up, down_mine
+    )
+
     back_query, back_key, back_value, back_logits = backward_call(
         where, query, key, value, log_decay, decay_slope, back_mixed, saved, out_state
     )
-    back_qkv = jnp.concatenate([back_query, back_key, back_value], axis=1)
-    qkv_0, qkv_1 = by_columns(normed_cells, back_qkv)
-    qkv_0, qkv_1, out_y, back_qkv, back_logits = lax.optimization_barrier(
-        (qkv_0, qkv_1, out_y, back_qkv, back_logits)
-    )
-    qkv_y = over_y((qkv_0, qkv_1))
+    own_parts = [out_low[r * local : (r + 1) * local] for r in range(HEADS)]
+    own_got = partners(own_parts[1:])
+    back_kvqs = jnp.concatenate([back_key, back_value, back_query, back_swish], axis=1)
+    back_kvqs, own_first = meet(back_kvqs, own_got[0])
+    kvqs_pair = by_columns(normed_cells, back_kvqs)
     back_rank = dot(back_logits, rankout_own, EXACT)
-    back_query, back_kv = back_qkv[:, :key_size], back_qkv[:, key_size:]
-    back_qs = jnp.concatenate([back_query, back_swish], axis=1)
-    back_normed = (
-        dot_nt(back_kv, kv_full)
-        + dot_nt(back_qs, qs_full)
-        + dot_nt(back_rank.astype(BF16), rankin_full)
-    )
-    back_tokens = scatter_rows(back_normed.astype(BF16))
+    back_normed, grad_attngain = back_to_norm(
+        back_kvqs, attn_full, back_rank.astype(BF16), rankin_full, tokens_all, inv_all
+    )
+    grad_attngain = grad_attngain[0]
+    own_out = own_parts[0].astype(F32)
+    for got in (own_first,) + own_got[1:]:
+        own_out = own_out + got.astype(F32)
+    back_low, kvqs_0, kvqs_1, other_out, own_out, gate_up_mine, out_0, out_1 = meet(
+        back_normed, *kvqs_pair, other_out, own_out, gate_up_mine, out_0, out_1
+    )
+
+    back_tokens = scatter_rows(back_low)
+    kvqs_y, gate_up_out = over_y((kvqs_0, kvqs_1)), halves_out(gate_up_mine)
     grad_bias = jnp.sum(back_logits, axis=0)
     grad_rankout = dot_tn(back_logits, low_rank, EXACT)
     grad_rankin = dot_tn(normed, back_rank.astype(BF16))
-    grad_attngain = jnp.sum(back_normed * unit_all, axis=0)
-    out_mine = half_hi(after(out_y, down_mine))
-    back_tokens, qkv_y, down_mine, out_mine, grad_attngain = lax.optimization_barrier(
-        (back_tokens, qkv_y, down_mine, out_mine, grad_attngain)
-    )
-    back_tokens, _ = norm_back(residual, attn_full, back_tokens)
-    grad_tokens = (back_hidden + back_tokens).astype(BF16)
-
-    qkv_mine = half_hi(qkv_y)
-    swish_y = over_y((swish_0, after(swish_1, qkv_y)))
-    (gate_home,) = columns_out(after(gate_mine, qkv_y), [gate_mine.shape[1]])
-    (up_home,) = columns_out(after(up_mine, gate_home), [up_mine.shape[1]])
-    swish_mine = half_hi(after(swish_y, qkv_mine))
-    down_home = rows_out(after(down_mine, up_home))
-    out_home = rows_out(after(out_mine, down_home))
-    query_home, key_home, value_home = columns_out(
-        after(qkv_mine, up_home), [key_size, key_size, value_size]
-    )
-    (swish_home,) = columns_out(after(swish_mine, query_home), [value_size])
 
     def own_head(grad):
         full = jnp.zeros((keys_all,) + grad.shape[1:], F32)
@@ -643,8 +884,28 @@
     )
     eighth = packed.shape[1] // 8
     cells = rows_in_cells(packed.reshape(devices, 8, eighth))
+    back_tokens, kvqs_y, other_out, gate_up_out, out_0, out_1, *cells = meet(
+        back_tokens, kvqs_y, other_out, gate_up_out, out_0, out_1, *cells
+    )
+
+    kvqs_mine, out_y = half_hi(kvqs_y), over_y((out_0, out_1))
+    gate_up_back = blocks_back(gate_up_out)
+    back_tokens, _ = norm_back(residual, attngain_full, back_tokens)
+    grad_tokens = (back_hidden + back_tokens).astype(BF16)
     pair = [cells[r] + swap(cells[r + 1], "core") for r in (0, 2)]
     half = pair[0] + swap(pair[1], "y")
+    gate_home, up_home = blocks_joined(gate_up_back, block, 2)
+    kvqs_mine, out_y, other_out, half, gate_home, up_home = meet(
+        kvqs_mine, out_y, other_out, half, gate_home, up_home
+    )
+
+    key_home, value_home, query_home, swish_home = columns_out(
+        kvqs_mine, [key_size, value_size, key_size, value_size]
+    )
+    block_out = (hidden + own_out + to_other(other_out)).astype(BF16)
+    out_home = rows_out(half_hi(out_y))
+    down_home = down_mine.astype(F32)
+
     if lax.axis_size("hi") == 2:
         first = lax.axis_index("hi") == 0
         one, two = half[:HEADS], half[HEADS:]

time: 798 us -> 712 us (0.89)
  matrix products: 94.6 us -> 14.3 us
  waiting for transfers between devices: 401 us -> 321 us
  Pallas kernels: 23.4 us -> 93.2 us
  starting transfers between devices: 134 us -> 150 us
  other arithmetic: 68.6 us -> 58.1 us
    ppermute x32 -> x19, waiting for transfers between devices: 129 us -> 46.2 us  [swap(): return lax.ppermute(value, axis, [(0, 1), (1, 0)])]
    pallas_call x0 -> x7, Pallas kernels: none -> 70.5 us  [the longest x1 27.3 us: feed(): kernel_call(body, (rows // tile,), [row_block(tile, width), row_block(til...]
    dot_general x8 -> x1, matrix products: 32.7 us -> 3.94 us  [dot_nt(): lax.dot_general(a, b, (((1,), (1,)), ((), ())), precision=precision, pref...]
    dot_general x14 -> x3, matrix products: 34.7 us -> 7.85 us  [dot_tn(): lax.dot_general(a, b, (((0,), (0,)), ((), ())), precision=precision, pref...]
    ppermute x54 -> x51, waiting for transfers between devices: 222 us -> 248 us  [partners(): lax.ppermute(v, 't', [(s, s ^ r + 1) for s in range(HEADS)])]
    dot_general x8 -> x2, matrix products: 27.3 us -> 2.47 us  [dot(): return jnp.dot(a, b, precision=precision, preferred_element_type=F32)]
    ppermute x2 -> x1, waiting for transfers between devices: 35.8 us -> 11.9 us  [rows_out(): lax.ppermute(part, WAYS, [(b, a) for a, b in row_pairs()]).astype(F32)]
    convert_element_type x10 -> x5, other arithmetic: 19.1 us -> 4.59 us  [add(): return (a.astype(F32) + b.astype(F32)).astype(BF16)]
  transfers between devices with their start and end apart: 97 -> 81, of which waited for: 45 -> 41; matrix products, arithmetic and copies ran while one was open for 22% -> 14% of each run, Pallas kernels for 3% -> 9%
where the time goes in v4:
time: 712 us; the launch traced here: 707 us
  waiting for transfers between devices  321 us (45%)
  starting transfers between devices  150 us (21%)
  Pallas kernels  93.2 us (13%)
  other arithmetic  58.1 us (8%)
  local copies, waits for them, and re-layouts  55.1 us (8%)
  between operations  15.4 us (2%)
  matrix products  14.3 us (2%)
    ppermute x51, waiting for transfers between devices, partners(): lax.ppermute(v, 't', [(s, s ^ r + 1) for s in range(HEADS)])  248 us
    ppermute x51, starting transfers between devices, partners(): lax.ppermute(v, 't', [(s, s ^ r + 1) for s in range(HEADS)])  57.6 us
    ppermute x19, starting transfers between devices, swap(): return lax.ppermute(value, axis, [(0, 1), (1, 0)])  56.6 us
    ppermute x19, waiting for transfers between devices, swap(): return lax.ppermute(value, axis, [(0, 1), (1, 0)])  46.2 us
    pallas_call x1, Pallas kernels, feed(): kernel_call(body, (rows // tile,), [row_block(tile, width), row_block(til...  27.3 us
    pallas_call x4, Pallas kernels, gradient(): kernel_call(body, (pl.cdiv(rows, tile),), [column_block(depth, tile), who...  24.7 us
    unnamed x135, local copies, waits for them, and re-layouts  15.8 us
  transfers between devices with their start and end apart: 81, of which 41 were waited for; matrix products, arithmetic and copies ran while one was open for 14% of the time, Pallas kernels for 9%

profile of v4, /device:TPU:5, one launch (start us, length us, event | category | flops | bytes accessed | tf_op | source)
XLA Modules:
  0.0 706.8 jit_solution(18290316786733049666)
XLA Ops:
  12.5 5.5 collective-permute-start.3
  22.2 7.2 %collective-permute-done.3 = bf16[64,2048]{1,0:T(8,128)(2,1)S(1)} collective-permute-done((bf16[64,2048]{1,0:T(8,128)(2,1)S(1)}, bf16[64,2048]{1,0:T(8,128)(2,1)S(1)}, u32[]{:S(2)}, u32[]{:S(2)}) %collective-permute-start.3) | collective-permute-done | bytes 262176 | tf_op jit(solution)/shard_map/ppermute | solution.py:147
  33.9 4.1 collective-permute-start.11
  39.0 5.9 collective-permute-start.12
  57.5 5.8 collective-permute-start.14
  65.1 14.2 %collective-permute-done.6 = bf16[128,2048]{1,0:T(8,128)(2,1)} collective-permute-done((bf16[128,2048]{1,0:T(8,128)(2,1)S(1)}, bf16[128,2048]{1,0:T(8,128)(2,1)}, u32[]{:S(2)}, u32[]{:S(2)}) %collective-permute-start.6) | collective-permute-done | bytes 524320 | tf_op jit(solution)/shard_map/ppermute | solution.py:45
  79.3 3.0 pad_maximum_fusion.x_ref
  82.2 2.6 collective-permute-start.7
  87.5 4.3 collective-permute-done.7
  91.8 13.7 %collective-permute-done.8 = bf16[128,2048]{1,0:T(8,128)(2,1)S(1)} collective-permute-done((bf16[128,2048]{1,0:T(8,128)(2,1)S(1)}, bf16[128,2048]{1,0:T(8,128)(2,1)S(1)}, u32[]{:S(2)}, u32[]{:S(2)}) %collective-permute-start.8) | collective-permute-done | bytes 524320 | tf_op jit(solution)/shard_map/ppermute | solution.py:45
  105.5 18.6 %collective-permute-done.9 = bf16[128,2048]{1,0:T(8,128)(2,1)} collective-permute-done((bf16[128,2048]{1,0:T(8,128)(2,1)S(1)}, bf16[128,2048]{1,0:T(8,128)(2,1)}, u32[]{:S(2)}, u32[]{:S(2)}) %collective-permute-start.9) | collective-permute-done | bytes 524320 | tf_op jit(solution)/shard_map/ppermute | solution.py:45
  126.7 3.2 all-gather.4.cloned.1.call-done.w_ref
  134.7 10.8 %shard_map.279 = (bf16[512,2048]{1,0:T(8,128)(2,1)}, f32[512,1]{1,0:T(8,128)S(1)}, bf16[512,256]{1,0:T(8,128)(2,1)S(1)}, bf16[512,512]{1,0:T(8,128)(2,1)S(1)}, b...) custom-call(bf16[512,2048]{1,0:T(8,128)(2,1)} %pad_maximum_fusion.x_, ...), custom_call_target="tpu_custom_call" | custom-call | flops 1 | bytes 1 | tf_op jit(solution)/shard_map/pallas_call | solution.py:586
  146.3 4.6 shard_map.280
  151.7 6.5 collective-permute-done.17
  163.7 2.9 collective-permute-start.19
  166.6 2.8 collective-permute-done.20
  169.4 12.1 %collective-permute-done.22 = bf16[128,2048]{1,0:T(8,128)(2,1)S(1)} collective-permute-done((bf16[128,2048]{1,0:T(8,128)(2,1)}, bf16[128,2048]{1,0:T(8,128)(2,1)S(1)}, u32[]{:S(2)}, u32[]{:S(2)}) %collective-permute-start.22) | collective-permute-done | bytes 524320 | tf_op jit(solution)/shard_map/ppermute | solution.py:45
  185.3 6.3 shard_map.281
  196.4 5.3 collective-permute-start.26
  202.5 28.9 %collective-permute-done.25 = bf16[128,2048]{1,0:T(8,128)(2,1)S(1)} collective-permute-done((bf16[128,2048]{1,0:T(8,128)(2,1)S(1)}, bf16[128,2048]{1,0:T(8,128)(2,1)S(1)}, u32[]{:S(2)}, u32[]{:S(2)}) %collective-permute-start.25) | collective-permute-done | bytes 524320 | tf_op jit(solution)/shard_map/ppermute | solution.py:45
  234.2 4.0 pad.4.d_ref
  241.2 4.3 collective-permute-start.28
  245.5 5.4 collective-permute-start.30
  252.7 9.2 %collective-permute-done.30 = bf16[128,2048]{1,0:T(8,128)(2,1)S(1)} collective-permute-done((bf16[128,2048]{1,0:T(8,128)(2,1)S(1)}, bf16[128,2048]{1,0:T(8,128)(2,1)S(1)}, u32[]{:S(2)}, u32[]{:S(2)}) %collective-permute-start.30) | collective-permute-done | bytes 524320 | tf_op jit(solution)/shard_map/ppermute | solution.py:40
  264.1 8.6 %collective-permute-start.32 = (bf16[128,2048]{1,0:T(8,128)(2,1)S(1)}, bf16[128,2048]{1,0:T(8,128)(2,1)S(1)}, u32[]{:S(2)}, u32[]{:S(2)}) collective-permute-start(bf16[128,2048]{1,0:T(8,128)(2,1)S(1)} %collective-permute-done.30), channel_id=1, source_target_pairs={{0,2},{1,3},{2,0},{3,1},{4,6},{5,7},{6,4},{7,5},{8,10},{9,11},{10,... | collective-permute-start | bytes 1572872 | tf_op jit(solution)/shard_map/ppermute | solution.py:45
  278.5 7.7 %collective-permute-done.32 = bf16[128,2048]{1,0:T(8,128)(2,1)S(1)} collective-permute-done((bf16[128,2048]{1,0:T(8,128)(2,1)S(1)}, bf16[128,2048]{1,0:T(8,128)(2,1)S(1)}, u32[]{:S(2)}, u32[]{:S(2)}) %collective-permute-start.32) | collective-permute-done | bytes 524320 | tf_op jit(solution)/shard_map/ppermute | solution.py:45
  287.1 11.4 %collective-permute-done.33 = bf16[128,2048]{1,0:T(8,128)(2,1)S(1)} collective-permute-done((bf16[128,2048]{1,0:T(8,128)(2,1)S(1)}, bf16[128,2048]{1,0:T(8,128)(2,1)S(1)}, u32[]{:S(2)}, u32[]{:S(2)}) %collective-permute-start.33) | collective-permute-done | bytes 524320 | tf_op jit(solution)/shard_map/ppermute | solution.py:45
  299.4 27.3 %shard_map.282 = (bf16[1024,768]{1,0:T(8,128)(2,1)S(1)}, bf16[1024,1536]{1,0:T(8,128)(2,1)}, bf16[1024,2048]{1,0:T(8,128)(2,1)}, bf16[1024,2048]{1,0:T(8,128)(2,1)}) custom-call(bf16[1024,2048]{1,0:T(8,128)(2,1)} %constant_dynamic-update-slice_fusion.h_ref.l_ref, bf16[1024,2048]{1,0:T(8,128)(2,1)} %copy-done.21, ...), custom_call_target="tpu_custom_call" | custom-call | flops 1 | bytes 1 | tf_op jit(solution)/shard_map/pallas_call | solution.py:617
  331.1 5.4 collective-permute-done.34
  336.6 11.8 %collective-permute-done.36 = bf16[128,2048]{1,0:T(8,128)(2,1)S(1)} collective-permute-done((bf16[128,2048]{1,0:T(8,128)(2,1)S(1)}, bf16[128,2048]{1,0:T(8,128)(2,1)S(1)}, u32[]{:S(2)}, u32[]{:S(2)}) %collective-permute-start.36) | collective-permute-done | bytes 524320 | tf_op jit(solution)/shard_map/ppermute | solution.py:45
  350.0 12.8 %collective-permute-start.40 = (bf16[128,2048]{1,0:T(8,128)(2,1)S(1)}, bf16[128,2048]{1,0:T(8,128)(2,1)S(1)}, u32[]{:S(2)}, u32[]{:S(2)}) collective-permute-start(bf16[128,2048]{1,0:T(8,128)(2,1)S(1)} %add_convert_fusion.7), channel_id=1, source_target_pairs={{0,4},{4,0},{1,5},{5,1},{2,6},{6,2},{3,7},{7,3},{8,12},{12,8},{9,1... | collective-permute-start | bytes 1572872 | tf_op jit(solution)/shard_map/ppermute | solution.py:40
  365.4 19.9 %collective-permute-done.40 = bf16[128,2048]{1,0:T(8,128)(2,1)S(1)} collective-permute-done((bf16[128,2048]{1,0:T(8,128)(2,1)S(1)}, bf16[128,2048]{1,0:T(8,128)(2,1)S(1)}, u32[]{:S(2)}, u32[]{:S(2)}) %collective-permute-start.40) | collective-permute-done | bytes 524320 | tf_op jit(solution)/shard_map/ppermute | solution.py:40
  385.4 9.2 %collective-permute-done.39 = bf16[128,2048]{1,0:T(8,128)(2,1)S(1)} collective-permute-done((bf16[128,2048]{1,0:T(8,128)(2,1)S(1)}, bf16[128,2048]{1,0:T(8,128)(2,1)S(1)}, u32[]{:S(2)}, u32[]{:S(2)}) %collective-permute-start.39) | collective-permute-done | bytes 524320 | tf_op jit(solution)/shard_map/ppermute | solution.py:45
  400.2 7.0 shard_map.283
  407.3 11.5 %collective-permute-done.43 = bf16[128,2048]{1,0:T(8,128)(2,1)} collective-permute-done((bf16[128,2048]{1,0:T(8,128)(2,1)}, bf16[128,2048]{1,0:T(8,128)(2,1)}, u32[]{:S(2)}, u32[]{:S(2)}) %collective-permute-start.43) | collective-permute-done | bytes 524320 | tf_op jit(solution)/shard_map/ppermute | solution.py:45
  418.8 3.1 pad_maximum_fusion.4
  421.9 12.4 %reduce-scatter.5.cloned.1.call-start = ((), (), s32[]{:S(2)}) async-start(), calls=%async_computation.6 | async-start | bytes 7864320 | tf_op jit(solution)/shard_map/reduce_scatter | solution.py:841
  434.4 3.9 fusion.46.bg_ref
  438.4 4.4 shard_map.284
  445.1 9.8 %shard_map.285 = bf16[2048,1536]{1,0:T(8,128)(2,1)} custom-call(bf16[1024,2048]{1,0:T(8,128)(2,1)} %constant_dynamic-update-slice_fusion.h_ref.l_ref, bf16[1024,1536]{1,0:T(8,128)(2,1)S(1)} %copy-done.2), custom_call_target="tpu_custom_call" | custom-call | flops 1 | bytes 1 | tf_op jit(solution)/shard_map/pallas_call | solution.py:641
  455.9 2.9 convolution_convert_fusion
  459.0 5.5 collective-permute-start.48
  468.7 7.6 %collective-permute-done.45 = bf16[128,2048]{1,0:T(8,128)(2,1)S(1)} collective-permute-done((bf16[128,2048]{1,0:T(8,128)(2,1)S(1)}, bf16[128,2048]{1,0:T(8,128)(2,1)S(1)}, u32[]{:S(2)}, u32[]{:S(2)}) %collective-permute-start.45) | collective-permute-done | bytes 524320 | tf_op jit(solution)/shard_map/ppermute | solution.py:45
  476.3 5.5 collective-permute-done.46
  481.8 12.2 %collective-permute-done.47 = bf16[128,2048]{1,0:T(8,128)(2,1)S(1)} collective-permute-done((bf16[128,2048]{1,0:T(8,128)(2,1)S(1)}, bf16[128,2048]{1,0:T(8,128)(2,1)S(1)}, u32[]{:S(2)}, u32[]{:S(2)}) %collective-permute-start.47) | collective-permute-done | bytes 524320 | tf_op jit(solution)/shard_map/ppermute | solution.py:45
  496.7 2.6 fusion.16
  502.4 7.4 %shard_map.286 = (bf16[512,256]{1,0:T(8,128)(2,1)S(1)}, bf16[512,256]{1,0:T(8,128)(2,1)S(1)}, bf16[512,512]{1,0:T(8,128)(2,1)S(1)}, f32[512,256]{1,0:T(8,128)S(1)}) custom-call(s32[1]{0:T(128)} %bitcast.1.t_ref, bf16[512,256]{1,0:T(8,128)(2,1)S(1)} %get-tuple-element.129.q_ref, bf16[512,256]{1,0:T(8,128)(2,1)S(1)} %get-tuple-element.130.k_ref, ...), custom_call_target="tpu_custom_call" | custom-call | flops 1 | bytes 1 | tf_op jit(solution)/shard_map/pallas_call | solution.py:848
  509.9 3.3 shard_map.288
  513.2 3.8 collective-permute-start.50
  523.8 3.3 fusion.47
  535.6 7.6 %shard_map.287 = (bf16[512,2048]{1,0:T(8,128)(2,1)}, f32[1,2048]{1,0:T(1,128)S(1)}) custom-call(bf16[512,1536]{1,0:T(8,128)(2,1)S(1)} %pad_maximum_fusion.7.b_ref.r_ref, bf16[2048,2048]{1,0:T(8,128)(2,1)} %all-gather.4.cloned.1.call-done.w_ref, bf16[512,16]{1,0:T(8,128)(2,1)S(1)} %convolution_convert_fusion.2.br_ref, ...), custom_call_target="tpu_custom_call" | custom-call | flops 1 | bytes 1 | tf_op jit(solution)/shard_map/pallas_call | solution.py:662
  546.2 2.8 convert_add_fusion.2
  549.1 4.6 shard_map.289
  562.6 7.5 %collective-permute-done.53 = bf16[128,2048]{1,0:T(8,128)(2,1)S(1)} collective-permute-done((bf16[128,2048]{1,0:T(8,128)(2,1)S(1)}, bf16[128,2048]{1,0:T(8,128)(2,1)S(1)}, u32[]{:S(2)}, u32[]{:S(2)}) %collective-permute-start.53) | collective-permute-done | bytes 524320 | tf_op jit(solution)/shard_map/ppermute | solution.py:45
  570.2 17.2 %collective-permute-done.54 = bf16[128,2048]{1,0:T(8,128)(2,1)S(1)} collective-permute-done((bf16[128,2048]{1,0:T(8,128)(2,1)S(1)}, bf16[128,2048]{1,0:T(8,128)(2,1)S(1)}, u32[]{:S(2)}, u32[]{:S(2)}) %collective-permute-start.54) | collective-permute-done | bytes 524320 | tf_op jit(solution)/shard_map/ppermute | solution.py:45
  587.3 11.8 %collective-permute-done.55 = bf16[128,2048]{1,0:T(8,128)(2,1)S(1)} collective-permute-done((bf16[128,2048]{1,0:T(8,128)(2,1)S(1)}, bf16[128,2048]{1,0:T(8,128)(2,1)S(1)}, u32[]{:S(2)}, u32[]{:S(2)}) %collective-permute-start.55) | collective-permute-done | bytes 524320 | tf_op jit(solution)/shard_map/ppermute | solution.py:45
  604.2 2.9 collective-permute-start.61
  613.1 9.5 %collective-permute-done.64 = bf16[64,3072]{1,0:T(8,128)(2,1)S(1)} collective-permute-done((bf16[64,3072]{1,0:T(8,128)(2,1)S(1)}, bf16[64,3072]{1,0:T(8,128)(2,1)S(1)}, u32[]{:S(2)}, u32[]{:S(2)}) %collective-permute-start.64) | collective-permute-done | bytes 393248 | tf_op jit(solution)/shard_map/ppermute | solution.py:45
  633.6 15.5 %collective-permute-done.58 = bf16[256,1536]{1,0:T(8,128)(2,1)} collective-permute-done((bf16[256,1536]{1,0:T(8,128)(2,1)}, bf16[256,1536]{1,0:T(8,128)(2,1)}, u32[]{:S(2)}, u32[]{:S(2)}) %collective-permute-start.58) | collective-permute-done | bytes 786464 | tf_op jit(solution)/shard_map/ppermute | solution.py:40
  663.1 4.4 collective-permute-done.67
  667.5 4.5 collective-permute-done.68
  675.6 9.2 %collective-permute-start.75 = (bf16[64,2048]{1,0:T(8,128)(2,1)S(1)}, bf16[64,2048]{1,0:T(8,128)(2,1)S(1)}, u32[]{:S(2)}, u32[]{:S(2)}) collective-permute-start(bf16[64,2048]{1,0:T(8,128)(2,1)S(1)} %add_convert_fusion.8), channel_id=1, source_target_pairs={{0,0},{1,8},{2,16},{3,24},{4,1},{5,9},{6,17},{7,25},{8,2},{9,10},{... | collective-permute-start | bytes 786440 | tf_op jit(solution)/shard_map/ppermute | solution.py:151
  686.3 11.9 %collective-permute-done.75 = bf16[64,2048]{1,0:T(8,128)(2,1)S(1)} collective-permute-done((bf16[64,2048]{1,0:T(8,128)(2,1)S(1)}, bf16[64,2048]{1,0:T(8,128)(2,1)S(1)}, u32[]{:S(2)}, u32[]{:S(2)}) %collective-permute-start.75) | collective-permute-done | bytes 262176 | tf_op jit(solution)/shard_map/ppermute | solution.py:151
  (417 shorter events, 170.2 us)
Async XLA Ops:
  7.2 122.7 %all-gather.4.cloned.1.call-start = ((), (), s32[]{:S(2)}) async-start(), calls=%async_computation.2 | async-start | bytes 9437184 | tf_op jit(solution)/shard_map/all_gather | solution.py:748
  12.2 9.5 %collective-permute-start.2 = (bf16[64,1536]{1,0:T(8,128)(2,1)S(1)}, bf16[64,1536]{1,0:T(8,128)(2,1)S(1)}, u32[]{:S(2)}, u32[]{:S(2)}) collective-permute-start(bf16[64,1536]{1,0:T(8,128)(2,1)S(1)} %broadcast_select_fusion.87), channel_id=1, source_target_pairs={{0,1},{1,0},{2,3},{3,2},{4,5},{5,4},{6,7},{7,6},{8,9},{9,8},{10,11... | collective-permute-start | bytes 589832 | tf_op jit(solution)/shard_map/ppermute | solution.py:45
  12.5 16.9 %collective-permute-start.3 = (bf16[64,2048]{1,0:T(8,128)(2,1)S(1)}, bf16[64,2048]{1,0:T(8,128)(2,1)S(1)}, u32[]{:S(2)}, u32[]{:S(2)}) collective-permute-start(bf16[64,2048]{1,0:T(8,128)(2,1)S(1)} %copy-done.60), channel_id=1, source_target_pairs={{0,0},{8,1},{16,2},{24,3},{1,4},{9,5},{17,6},{25,7},{2,8},{10,9},{... | collective-permute-start | bytes 786440 | tf_op jit(solution)/shard_map/ppermute | solution.py:147
  30.5 203.6 %all-gather.8.cloned.1.call-start = ((), (), s32[]{:S(2)}) async-start(), calls=%async_computation.4 | async-start | bytes 3604480 | tf_op jit(solution)/shard_map/all_gather | solution.py:765
  31.3 268.1 %all-gather.6.cloned.1.call-start = ((), (), s32[]{:S(2)}) async-start(), calls=%async_computation.3 | async-start | bytes 7864320 | tf_op jit(solution)/shard_map/all_gather | solution.py:806
  39.0 9.7 %collective-permute-start.12 = (bf16[4,8,256]{2,1,0:T(8,128)(2,1)S(1)}, bf16[4,8,256]{2,1,0:T(8,128)(2,1)}, u32[]{:S(2)}, u32[]{:S(2)}) collective-permute-start(bf16[4,8,256]{2,1,0:T(8,128)(2,1)S(1)} %pad_maximum_fusion.19), channel_id=1, source_target_pairs={{0,4},{4,0},{1,5},{5,1},{2,6},{6,2},{3,7},{7,3},{8,12},{12,8},{9,1... | collective-permute-start | bytes 49160 | tf_op jit(solution)/shard_map/ppermute | solution.py:40
  45.9 17.3 %collective-permute-start.4 = (bf16[128,2048]{1,0:T(8,128)(2,1)S(1)}, bf16[128,2048]{1,0:T(8,128)(2,1)S(1)}, u32[]{:S(2)}, u32[]{:S(2)}) collective-permute-start(bf16[128,2048]{1,0:T(8,128)(2,1)S(1)} %bitcast.53), channel_id=1, source_target_pairs={{0,1},{1,0},{2,3},{3,2},{4,5},{5,4},{6,7},{7,6},{8,9},{9,8},{10,11... | collective-permute-start | bytes 1572872 | tf_op jit(solution)/shard_map/ppermute | solution.py:45
  47.4 17.6 %collective-permute-start.5 = (bf16[128,2048]{1,0:T(8,128)(2,1)S(1)}, bf16[128,2048]{1,0:T(8,128)(2,1)}, u32[]{:S(2)}, u32[]{:S(2)}) collective-permute-start(bf16[128,2048]{1,0:T(8,128)(2,1)S(1)} %bitcast.54), channel_id=1, source_target_pairs={{0,2},{1,3},{2,0},{3,1},{4,6},{5,7},{6,4},{7,5},{8,10},{9,11},{10,... | collective-permute-start | bytes 1572872 | tf_op jit(solution)/shard_map/ppermute | solution.py:45
  47.4 31.8 %collective-permute-start.6 = (bf16[128,2048]{1,0:T(8,128)(2,1)S(1)}, bf16[128,2048]{1,0:T(8,128)(2,1)}, u32[]{:S(2)}, u32[]{:S(2)}) collective-permute-start(bf16[128,2048]{1,0:T(8,128)(2,1)S(1)} %bitcast.55), channel_id=1, source_target_pairs={{0,3},{1,2},{2,1},{3,0},{4,7},{5,6},{6,5},{7,4},{8,11},{9,10},{10,... | collective-permute-start | bytes 1572872 | tf_op jit(solution)/shard_map/ppermute | solution.py:45
  57.5 29.9 %collective-permute-start.14 = (bf16[16,8,256]{2,1,0:T(8,128)(2,1)S(1)}, bf16[16,8,256]{2,1,0:T(8,128)(2,1)S(1)}, u32[]{:S(2)}, u32[]{:S(2)}) collective-permute-start(bf16[16,8,256]{2,1,0:T(8,128)(2,1)S(1)} %pad_maximum_fusion.17), channel_id=1, source_target_pairs={{0,8},{8,0},{1,9},{9,1},{2,10},{10,2},{3,11},{11,3},{4,12},{12,4},... | collective-permute-start | bytes 196616 | tf_op jit(solution)/shard_map/ppermute | solution.py:40
  82.2 9.6 %collective-permute-start.7 = (bf16[128,2048]{1,0:T(8,128)(2,1)S(1)}, bf16[128,2048]{1,0:T(8,128)(2,1)S(1)}, u32[]{:S(2)}, u32[]{:S(2)}) collective-permute-start(bf16[128,2048]{1,0:T(8,128)(2,1)S(1)} %bitcast.57), channel_id=1, source_target_pairs={{0,1},{1,0},{2,3},{3,2},{4,5},{5,4},{6,7},{7,6},{8,9},{9,8},{10,11... | collective-permute-start | bytes 1572872 | tf_op jit(solution)/shard_map/ppermute | solution.py:45
  84.9 20.7 %collective-permute-start.8 = (bf16[128,2048]{1,0:T(8,128)(2,1)S(1)}, bf16[128,2048]{1,0:T(8,128)(2,1)S(1)}, u32[]{:S(2)}, u32[]{:S(2)}) collective-permute-start(bf16[128,2048]{1,0:T(8,128)(2,1)S(1)} %bitcast.58), channel_id=1, source_target_pairs={{0,2},{1,3},{2,0},{3,1},{4,6},{5,7},{6,4},{7,5},{8,10},{9,11},{10,... | collective-permute-start | bytes 1572872 | tf_op jit(solution)/shard_map/ppermute | solution.py:45
  85.2 39.0 %collective-permute-start.9 = (bf16[128,2048]{1,0:T(8,128)(2,1)S(1)}, bf16[128,2048]{1,0:T(8,128)(2,1)}, u32[]{:S(2)}, u32[]{:S(2)}) collective-permute-start(bf16[128,2048]{1,0:T(8,128)(2,1)S(1)} %bitcast.59), channel_id=1, source_target_pairs={{0,3},{1,2},{2,1},{3,0},{4,7},{5,6},{6,5},{7,4},{8,11},{9,10},{10,... | collective-permute-start | bytes 1572872 | tf_op jit(solution)/shard_map/ppermute | solution.py:45
  129.9 21.9 %collective-permute-start.16 = (bf16[64,3072]{1,0:T(8,128)(2,1)}, bf16[64,3072]{1,0:T(8,128)(2,1)}, u32[]{:S(2)}, u32[]{:S(2)}) collective-permute-start(bf16[64,3072]{1,0:T(8,128)(2,1)} %get-tuple-element.139), channel_id=1, source_target_pairs={{0,3},{1,2},{2,1},{3,0},{4,7},{5,6},{6,5},{7,4},{8,11},{9,10},{10,... | collective-permute-start | bytes 1179656 | tf_op jit(solution)/shard_map/ppermute | solution.py:45
  129.9 28.3 %collective-permute-start.17 = (bf16[64,3072]{1,0:T(8,128)(2,1)}, bf16[64,3072]{1,0:T(8,128)(2,1)}, u32[]{:S(2)}, u32[]{:S(2)}) collective-permute-start(bf16[64,3072]{1,0:T(8,128)(2,1)} %get-tuple-element.140), channel_id=1, source_target_pairs={{0,2},{1,3},{2,0},{3,1},{4,6},{5,7},{6,4},{7,5},{8,10},{9,11},{10,... | collective-permute-start | bytes 1179656 | tf_op jit(solution)/shard_map/ppermute | solution.py:45
  132.2 26.0 %collective-permute-start.18 = (bf16[64,3072]{1,0:T(8,128)(2,1)}, bf16[64,3072]{1,0:T(8,128)(2,1)}, u32[]{:S(2)}, u32[]{:S(2)}) collective-permute-start(bf16[64,3072]{1,0:T(8,128)(2,1)} %get-tuple-element.141), channel_id=1, source_target_pairs={{0,1},{1,0},{2,3},{3,2},{4,5},{5,4},{6,7},{7,6},{8,9},{9,8},{10,11... | collective-permute-start | bytes 1179656 | tf_op jit(solution)/shard_map/ppermute | solution.py:45
  133.6 26.2 %collective-permute-start.15 = (bf16[128,2048]{1,0:T(8,128)(2,1)S(1)}, bf16[128,2048]{1,0:T(8,128)(2,1)}, u32[]{:S(2)}, u32[]{:S(2)}) collective-permute-start(bf16[128,2048]{1,0:T(8,128)(2,1)S(1)} %bitcast.61), channel_id=1, source_target_pairs={{0,4},{4,0},{1,5},{5,1},{2,6},{6,2},{3,7},{7,3},{8,12},{12,8},{9,1... | collective-permute-start | bytes 1572872 | tf_op jit(solution)/shard_map/ppermute | solution.py:40
  159.8 9.6 %collective-permute-start.20 = (bf16[128,2048]{1,0:T(8,128)(2,1)}, bf16[128,2048]{1,0:T(8,128)(2,1)S(1)}, u32[]{:S(2)}, u32[]{:S(2)}) collective-permute-start(bf16[128,2048]{1,0:T(8,128)(2,1)} %collective-permute-done.15), channel_id=1, source_target_pairs={{0,1},{1,0},{2,3},{3,2},{4,5},{5,4},{6,7},{7,6},{8,9},{9,8},{10,11... | collective-permute-start | bytes 1572872 | tf_op jit(solution)/shard_map/ppermute | solution.py:45
  160.7 20.9 %collective-permute-start.22 = (bf16[128,2048]{1,0:T(8,128)(2,1)}, bf16[128,2048]{1,0:T(8,128)(2,1)S(1)}, u32[]{:S(2)}, u32[]{:S(2)}) collective-permute-start(bf16[128,2048]{1,0:T(8,128)(2,1)} %collective-permute-done.15), channel_id=1, source_target_pairs={{0,3},{1,2},{2,1},{3,0},{4,7},{5,6},{6,5},{7,4},{8,11},{9,10},{10,... | collective-permute-start | bytes 1572872 | tf_op jit(solution)/shard_map/ppermute | solution.py:45
  163.7 21.6 %collective-permute-start.19 = (bf16[512,256]{1,0:T(8,128)(2,1)S(1)}, bf16[512,256]{1,0:T(8,128)(2,1)S(1)}, u32[]{:S(2)}, u32[]{:S(2)}) collective-permute-start(bf16[512,256]{1,0:T(8,128)(2,1)S(1)} %copy-done.20), channel_id=1, source_target_pairs={{0,4},{1,5},{2,6},{3,7},{8,12},{9,13},{10,14},{11,15},{16,20},{17,... | collective-permute-start | bytes 786440 | tf_op jit(solution)/shard_map/ppermute | solution.py:683
  193.9 37.4 %collective-permute-start.25 = (bf16[128,2048]{1,0:T(8,128)(2,1)S(1)}, bf16[128,2048]{1,0:T(8,128)(2,1)S(1)}, u32[]{:S(2)}, u32[]{:S(2)}) collective-permute-start(bf16[128,2048]{1,0:T(8,128)(2,1)S(1)} %get-tuple-element.284), channel_id=1, source_target_pairs={{0,3},{1,2},{2,1},{3,0},{4,7},{5,6},{6,5},{7,4},{8,11},{9,10},{10,... | collective-permute-start | bytes 1572872 | tf_op jit(solution)/shard_map/ppermute | solution.py:45
  196.4 36.3 %collective-permute-start.26 = (bf16[256,1536]{1,0:T(8,128)(2,1)S(1)}, bf16[256,1536]{1,0:T(8,128)(2,1)S(1)}, u32[]{:S(2)}, u32[]{:S(2)}) collective-permute-start(bf16[256,1536]{1,0:T(8,128)(2,1)S(1)} %broadcast_select_fusion.7), channel_id=1, source_target_pairs={{0,4},{4,0},{1,5},{5,1},{2,6},{6,2},{3,7},{7,3},{8,12},{12,8},{9,1... | collective-permute-start | bytes 2359304 | tf_op jit(solution)/shard_map/ppermute | solution.py:40
  234.1 262.6 %reduce-scatter.3.cloned.1.call-start = ((), (), s32[]{:S(2)}) async-start(), calls=%async_computation.5 | async-start | bytes 3604480 | tf_op jit(solution)/shard_map/reduce_scatter | solution.py:832
  241.2 31.5 %collective-permute-start.27 = (bf16[128,2048]{1,0:T(8,128)(2,1)S(1)}, bf16[128,2048]{1,0:T(8,128)(2,1)S(1)}, u32[]{:S(2)}, u32[]{:S(2)}) collective-permute-start(bf16[128,2048]{1,0:T(8,128)(2,1)S(1)} %get-tuple-element.247), channel_id=1, source_target_pairs={{0,1},{1,0},{2,3},{3,2},{4,5},{5,4},{6,7},{7,6},{8,9},{9,8},{10,11... | collective-permute-start | bytes 1572872 | tf_op jit(solution)/shard_map/ppermute | solution.py:45
  241.2 32.4 %collective-permute-start.28 = (bf16[128,2048]{1,0:T(8,128)(2,1)S(1)}, bf16[128,2048]{1,0:T(8,128)(2,1)S(1)}, u32[]{:S(2)}, u32[]{:S(2)}) collective-permute-start(bf16[128,2048]{1,0:T(8,128)(2,1)S(1)} %get-tuple-element.247), channel_id=1, source_target_pairs={{0,2},{1,3},{2,0},{3,1},{4,6},{5,7},{6,4},{7,5},{8,10},{9,11},{10,... | collective-permute-start | bytes 1572872 | tf_op jit(solution)/shard_map/ppermute | solution.py:45
  245.5 16.4 %collective-permute-start.30 = (bf16[128,2048]{1,0:T(8,128)(2,1)S(1)}, bf16[128,2048]{1,0:T(8,128)(2,1)S(1)}, u32[]{:S(2)}, u32[]{:S(2)}) collective-permute-start(bf16[128,2048]{1,0:T(8,128)(2,1)S(1)} %get-tuple-element.247), channel_id=1, source_target_pairs={{0,4},{4,0},{1,5},{5,1},{2,6},{6,2},{3,7},{7,3},{8,12},{12,8},{9,1... | collective-permute-start | bytes 1572872 | tf_op jit(solution)/shard_map/ppermute | solution.py:40
  251.2 24.9 %collective-permute-start.29 = (bf16[128,2048]{1,0:T(8,128)(2,1)S(1)}, bf16[128,2048]{1,0:T(8,128)(2,1)S(1)}, u32[]{:S(2)}, u32[]{:S(2)}) collective-permute-start(bf16[128,2048]{1,0:T(8,128)(2,1)S(1)} %get-tuple-element.247), channel_id=1, source_target_pairs={{0,3},{1,2},{2,1},{3,0},{4,7},{5,6},{6,5},{7,4},{8,11},{9,10},{10,... | collective-permute-start | bytes 1572872 | tf_op jit(solution)/shard_map/ppermute | solution.py:45
  261.9 15.8 %collective-permute-start.31 = (bf16[128,2048]{1,0:T(8,128)(2,1)S(1)}, bf16[128,2048]{1,0:T(8,128)(2,1)S(1)}, u32[]{:S(2)}, u32[]{:S(2)}) collective-permute-start(bf16[128,2048]{1,0:T(8,128)(2,1)S(1)} %collective-permute-done.30), channel_id=1, source_target_pairs={{0,1},{1,0},{2,3},{3,2},{4,5},{5,4},{6,7},{7,6},{8,9},{9,8},{10,11... | collective-permute-start | bytes 1572872 | tf_op jit(solution)/shard_map/ppermute | solution.py:45
  264.1 22.1 %collective-permute-start.32 = (bf16[128,2048]{1,0:T(8,128)(2,1)S(1)}, bf16[128,2048]{1,0:T(8,128)(2,1)S(1)}, u32[]{:S(2)}, u32[]{:S(2)}) collective-permute-start(bf16[128,2048]{1,0:T(8,128)(2,1)S(1)} %collective-permute-done.30), channel_id=1, source_target_pairs={{0,2},{1,3},{2,0},{3,1},{4,6},{5,7},{6,4},{7,5},{8,10},{9,11},{10,... | collective-permute-start | bytes 1572872 | tf_op jit(solution)/shard_map/ppermute | solution.py:45
  272.7 25.7 %collective-permute-start.33 = (bf16[128,2048]{1,0:T(8,128)(2,1)S(1)}, bf16[128,2048]{1,0:T(8,128)(2,1)S(1)}, u32[]{:S(2)}, u32[]{:S(2)}) collective-permute-start(bf16[128,2048]{1,0:T(8,128)(2,1)S(1)} %collective-permute-done.30), channel_id=1, source_target_pairs={{0,3},{1,2},{2,1},{3,0},{4,7},{5,6},{6,5},{7,4},{8,11},{9,10},{10,... | collective-permute-start | bytes 1572872 | tf_op jit(solution)/shard_map/ppermute | solution.py:45
  329.8 18.6 %collective-permute-start.36 = (bf16[128,2048]{1,0:T(8,128)(2,1)S(1)}, bf16[128,2048]{1,0:T(8,128)(2,1)S(1)}, u32[]{:S(2)}, u32[]{:S(2)}) collective-permute-start(bf16[128,2048]{1,0:T(8,128)(2,1)S(1)} %get-tuple-element.264), channel_id=1, source_target_pairs={{0,3},{1,2},{2,1},{3,0},{4,7},{5,6},{6,5},{7,4},{8,11},{9,10},{10,... | collective-permute-start | bytes 1572872 | tf_op jit(solution)/shard_map/ppermute | solution.py:45
  350.0 35.4 %collective-permute-start.37 = (bf16[128,2048]{1,0:T(8,128)(2,1)S(1)}, bf16[128,2048]{1,0:T(8,128)(2,1)S(1)}, u32[]{:S(2)}, u32[]{:S(2)}) collective-permute-start(bf16[128,2048]{1,0:T(8,128)(2,1)S(1)} %get-tuple-element.260), channel_id=1, source_target_pairs={{0,1},{1,0},{2,3},{3,2},{4,5},{5,4},{6,7},{7,6},{8,9},{9,8},{10,11... | collective-permute-start | bytes 1572872 | tf_op jit(solution)/shard_map/ppermute | solution.py:45
  350.0 35.2 %collective-permute-start.40 = (bf16[128,2048]{1,0:T(8,128)(2,1)S(1)}, bf16[128,2048]{1,0:T(8,128)(2,1)S(1)}, u32[]{:S(2)}, u32[]{:S(2)}) collective-permute-start(bf16[128,2048]{1,0:T(8,128)(2,1)S(1)} %add_convert_fusion.7), channel_id=1, source_target_pairs={{0,4},{4,0},{1,5},{5,1},{2,6},{6,2},{3,7},{7,3},{8,12},{12,8},{9,1... | collective-permute-start | bytes 1572872 | tf_op jit(solution)/shard_map/ppermute | solution.py:40
  362.9 22.5 %collective-permute-start.38 = (bf16[128,2048]{1,0:T(8,128)(2,1)S(1)}, bf16[128,2048]{1,0:T(8,128)(2,1)S(1)}, u32[]{:S(2)}, u32[]{:S(2)}) collective-permute-start(bf16[128,2048]{1,0:T(8,128)(2,1)S(1)} %get-tuple-element.262), channel_id=1, source_target_pairs={{0,2},{1,3},{2,0},{3,1},{4,6},{5,7},{6,4},{7,5},{8,10},{9,11},{10,... | collective-permute-start | bytes 1572872 | tf_op jit(solution)/shard_map/ppermute | solution.py:45
  364.4 30.2 %collective-permute-start.39 = (bf16[128,2048]{1,0:T(8,128)(2,1)S(1)}, bf16[128,2048]{1,0:T(8,128)(2,1)S(1)}, u32[]{:S(2)}, u32[]{:S(2)}) collective-permute-start(bf16[128,2048]{1,0:T(8,128)(2,1)S(1)} %get-tuple-element.261), channel_id=1, source_target_pairs={{0,3},{1,2},{2,1},{3,0},{4,7},{5,6},{6,5},{7,4},{8,11},{9,10},{10,... | collective-permute-start | bytes 1572872 | tf_op jit(solution)/shard_map/ppermute | solution.py:45
  397.4 9.8 %collective-permute-start.41 = (bf16[128,2048]{1,0:T(8,128)(2,1)}, bf16[128,2048]{1,0:T(8,128)(2,1)}, u32[]{:S(2)}, u32[]{:S(2)}) collective-permute-start(bf16[128,2048]{1,0:T(8,128)(2,1)} %get-tuple-element.244), channel_id=1, source_target_pairs={{0,1},{1,0},{2,3},{3,2},{4,5},{5,4},{6,7},{7,6},{8,9},{9,8},{10,11... | collective-permute-start | bytes 1572872 | tf_op jit(solution)/shard_map/ppermute | solution.py:45
  397.7 9.6 %collective-permute-start.42 = (bf16[128,2048]{1,0:T(8,128)(2,1)}, bf16[128,2048]{1,0:T(8,128)(2,1)}, u32[]{:S(2)}, u32[]{:S(2)}) collective-permute-start(bf16[128,2048]{1,0:T(8,128)(2,1)} %get-tuple-element.244), channel_id=1, source_target_pairs={{0,2},{1,3},{2,0},{3,1},{4,6},{5,7},{6,4},{7,5},{8,10},{9,11},{10,... | collective-permute-start | bytes 1572872 | tf_op jit(solution)/shard_map/ppermute | solution.py:45
  399.3 19.5 %collective-permute-start.43 = (bf16[128,2048]{1,0:T(8,128)(2,1)}, bf16[128,2048]{1,0:T(8,128)(2,1)}, u32[]{:S(2)}, u32[]{:S(2)}) collective-permute-start(bf16[128,2048]{1,0:T(8,128)(2,1)} %get-tuple-element.244), channel_id=1, source_target_pairs={{0,3},{1,2},{2,1},{3,0},{4,7},{5,6},{6,5},{7,4},{8,11},{9,10},{10,... | collective-permute-start | bytes 1572872 | tf_op jit(solution)/shard_map/ppermute | solution.py:45
  421.9 133.9 %reduce-scatter.5.cloned.1.call-start = ((), (), s32[]{:S(2)}) async-start(), calls=%async_computation.6 | async-start | bytes 7864320 | tf_op jit(solution)/shard_map/reduce_scatter | solution.py:841
  459.0 36.2 %collective-permute-start.48 = (bf16[256,2048]{1,0:T(8,128)(2,1)S(1)}, bf16[256,2048]{1,0:T(8,128)(2,1)S(1)}, u32[]{:S(2)}, u32[]{:S(2)}) collective-permute-start(bf16[256,2048]{1,0:T(8,128)(2,1)S(1)} %pad_maximum_fusion.9), channel_id=1, source_target_pairs={{0,8},{8,0},{1,9},{9,1},{2,10},{10,2},{3,11},{11,3},{4,12},{12,4},... | collective-permute-start | bytes 3145736 | tf_op jit(solution)/shard_map/ppermute | solution.py:40
  464.7 11.6 %collective-permute-start.45 = (bf16[128,2048]{1,0:T(8,128)(2,1)S(1)}, bf16[128,2048]{1,0:T(8,128)(2,1)S(1)}, u32[]{:S(2)}, u32[]{:S(2)}) collective-permute-start(bf16[128,2048]{1,0:T(8,128)(2,1)S(1)} %get-tuple-element.257), channel_id=1, source_target_pairs={{0,1},{1,0},{2,3},{3,2},{4,5},{5,4},{6,7},{7,6},{8,9},{9,8},{10,11... | collective-permute-start | bytes 1572872 | tf_op jit(solution)/shard_map/ppermute | solution.py:45
  465.0 16.8 %collective-permute-start.46 = (bf16[128,2048]{1,0:T(8,128)(2,1)S(1)}, bf16[128,2048]{1,0:T(8,128)(2,1)S(1)}, u32[]{:S(2)}, u32[]{:S(2)}) collective-permute-start(bf16[128,2048]{1,0:T(8,128)(2,1)S(1)} %get-tuple-element.259), channel_id=1, source_target_pairs={{0,2},{1,3},{2,0},{3,1},{4,6},{5,7},{6,4},{7,5},{8,10},{9,11},{10,... | collective-permute-start | bytes 1572872 | tf_op jit(solution)/shard_map/ppermute | solution.py:45
  466.5 27.6 %collective-permute-start.47 = (bf16[128,2048]{1,0:T(8,128)(2,1)S(1)}, bf16[128,2048]{1,0:T(8,128)(2,1)S(1)}, u32[]{:S(2)}, u32[]{:S(2)}) collective-permute-start(bf16[128,2048]{1,0:T(8,128)(2,1)S(1)} %get-tuple-element.258), channel_id=1, source_target_pairs={{0,3},{1,2},{2,1},{3,0},{4,7},{5,6},{6,5},{7,4},{8,11},{9,10},{10,... | collective-permute-start | bytes 1572872 | tf_op jit(solution)/shard_map/ppermute | solution.py:45
  467.4 29.3 %collective-permute-start.44 = (bf16[512,256]{1,0:T(8,128)(2,1)S(1)}, bf16[512,256]{1,0:T(8,128)(2,1)S(1)}, u32[]{:S(2)}, u32[]{:S(2)}) collective-permute-start(bf16[512,256]{1,0:T(8,128)(2,1)S(1)} %copy-done.18), channel_id=1, source_target_pairs={{4,0},{5,1},{6,2},{7,3},{12,8},{13,9},{14,10},{15,11},{20,16},{21,... | collective-permute-start | bytes 786440 | tf_op jit(solution)/shard_map/ppermute | solution.py:683
  499.4 10.5 %collective-permute-start.49 = (bf16[128,2048]{1,0:T(8,128)(2,1)S(1)}, bf16[128,2048]{1,0:T(8,128)(2,1)S(1)}, u32[]{:S(2)}, u32[]{:S(2)}) collective-permute-start(bf16[128,2048]{1,0:T(8,128)(2,1)S(1)} %get-tuple-element.256), channel_id=1, source_target_pairs={{0,1},{1,0},{2,3},{3,2},{4,5},{5,4},{6,7},{7,6},{8,9},{9,8},{10,11... | collective-permute-start | bytes 1572872 | tf_op jit(solution)/shard_map/ppermute | solution.py:45
  513.2 35.9 %collective-permute-start.50 = (bf16[1024,1536]{1,0:T(8,128)(2,1)}, bf16[1024,1536]{1,0:T(8,128)(2,1)}, u32[]{:S(2)}, u32[]{:S(2)}) collective-permute-start(bf16[1024,1536]{1,0:T(8,128)(2,1)} %shard_map.288), channel_id=1, source_target_pairs={{0,8},{8,0},{1,9},{9,1},{2,10},{10,2},{3,11},{11,3},{4,12},{12,4},... | collective-permute-start | bytes 9437192 | tf_op jit(solution)/shard_map/ppermute | solution.py:40
  520.6 23.7 %collective-permute-start.51 = (bf16[128,2048]{1,0:T(8,128)(2,1)}, bf16[128,2048]{1,0:T(8,128)(2,1)}, u32[]{:S(2)}, u32[]{:S(2)}) collective-permute-start(bf16[128,2048]{1,0:T(8,128)(2,1)} %get-tuple-element.254), channel_id=1, source_target_pairs={{0,2},{1,3},{2,0},{3,1},{4,6},{5,7},{6,4},{7,5},{8,10},{9,11},{10,... | collective-permute-start | bytes 1572872 | tf_op jit(solution)/shard_map/ppermute | solution.py:45
  520.6 25.7 %collective-permute-start.52 = (bf16[128,2048]{1,0:T(8,128)(2,1)}, bf16[128,2048]{1,0:T(8,128)(2,1)}, u32[]{:S(2)}, u32[]{:S(2)}) collective-permute-start(bf16[128,2048]{1,0:T(8,128)(2,1)} %get-tuple-element.255), channel_id=1, source_target_pairs={{0,3},{1,2},{2,1},{3,0},{4,7},{5,6},{6,5},{7,4},{8,11},{9,10},{10,... | collective-permute-start | bytes 1572872 | tf_op jit(solution)/shard_map/ppermute | solution.py:45
  557.5 12.7 %collective-permute-start.53 = (bf16[128,2048]{1,0:T(8,128)(2,1)S(1)}, bf16[128,2048]{1,0:T(8,128)(2,1)S(1)}, u32[]{:S(2)}, u32[]{:S(2)}) collective-permute-start(bf16[128,2048]{1,0:T(8,128)(2,1)S(1)} %get-tuple-element.274), channel_id=1, source_target_pairs={{0,1},{1,0},{2,3},{3,2},{4,5},{5,4},{6,7},{7,6},{8,9},{9,8},{10,11... | collective-permute-start | bytes 1572872 | tf_op jit(solution)/shard_map/ppermute | solution.py:45
  558.1 29.2 %collective-permute-start.54 = (bf16[128,2048]{1,0:T(8,128)(2,1)S(1)}, bf16[128,2048]{1,0:T(8,128)(2,1)S(1)}, u32[]{:S(2)}, u32[]{:S(2)}) collective-permute-start(bf16[128,2048]{1,0:T(8,128)(2,1)S(1)} %get-tuple-element.276), channel_id=1, source_target_pairs={{0,2},{1,3},{2,0},{3,1},{4,6},{5,7},{6,4},{7,5},{8,10},{9,11},{10,... | collective-permute-start | bytes 1572872 | tf_op jit(solution)/shard_map/ppermute | solution.py:45
  558.3 40.8 %collective-permute-start.55 = (bf16[128,2048]{1,0:T(8,128)(2,1)S(1)}, bf16[128,2048]{1,0:T(8,128)(2,1)S(1)}, u32[]{:S(2)}, u32[]{:S(2)}) collective-permute-start(bf16[128,2048]{1,0:T(8,128)(2,1)S(1)} %get-tuple-element.275), channel_id=1, source_target_pairs={{0,3},{1,2},{2,1},{3,0},{4,7},{5,6},{6,5},{7,4},{8,11},{9,10},{10,... | collective-permute-start | bytes 1572872 | tf_op jit(solution)/shard_map/ppermute | solution.py:45
  560.3 40.2 %collective-permute-start.57 = (bf16[256,1536]{1,0:T(8,128)(2,1)S(1)}, bf16[256,1536]{1,0:T(8,128)(2,1)S(1)}, u32[]{:S(2)}, u32[]{:S(2)}) collective-permute-start(bf16[256,1536]{1,0:T(8,128)(2,1)S(1)} %broadcast_select_fusion.3), channel_id=1, source_target_pairs={{0,4},{4,0},{1,5},{5,1},{2,6},{6,2},{3,7},{7,3},{8,12},{12,8},{9,1... | collective-permute-start | bytes 2359304 | tf_op jit(solution)/shard_map/ppermute | solution.py:40
  560.3 40.5 %collective-permute-start.56 = (bf16[512,1536]{1,0:T(8,128)(2,1)S(1)}, bf16[512,1536]{1,0:T(8,128)(2,1)S(1)}, u32[]{:S(2)}, u32[]{:S(2)}) collective-permute-start(bf16[512,1536]{1,0:T(8,128)(2,1)S(1)} %get-tuple-element.195), channel_id=1, source_target_pairs={{0,16},{16,0},{1,17},{17,1},{2,18},{18,2},{3,19},{19,3},{4,20},{20... | collective-permute-start | bytes 4718600 | tf_op jit(solution)/shard_map/ppermute | solution.py:40
  601.4 11.7 %collective-permute-start.63 = (bf16[64,3072]{1,0:T(8,128)(2,1)S(1)}, bf16[64,3072]{1,0:T(8,128)(2,1)S(1)}, u32[]{:S(2)}, u32[]{:S(2)}) collective-permute-start(bf16[64,3072]{1,0:T(8,128)(2,1)S(1)} %get-tuple-element.295), channel_id=1, source_target_pairs={{0,3},{1,2},{2,1},{3,0},{4,7},{5,6},{6,5},{7,4},{8,11},{9,10},{10,... | collective-permute-start | bytes 1179656 | tf_op jit(solution)/shard_map/ppermute | solution.py:45
  601.5 21.1 %collective-permute-start.64 = (bf16[64,3072]{1,0:T(8,128)(2,1)S(1)}, bf16[64,3072]{1,0:T(8,128)(2,1)S(1)}, u32[]{:S(2)}, u32[]{:S(2)}) collective-permute-start(bf16[64,3072]{1,0:T(8,128)(2,1)S(1)} %get-tuple-element.296), channel_id=1, source_target_pairs={{0,2},{1,3},{2,0},{3,1},{4,6},{5,7},{6,4},{7,5},{8,10},{9,11},{10,... | collective-permute-start | bytes 1179656 | tf_op jit(solution)/shard_map/ppermute | solution.py:45
  603.3 19.3 %collective-permute-start.65 = (bf16[64,3072]{1,0:T(8,128)(2,1)S(1)}, bf16[64,3072]{1,0:T(8,128)(2,1)S(1)}, u32[]{:S(2)}, u32[]{:S(2)}) collective-permute-start(bf16[64,3072]{1,0:T(8,128)(2,1)S(1)} %get-tuple-element.294), channel_id=1, source_target_pairs={{0,1},{1,0},{2,3},{3,2},{4,5},{5,4},{6,7},{7,6},{8,9},{9,8},{10,11... | collective-permute-start | bytes 1179656 | tf_op jit(solution)/shard_map/ppermute | solution.py:45
  612.0 20.5 %collective-permute-start.59 = (bf16[128,2048]{1,0:T(8,128)(2,1)S(1)}, bf16[128,2048]{1,0:T(8,128)(2,1)}, u32[]{:S(2)}, u32[]{:S(2)}) collective-permute-start(bf16[128,2048]{1,0:T(8,128)(2,1)S(1)} %copy-done.44), channel_id=1, source_target_pairs={{0,16},{16,0},{1,17},{17,1},{2,18},{18,2},{3,19},{19,3},{4,20},{20... | collective-permute-start | bytes 1572872 | tf_op jit(solution)/shard_map/ppermute | solution.py:40
  613.1 36.0 %collective-permute-start.58 = (bf16[256,1536]{1,0:T(8,128)(2,1)}, bf16[256,1536]{1,0:T(8,128)(2,1)}, u32[]{:S(2)}, u32[]{:S(2)}) collective-permute-start(bf16[256,1536]{1,0:T(8,128)(2,1)} %broadcast_select_fusion), channel_id=1, source_target_pairs={{0,4},{4,0},{1,5},{5,1},{2,6},{6,2},{3,7},{7,3},{8,12},{12,8},{9,1... | collective-permute-start | bytes 2359304 | tf_op jit(solution)/shard_map/ppermute | solution.py:40
  651.4 24.1 %collective-permute-start.74 = (bf16[64,2048]{1,0:T(8,128)(2,1)}, bf16[64,2048]{1,0:T(8,128)(2,1)S(1)}, u32[]{:S(2)}, u32[]{:S(2)}) collective-permute-start(bf16[64,2048]{1,0:T(8,128)(2,1)} %broadcast_select_fusion.55), channel_id=1, source_target_pairs={{0,4},{4,0},{1,5},{5,1},{2,6},{6,2},{3,7},{7,3},{8,12},{12,8},{9,1... | collective-permute-start | bytes 786440 | tf_op jit(solution)/shard_map/ppermute | solution.py:40
  657.1 10.4 %collective-permute-start.67 = (bf16[64,1536]{1,0:T(8,128)(2,1)S(1)}, bf16[64,1536]{1,0:T(8,128)(2,1)S(1)}, u32[]{:S(2)}, u32[]{:S(2)}) collective-permute-start(bf16[64,1536]{1,0:T(8,128)(2,1)S(1)} %get-tuple-element.312), channel_id=1, source_target_pairs={{0,3},{1,2},{2,1},{3,0},{4,7},{5,6},{6,5},{7,4},{8,11},{9,10},{10,... | collective-permute-start | bytes 589832 | tf_op jit(solution)/shard_map/ppermute | solution.py:45
  657.6 14.4 %collective-permute-start.68 = (bf16[64,1536]{1,0:T(8,128)(2,1)S(1)}, bf16[64,1536]{1,0:T(8,128)(2,1)S(1)}, u32[]{:S(2)}, u32[]{:S(2)}) collective-permute-start(bf16[64,1536]{1,0:T(8,128)(2,1)S(1)} %get-tuple-element.313), channel_id=1, source_target_pairs={{0,2},{1,3},{2,0},{3,1},{4,6},{5,7},{6,4},{7,5},{8,10},{9,11},{10,... | collective-permute-start | bytes 589832 | tf_op jit(solution)/shard_map/ppermute | solution.py:45
  659.1 12.9 %collective-permute-start.69 = (bf16[64,1536]{1,0:T(8,128)(2,1)S(1)}, bf16[64,1536]{1,0:T(8,128)(2,1)}, u32[]{:S(2)}, u32[]{:S(2)}) collective-permute-start(bf16[64,1536]{1,0:T(8,128)(2,1)S(1)} %get-tuple-element.311), channel_id=1, source_target_pairs={{0,1},{1,0},{2,3},{3,2},{4,5},{5,4},{6,7},{7,6},{8,9},{9,8},{10,11... | collective-permute-start | bytes 589832 | tf_op jit(solution)/shard_map/ppermute | solution.py:45
  659.8 39.2 %collective-permute-start.66 = (bf16[128,2048]{1,0:T(8,128)(2,1)S(1)}, bf16[128,2048]{1,0:T(8,128)(2,1)S(1)}, u32[]{:S(2)}, u32[]{:S(2)}) collective-permute-start(bf16[128,2048]{1,0:T(8,128)(2,1)S(1)} %copy-done.43), channel_id=1, source_target_pairs={{0,4},{4,0},{1,5},{5,1},{2,6},{6,2},{3,7},{7,3},{8,12},{12,8},{9,1... | collective-permute-start | bytes 1572872 | tf_op jit(solution)/shard_map/ppermute | solution.py:40
  675.6 22.6 %collective-permute-start.75 = (bf16[64,2048]{1,0:T(8,128)(2,1)S(1)}, bf16[64,2048]{1,0:T(8,128)(2,1)S(1)}, u32[]{:S(2)}, u32[]{:S(2)}) collective-permute-start(bf16[64,2048]{1,0:T(8,128)(2,1)S(1)} %add_convert_fusion.8), channel_id=1, source_target_pairs={{0,0},{1,8},{2,16},{3,24},{4,1},{5,9},{6,17},{7,25},{8,2},{9,10},{... | collective-permute-start | bytes 786440 | tf_op jit(solution)/shard_map/ppermute | solution.py:151
  (79 other events, 579.6 us)
Sparse Core Ops, SparseCore 0:
  30.7 99.1 all-gather.3
  131.4 24.8 all-gather.7
  234.2 56.5 all-gather.5
  422.1 41.1 reduce-scatter.2
  465.8 58.3 reduce-scatter.4
